TPU v7x, 32 devices: a whole 2x2x4 slice. The times are simulated.
32 devices in a mesh: wide: 8 (over z, y), narrow: 4 (over x, core).
Axes of the slice: x: 2, y: 2, z: 4, core: 2. Of those that a mesh axis runs over, the one named last changes fastest.
Arguments:
- residual: bfloat16 [8, 4, 2048, 256], P('wide', 'narrow'), may hold values from -6 to 6
- scaling: float32 [8, 4, 2048], P('wide', 'narrow'), may hold values from 0.25 to 1
- local_inverse: bfloat16 [8, 4, 2048, 2048], P('wide', 'narrow'), may hold values from -0.125 to 0.125
- coarse_basis: bfloat16 [8, 4, 24, 2048], P('wide', 'narrow'), may hold values from -0.125 to 0.125
- primal_map: int32 [8, 4, 24], P('wide', 'narrow'), may hold values from 0 to 95
- slot_index: int32 [8, 4, 6, 256], P('wide', 'narrow'), may hold values from 0 to 2047, as said below
- slot_length: int32 [8, 4, 6], P('wide', 'narrow'), may hold values from 0 to 256, as said below
- coarse_sub: float32 [8, 96, 96], P('wide'), may hold values from -0.625 to 0.625
- coarse_pivot: float32 [8, 96, 96], P('wide'), as said below
Outputs:
- interface_sum: float32 [8, 4, 2048, 256], P('wide', 'narrow')
Inputs may be any that keep to these rules, and one draw needn't show every extreme that they name: `slot_index`: within one slot of one subdomain the 256 entries are distinct. `slot_length`: paired slots have equal lengths: slot j of subdomain (w, n) and slot n of (w, j); slot 4 of (w, n) and slot 5 of (w - 1, n). A subdomain's own narrow slot n, the slot 4 of slab 0 and the slot 5 of slab 8 - 1 have length 0. `coarse_pivot`: Symmetric.
All inputs are finite; a program needn't handle non-finite values.
Results may differ from a plain program's by a relative error of at most 0.0039.
The roundings to bfloat16 on the way count: a program that leaves them out, or rounds other values in their place, can miss the bound.
Values may be sent and summed in bfloat16 or wider, within the bound.
No kernel may reach another device: no remote copies, remote signals or barrier semaphores. Data moves between devices by JAX's collectives and lax.ppermute only.
A program may use at most 128 MiB of HBM per device.

v0:
```python
import jax
import jax.numpy as jnp
from jax import lax
from jax.sharding import PartitionSpec as P

highest = lax.Precision.HIGHEST


def entering(part, axis, combine, identity, reverse):
    count = lax.axis_size(axis)
    place = lax.axis_index(axis)
    ahead = count - 1 - place if reverse else place
    gathered = jax.tree.map(lambda a: lax.all_gather(a, axis), part)
    state = jax.tree.map(lambda a, e: jnp.zeros_like(a) + jnp.asarray(e, a.dtype), part, identity)

    def one(turn, state):
        source = count - 1 - turn if reverse else turn
        return combine(
            state, jax.tree.map(lambda a: lax.dynamic_index_in_dim(a, source, 0, False), gathered)
        )

    return lax.fori_loop(0, ahead, one, state)


def shifted(block, axis, distance):
    devices = range(lax.axis_size(axis))
    route = [(i - distance, i) for i in devices if i - distance in devices]
    return lax.ppermute(block, axis, route)


def exact_dot(left, right):
    return jnp.dot(left, right, precision=highest, preferred_element_type=jnp.float32)


def compose(earlier, later):
    return (exact_dot(later[0], earlier[0]), exact_dot(later[0], earlier[1]) + later[1])


def coarse_solve(coarse_rhs, sub_block, pivot_block):
    order = sub_block.shape[0]
    identity = jnp.eye(order, dtype=jnp.float32)
    empty = jnp.zeros_like(coarse_rhs)
    sub_trans = sub_block.T
    before = entering((-sub_block, coarse_rhs), "wide", compose, (identity, empty), False)
    chain_y = coarse_rhs - exact_dot(sub_block, before[1])
    pivoted = exact_dot(pivot_block, chain_y)
    after = entering(
        (-sub_trans, exact_dot(sub_trans, pivoted)), "wide", compose, (identity, empty), True
    )
    return pivoted - after[1]


def body(
    residual,
    scaling,
    local_inverse,
    coarse_basis,
    primal_map,
    slot_index,
    slot_length,
    coarse_sub,
    coarse_pivot,
):
    groups = lax.axis_size("narrow")
    weights = scaling[0, 0]
    weighted = (weights[:, None] * residual[0, 0].astype(jnp.float32)).astype(jnp.bfloat16)
    local_part = jnp.dot(local_inverse[0, 0], weighted, preferred_element_type=jnp.float32)
    basis = coarse_basis[0, 0]
    primal = jnp.dot(basis, weighted, preferred_element_type=jnp.float32)
    order = coarse_sub.shape[1]
    one_hot = (primal_map[0, 0][:, None] == jnp.arange(order, dtype=jnp.int32)[None, :]).astype(
        jnp.float32
    )
    assembly = lax.dot_general(
        one_hot,
        primal,
        (((0,), (0,)), ((), ())),
        precision=highest,
        preferred_element_type=jnp.float32,
    )
    coarse_share = lax.psum_scatter(assembly, "narrow", scatter_dimension=1, tiled=True)
    solved_share = coarse_solve(coarse_share, coarse_sub[0], coarse_pivot[0])
    coarse_sol = lax.all_gather(solved_share, "narrow", axis=1, tiled=True)
    coarse_vals = exact_dot(one_hot, coarse_sol)
    spread = lax.dot_general(
        basis.astype(jnp.float32),
        coarse_vals,
        (((0,), (0,)), ((), ())),
        precision=highest,
        preferred_element_type=jnp.float32,
    )
    combined = (weights[:, None] * (local_part + spread)).astype(jnp.bfloat16)
    indices = slot_index[0, 0]
    lengths = slot_length[0, 0]
    capacity = indices.shape[1]
    live_mask = jnp.arange(capacity, dtype=jnp.int32)[None, :] < lengths[:, None]
    outgoing = jnp.where(live_mask[:, :, None], combined[indices], jnp.zeros((), jnp.bfloat16))
    narrow_in = lax.all_to_all(outgoing[:groups], "narrow", split_axis=0, concat_axis=0, tiled=True)
    below = shifted(outgoing[groups + 1], "wide", 1)
    above = shifted(outgoing[groups], "wide", -1)
    incoming = jnp.concatenate([narrow_in, below[None], above[None]], axis=0)
    columns = combined.shape[1]
    summed = (
        combined.astype(jnp.float32)
        .at[indices.reshape(-1)]
        .add(incoming.reshape(-1, columns).astype(jnp.float32))
    )
    return summed[None, None]


def solution(mesh):
    in_specs = (
        P("wide", "narrow", None, None),
        P("wide", "narrow", None),
        P("wide", "narrow", None, None),
        P("wide", "narrow", None, None),
        P("wide", "narrow", None),
        P("wide", "narrow", None, None),
        P("wide", "narrow", None),
        P("wide", None, None),
        P("wide", None, None),
    )
    out_specs = P("wide", "narrow", None, None)
    return jax.shard_map(body, mesh=mesh, in_specs=in_specs, out_specs=out_specs, check_vma=False)
```

profile of v0, /device:TPU:0, one launch (start us, length us, event | category | flops | bytes accessed | tf_op | source)
XLA Modules:
  0.0 194.7 jit_solution(11893826487892499667)
XLA Ops:
  6.5 0.0 copy-start
  6.5 0.0 copy-start.4
  6.5 0.0 reduce-scatter.2.cloned.1.call-start
  6.6 0.9 copy-done
  7.5 2.1 %fusion.15 = f32[256,24]{1,0:T(8,128)S(1)} fusion(bf16[1,1,2048,256]{3,2,1,0:T(8,128)(2,1)} %param.13, f32[2048]{0:T(1024)} %bitcast.94, bf16[1,1,24,2048]{3,2,1,0:T(8,128)(2,1)S(1)} %copy-done), kind=kOutput, calls=%fused_computation.25 | convolution fusion | flops 26738688 | bytes 1179648 | tf_op jit(solution)/shard_map/dot_general | solution.py:69
  9.5 1.6 fusion.26
  11.1 0.0 reduce-scatter.2.cloned.1.call-update
  11.1 0.0 copy-done.1
  11.1 0.1 copy.13
  11.2 0.0 copy-done.3
  11.3 32.9 %all_gather.25 = f32[8,96,96]{2,1,0:T(8,128)S(1)} all-gather(f32[1,96,96]{2,1,0:T(8,128)S(1)} %neg.10), channel_id=1, replica_groups=mesh['wide'=8,'narrow'=4] {'wide'}, dimensions={0}, use_global_device_ids=true | all-gather | bytes 331776 | tf_op jit(solution)/shard_map/all_gather | solution.py:13
  44.3 30.9 %all-gather.1 = f32[768,96]{1,0:T(8,128)S(1)} all-gather(f32[96,96]{1,0:T(8,128)S(1)} %fusion.24), channel_id=3, replica_groups=mesh['wide'=8,'narrow'=4] {'wide'}, dimensions={0}, use_global_device_ids=true | all-gather | bytes 331776 | tf_op jit(solution)/shard_map/all_gather | solution.py:13
  75.2 0.0 copy-done.4
  75.2 6.5 %fusion.6 = f32[256,2048]{1,0:T(8,128)S(1)} fusion(bf16[1,1,2048,2048]{3,2,1,0:T(8,128)(2,1)} %param.15, bf16[1,1,2048,256]{3,2,1,0:T(8,128)(2,1)} %param.13, f32[2048]{0:T(1024)S(1)} %bitcast.95), kind=kOutput, calls=%fused_computation.10 | convolution fusion | flops 2149056512 | bytes 11542528 | tf_op jit(solution)/shard_map/dot_general | solution.py:67
  81.7 0.0 copy-start.5
  81.7 0.0 copy-done.6
  81.7 0.1 iota_compare_fusion.3
  81.8 30.9 %all-gather.3 = f32[8,96,64]{1,2,0:T(8,128)S(1)} all-gather(f32[1,96,64]{1,2,0:T(8,128)} %bitcast.92), channel_id=2, replica_groups=mesh['wide'=8,'narrow'=4] {'wide'}, dimensions={0}, use_global_device_ids=true | all-gather | bytes 221184 | tf_op jit(solution)/shard_map/all_gather | solution.py:13
  112.7 1.0 fusion.13
  113.7 0.0 copy-done.2
  113.7 0.2 fusion.22
  114.0 0.2 convolution_bitcast_fusion
  114.1 32.2 %all-gather.4 = f32[8,96,64]{1,2,0:T(8,128)S(1)} all-gather(f32[1,96,64]{1,2,0:T(8,128)S(1)} %convolution_bitcast_fusion), channel_id=4, replica_groups=mesh['wide'=8,'narrow'=4] {'wide'}, dimensions={0}, use_global_device_ids=true | all-gather | bytes 221184 | tf_op jit(solution)/shard_map/all_gather | solution.py:13
  146.4 1.8 while.27
  146.4 0.2 convolution_add_fusion.6
  146.6 0.2 convolution_add_fusion.6
  146.9 0.2 convolution_add_fusion.6
  147.1 0.2 convolution_add_fusion.6
  147.4 0.2 convolution_add_fusion.6
  147.7 0.2 convolution_add_fusion.6
  147.9 0.2 convolution_add_fusion.6
  148.2 5.4 %all_gather.32 = f32[96,256]{0,1:T(8,128)S(1)} all-gather(f32[96,64]{0,1:T(8,128)S(1)} %bitcast_subtract_fusion), channel_id=1, replica_groups=mesh['wide'=8,'narrow'=4] {'narrow'}, dimensions={1}, use_global_device_ids=true | all-gather | bytes 122880 | tf_op jit(solution)/shard_map/all_gather | solution.py:83
  153.6 0.0 copy-done.5
  153.6 0.2 fusion.25
  153.8 1.2 fusion.10
  155.0 0.5 copy.14
  155.5 4.8 %gather_fusion = bf16[1536,256]{1,0:T(8,128)(2,1)S(1)} fusion(bf16[2048,256]{1,0:T(8,128)(2,1)S(1)} %copy.14, s32[2048]{0:T(1024)S(1)} %pad_clamp_fusion), kind=kCustom, calls=%fused_computation | custom fusion | bytes 1579008 | tf_op jit(solution)/shard_map/gather | solution.py:97
  160.3 0.3 broadcast_select_fusion
  160.6 0.8 slice.14
  161.4 3.5 %all-to-all-start = ((bf16[4,256,256]{2,1,0:T(8,128)(2,1)}), bf16[4,256,256]{2,1,0:T(8,128)(2,1)S(1)}, u32[]{:S(2)}, u32[]{:S(2)}) async-start(bf16[4,256,256]{2,1,0:T(8,128)(2,1)} %slice.14), calls=%async_computation.1 | async-start | bytes 1048576 | tf_op jit(solution)/shard_map/all_to_all | solution.py:98
  164.9 3.7 %collective-permute-start = (bf16[256,256]{1,0:T(8,128)(2,1)S(1)}, bf16[256,256]{1,0:T(8,128)(2,1)S(1)}, u32[]{:S(2)}, u32[]{:S(2)}) collective-permute-start(bf16[256,256]{1,0:T(8,128)(2,1)S(1)} %get-tuple-element.155), channel_id=1, source_target_pairs={{0,4},{4,8},{8,12},{12,16},{16,20},{20,24},{24,28},{1,5},{5,9},{9,... | collective-permute-start | bytes 393224 | tf_op jit(solution)/shard_map/ppermute | solution.py:28
  168.6 1.3 collective-permute-start.1
  169.9 1.6 copy.15
  171.5 0.4 collective-permute-done
  171.9 4.1 %collective-permute-done.1 = bf16[256,256]{1,0:T(8,128)(2,1)S(1)} collective-permute-done((bf16[256,256]{1,0:T(8,128)(2,1)S(1)}, bf16[256,256]{1,0:T(8,128)(2,1)S(1)}, u32[]{:S(2)}, u32[]{:S(2)}) %collective-permute-start.1) | collective-permute-done | bytes 131104 | tf_op jit(solution)/shard_map/ppermute | solution.py:28
  176.1 0.0 all-to-all-done
  176.1 0.1 pad_maximum_fusion
  176.2 11.7 %scatter_custom_fusion = f32[2048,256]{1,0:T(8,128)} fusion(f32[2048,256]{1,0:T(8,128)} %copy.15, s32[1536]{0:T(1024)S(1)} %fusion.27, bf16[1536,256]{1,0:T(8,128)(2,1)S(1)} %bitcast.87), kind=kCustom, calls=%fused_computation.17 | custom fusion | flops 786432 | bytes 2883584 | tf_op jit(solution)/shard_map/scatter-add | solution.py:106
  (23 shorter events, 0.1 us)
Async XLA Ops:
  6.5 0.9 copy-start
  6.5 68.7 %copy-start.4 = (f32[1,1,2048]{2,1,0:T(1,128)S(1)}, f32[1,1,2048]{2,1,0:T(1,128)}, u32[]{:S(2)}) copy-start(f32[1,1,2048]{2,1,0:T(1,128)} %param.14) | copy-start | bytes 24580
  6.5 4.6 %copy-start.1 = (f32[1,96,96]{2,1,0:T(8,128)S(1)}, f32[1,96,96]{2,1,0:T(8,128)}, u32[]{:S(2)}) copy-start(f32[1,96,96]{2,1,0:T(8,128)} %param.20) | copy-start | bytes 110596
  6.5 4.7 %copy-start.3 = (s32[1,1,6,256]{3,1,2,0:T(1,128)S(1)}, s32[1,1,6,256]{3,1,2,0:T(1,128)}, u32[]{:S(2)}) copy-start(s32[1,1,6,256]{3,1,2,0:T(1,128)} %param.18) | copy-start | bytes 18436
  6.5 75.3 %reduce-scatter.2.cloned.1.call-start = ((), (), s32[]{:S(2)}) async-start(), calls=%async_computation.2 | async-start | bytes 163840 | tf_op jit(solution)/shard_map/reduce_scatter | solution.py:81
  75.2 6.5 %copy-start.6 = (s32[1,1,6]{2,1,0:T(1,128)S(1)}, s32[1,1,6]{2,1,0:T(1,128)}, u32[]{:S(2)}) copy-start(s32[1,1,6]{2,1,0:T(1,128)} %param.19) | copy-start | bytes 76
  75.2 38.5 %copy-start.2 = (f32[1,96,96]{2,1,0:T(8,128)S(1)}, f32[1,96,96]{2,1,0:T(8,128)}, u32[]{:S(2)}) copy-start(f32[1,96,96]{2,1,0:T(8,128)} %param.21) | copy-start | bytes 110596
  81.7 71.9 %copy-start.5 = (s32[1,1,24]{2,1,0:T(1,128)S(1)}, s32[1,1,24]{2,1,0:T(1,128)}, u32[]{:S(2)}) copy-start(s32[1,1,24]{2,1,0:T(1,128)} %param.17) | copy-start | bytes 292
  161.4 14.7 %all-to-all-start = ((bf16[4,256,256]{2,1,0:T(8,128)(2,1)}), bf16[4,256,256]{2,1,0:T(8,128)(2,1)S(1)}, u32[]{:S(2)}, u32[]{:S(2)}) async-start(bf16[4,256,256]{2,1,0:T(8,128)(2,1)} %slice.14), calls=%async_computation.1 | async-start | bytes 1048576 | tf_op jit(solution)/shard_map/all_to_all | solution.py:98
  164.9 7.0 %collective-permute-start = (bf16[256,256]{1,0:T(8,128)(2,1)S(1)}, bf16[256,256]{1,0:T(8,128)(2,1)S(1)}, u32[]{:S(2)}, u32[]{:S(2)}) collective-permute-start(bf16[256,256]{1,0:T(8,128)(2,1)S(1)} %get-tuple-element.155), channel_id=1, source_target_pairs={{0,4},{4,8},{8,12},{12,16},{16,20},{20,24},{24,28},{1,5},{5,9},{9,... | collective-permute-start | bytes 393224 | tf_op jit(solution)/shard_map/ppermute | solution.py:28
  168.6 7.5 %collective-permute-start.1 = (bf16[256,256]{1,0:T(8,128)(2,1)S(1)}, bf16[256,256]{1,0:T(8,128)(2,1)S(1)}, u32[]{:S(2)}, u32[]{:S(2)}) collective-permute-start(bf16[256,256]{1,0:T(8,128)(2,1)S(1)} %get-tuple-element.156), channel_id=1, source_target_pairs={{4,0},{8,4},{12,8},{16,12},{20,16},{24,20},{28,24},{5,1},{9,5},{13... | collective-permute-start | bytes 393224 | tf_op jit(solution)/shard_map/ppermute | solution.py:28
Sparse Core Ops, SparseCore 0:
  11.2 22.3 reduce-scatter.1
where the time goes:
time: 195 us
  blocking collectives  132 us (68%)
  matrix products  14.4 us (7%)
  between operations  13.6 us (7%)
  other arithmetic  12.2 us (6%)
  local copies, waits for them, and re-layouts  8.77 us (4%)
  starting transfers between devices  8.46 us (4%)
  waiting for transfers between devices  4.55 us (2%)
    all_gather x4, blocking collectives, entering(): gathered = jax.tree.map(lambda a: lax.all_gather(a, axis), part)  127 us
    scatter-add x1, other arithmetic, body(): summed = combined.astype(jnp.float32).at[indices.reshape(-1)].add(incomin...  11.7 us
    dot_general x1, matrix products, body(): jnp.dot(local_inverse[0, 0], weighted, preferred_element_type=jnp.float32)  6.48 us
    all_gather x1, blocking collectives, body(): coarse_sol = lax.all_gather(solved_share, 'narrow', axis=1, tiled=True)  5.42 us
    ppermute x2, starting transfers between devices, shifted(): return lax.ppermute(block, axis, route)  4.95 us
    gather x1, local copies, waits for them, and re-layouts, body(): combined[indices]  4.76 us
    ppermute x2, waiting for transfers between devices, shifted(): return lax.ppermute(block, axis, route)  4.53 us
  transfers between devices with their start and end apart: 4, of which 2 were waited for; matrix products, arithmetic and copies ran while one was open for 4% of the time, Pallas kernels for 0%

commit v1 on v0

v1 whole, which is shorter than its diff:
```python
import jax
import jax.numpy as jnp
from jax import lax
from jax.sharding import PartitionSpec as P

highest = lax.Precision.HIGHEST
f32 = jnp.float32
bf16 = jnp.bfloat16


def swap(block, axis, mask):
    count = lax.axis_size(axis)
    return lax.ppermute(block, axis, [(i, i ^ mask) for i in range(count)])


def swap_odd(block, axis):
    count = lax.axis_size(axis)
    pairs = [(i, i + 1) for i in range(1, count - 1, 2)]
    return lax.ppermute(block, axis, pairs + [(b, a) for a, b in pairs])


def exact(left, right, dims=None):
    if dims is None:
        return jnp.dot(left, right, precision=highest, preferred_element_type=f32)
    return lax.dot_general(left, right, dims, precision=highest, preferred_element_type=f32)


def gather_pairs(block, axis):
    count = lax.axis_size(axis)
    held, offsets, mask = block[None], [0], count // 2
    while mask:
        held = jnp.concatenate([held, swap(held, axis, mask)], axis=0)
        offsets += [o ^ mask for o in offsets]
        mask //= 2
    return held, offsets


def one_hot(index, size, dtype):
    return (index[..., None] == jnp.arange(size, dtype=index.dtype)).astype(dtype)


def body(
    residual,
    scaling,
    local_inverse,
    coarse_basis,
    primal_map,
    slot_index,
    slot_length,
    coarse_sub,
    coarse_pivot,
):
    slabs, groups = lax.axis_size("wide"), lax.axis_size("narrow")
    w, n = lax.axis_index("wide"), lax.axis_index("narrow")
    order = coarse_sub.shape[1]
    basis = coarse_basis[0, 0]
    constraints, rows = basis.shape
    columns = residual.shape[3]
    own_columns = columns // groups
    weights = scaling[0, 0]
    own_map = primal_map[0, 0]

    factors, offsets = gather_pairs(jnp.stack([coarse_sub[0], coarse_pivot[0]]), "wide")
    place = jnp.zeros((slabs,), jnp.int32).at[jnp.array(offsets, jnp.int32) ^ w].set(
        jnp.arange(slabs, dtype=jnp.int32)
    )

    weighted = (weights[:, None] * residual[0, 0].astype(f32)).astype(bf16)
    primal = lax.dot_general(weighted, basis, (((0,), (1,)), ((), ())), preferred_element_type=f32)
    quarter, lanes = own_columns // 4, 32
    packed = jnp.pad(primal, ((0, 0), (0, lanes - constraints)))
    packed = packed.reshape(groups, 4, quarter, lanes)
    tail = jnp.zeros((quarter * (lanes - constraints),), f32).at[:constraints].set(own_map.astype(f32))
    tail = jnp.pad(tail.reshape(quarter, lanes - constraints), ((0, 0), (constraints, 0)))
    packed = packed.at[:, 0].add(tail)
    packed = jnp.swapaxes(packed, 1, 2).reshape(groups, quarter, 4 * lanes)
    sent = jnp.broadcast_to(packed[None], (slabs,) + packed.shape).reshape(
        slabs * groups, quarter, 4 * lanes
    )
    got = lax.all_to_all(sent, ("wide", "narrow"), split_axis=0, concat_axis=0, tiled=True)

    local_part = jnp.dot(local_inverse[0, 0], weighted, preferred_element_type=f32)
    scaled = weights[:, None] * local_part
    parity = w & 1
    picks = jnp.concatenate(
        [n ^ jnp.arange(1, groups), jnp.stack([groups + 1 - parity, groups + parity])]
    )
    indices = slot_index[0, 0][picks]
    lengths = slot_length[0, 0][picks]
    slots, capacity = indices.shape
    live = jnp.arange(capacity, dtype=jnp.int32)[None, :] < lengths[:, None]
    targets = jnp.where(live, indices, -1).reshape(-1)
    chosen = scaled.astype(bf16)[indices]
    scaled_basis = weights[None, :] * basis.astype(f32)
    basis_high = scaled_basis.astype(bf16)
    basis_low = (scaled_basis - basis_high.astype(f32)).astype(bf16)
    basis_both = jnp.concatenate([basis_high, basis_low], axis=0)
    picked_basis = jnp.swapaxes(basis_both[:, indices], 0, 1)
    outgoing = jnp.concatenate([chosen, picked_basis], axis=1)
    arrived = [swap(outgoing[k - 1], "narrow", k) for k in range(1, groups)]
    arrived += [swap(outgoing[groups - 1], "wide", 1), swap_odd(outgoing[groups], "wide")]
    arrived = jnp.stack(arrived)
    scatter = (jnp.arange(rows, dtype=jnp.int32)[:, None] == targets[None, :]).astype(bf16)
    early = jnp.dot(
        scatter, arrived[:, :capacity].reshape(-1, columns), preferred_element_type=f32
    )
    late_basis = jnp.einsum(
        "ikb,kpb->kip",
        scatter.reshape(rows, slots, capacity),
        arrived[:, capacity:],
        preferred_element_type=f32,
    )
    late_basis = late_basis[..., :constraints] + late_basis[..., constraints:]

    got = got.reshape(slabs, groups, quarter, 4, lanes)
    maps = got[:, :, :, 0, constraints:].reshape(slabs, groups, -1)[..., :constraints]
    maps = maps.astype(jnp.int32)
    hots = one_hot(maps, order, f32)
    values = jnp.swapaxes(got[..., :constraints], 2, 3).reshape(
        slabs, groups, own_columns, constraints
    )
    right = jnp.einsum("vmcp,vmpg->vcg", values, hots, precision=highest)

    subs = factors[:, 0][place]
    pivots = factors[:, 1][place]
    flip = (((1,), (1,)), ((), ()))
    chain, carry = [], None
    for v in range(slabs):
        carry = right[v] if v == 0 else right[v] - exact(carry, subs[v], flip)
        chain.append(carry)
    pivoted = [exact(chain[v], pivots[v]) for v in range(slabs)]
    solved, carry = [None] * slabs, None
    for v in reversed(range(slabs)):
        solved[v] = pivoted[v] if carry is None else pivoted[v] - carry
        if v:
            carry = exact(solved[v], subs[v])
    solved = jnp.stack(solved)
    above = jnp.clip(jnp.stack([w ^ 1, w - 1 + 2 * parity]), 0, slabs - 1)
    mine = jnp.broadcast_to(solved[w][None], (groups, own_columns, order))
    sides = [
        jnp.einsum("cg,mpg->mcp", solved[above[i]], hots[above[i]], precision=highest)
        for i in range(2)
    ]
    share = jnp.concatenate([mine] + sides, axis=2)
    share = share[n ^ jnp.arange(groups)]
    pieces = [share[0]] + [swap(share[k], "narrow", k) for k in range(1, groups)]
    solution_t = jnp.stack(pieces)[n ^ jnp.arange(groups)].reshape(columns, -1)

    slab_t, first_t, second_t = (
        solution_t[:, :order],
        solution_t[:, order : order + constraints],
        solution_t[:, order + constraints :],
    )
    near = hots[w]
    joined = sum(exact(late_basis[k - 1], near[n ^ k]) for k in range(1, groups))
    late = exact(
        jnp.concatenate([joined, late_basis[groups - 1], late_basis[groups]], axis=1),
        solution_t,
        flip,
    )
    coarse_vals = exact(one_hot(own_map, order, f32), slab_t, flip)
    spread = exact(basis.astype(f32), coarse_vals, (((0,), (0,)), ((), ())))
    combined = (weights[:, None] * (local_part + spread)).astype(bf16)
    return (combined.astype(f32) + early + late)[None, None]


def solution(mesh):
    in_specs = (
        P("wide", "narrow", None, None),
        P("wide", "narrow", None),
        P("wide", "narrow", None, None),
        P("wide", "narrow", None, None),
        P("wide", "narrow", None),
        P("wide", "narrow", None, None),
        P("wide", "narrow", None),
        P("wide", None, None),
        P("wide", None, None),
    )
    out_specs = P("wide", "narrow", None, None)
    return jax.shard_map(body, mesh=mesh, in_specs=in_specs, out_specs=out_specs, check_vma=False)
```

time: 195 us -> 111 us (0.57)
  blocking collectives: 132 us -> 0 us
  matrix products: 14.4 us -> 40 us
  local copies, waits for them, and re-layouts: 8.77 us -> 32.1 us
  starting transfers between devices: 8.46 us -> 19.9 us
  between operations: 13.6 us -> 4.48 us
  other arithmetic: 12.2 us -> 9.27 us
    all_gather x5 -> x0, blocking collectives: 132 us -> none  [the longest x4 127 us: entering(): gathered = jax.tree.map(lambda a: lax.all_gather(a, axis), part)]
    dot_general x15 -> x34, matrix products: 14.4 us -> 37.9 us  [the longest x18 13.5 us: exact(): return jnp.dot(left, right, precision=highest, preferred_element_type=f32)]
    scatter-add x1, other arithmetic: 11.7 us -> 0.01 us  [body(): packed = packed.at[:, 0].add(tail)]
    ppermute x2 -> x11, starting transfers between devices: 4.95 us -> 16 us  [the longest x10 15.4 us: swap(): return lax.ppermute(block, axis, [(i, i ^ mask) for i in range(count)])]
    gather x1 -> x9, local copies, waits for them, and re-layouts: 4.76 us -> 15.5 us  [the longest x1 4.67 us: body(): chosen = scaled.astype(bf16)[indices]]
    concatenate x1 -> x6, other arithmetic: 0.1 us -> 4.67 us  [the longest x3 3.75 us: gather_pairs(): held = jnp.concatenate([held, swap(held, axis, mask)], axis=0)]
    unnamed x15 -> x43, local copies, waits for them, and re-layouts: 0.99 us -> 3.87 us
    broadcast_in_dim x2 -> x5, local copies, waits for them, and re-layouts: 0.01 us -> 2.7 us  [the longest x1 1.81 us: body(): return (combined.astype(f32) + early + late)[None, None]]
  transfers between devices with their start and end apart: 4 -> 12, of which waited for: 2 -> 2; matrix products, arithmetic and copies ran while one was open for 4% -> 41% of each run, Pallas kernels for 0% -> 0%
where the time goes in v1:
time: 111 us; the launch traced here: 109 us
  matrix products  40 us (36%)
  local copies, waits for them, and re-layouts  32.1 us (29%)
  starting transfers between devices  19.9 us (18%)
  other arithmetic  9.27 us (8%)
  between operations  4.48 us (4%)
  waiting for transfers between devices  3.17 us (3%)
    ppermute x10, starting transfers between devices, swap(): return lax.ppermute(block, axis, [(i, i ^ mask) for i in range(count)])  15.4 us
    dot_general x18, matrix products, exact(): return jnp.dot(left, right, precision=highest, preferred_element_type=f32)  13.5 us
    dot_general x10, matrix products, exact(): lax.dot_general(left, right, dims, precision=highest, preferred_element_t...  10.1 us
    dot_general x1, matrix products, body(): jnp.dot(local_inverse[0, 0], weighted, preferred_element_type=f32)  6.46 us
    gather x1, local copies, waits for them, and re-layouts, body(): chosen = scaled.astype(bf16)[indices]  4.67 us
    unnamed x43, local copies, waits for them, and re-layouts  3.87 us
    all_to_all x1, starting transfers between devices, body(): lax.all_to_all(sent, ('wide', 'narrow'), split_axis=0, concat_axis=0, til...  3.82 us
    concatenate x3, other arithmetic, gather_pairs(): held = jnp.concatenate([held, swap(held, axis, mask)], axis=0)  3.75 us
  transfers between devices with their start and end apart: 12, of which 2 were waited for; matrix products, arithmetic and copies ran while one was open for 41% of the time, Pallas kernels for 0%

profile of v1, /device:TPU:0, one launch (start us, length us, event | category | flops | bytes accessed | tf_op | source)
XLA Modules:
  0.0 108.8 jit_solution(14815082868876185268)
XLA Ops:
  0.9 4.2 %collective-permute-start = (f32[1,2,96,96]{3,2,1,0:T(8,128)S(1)}, f32[1,2,96,96]{3,2,1,0:T(8,128)}, u32[]{:S(2)}, u32[]{:S(2)}) collective-permute-start(f32[1,2,96,96]{3,2,1,0:T(8,128)S(1)} %maximum_bitcast_fusion), channel_id=1, source_target_pairs={{0,16},{4,20},{8,24},{12,28},{16,0},{20,4},{24,8},{28,12},{1,17},{... | collective-permute-start | bytes 221192 | tf_op jit(solution)/shard_map/ppermute | solution.py:13
  5.9 2.1 %fusion.21 = f32[256,24]{1,0:T(8,128)S(1)} fusion(bf16[1,1,2048,256]{3,2,1,0:T(8,128)(2,1)} %param.14, f32[2048]{0:T(1024)} %bitcast.277, bf16[1,1,24,2048]{3,2,1,0:T(8,128)(2,1)} %param.17), kind=kOutput, calls=%fused_computation.66 | convolution fusion | flops 26738688 | bytes 1179648
  8.9 3.8 %all-to-all-start = ((f32[32,16,128]{2,1,0:T(8,128)}), f32[32,16,128]{2,1,0:T(8,128)S(1)}, u32[]{:S(2)}, u32[]{:S(2)}) async-start(f32[32,16,128]{2,1,0:T(8,128)} %bitcast.7), calls=%async_computation | async-start | bytes 524288 | tf_op jit(solution)/shard_map/all_to_all | solution.py:80
  13.9 2.8 %gather_fusion.7 = bf16[1280,48]{1,0:T(8,128)(2,1)S(1)} fusion(bf16[48,2048]{0,1:T(8,128)(2,1)S(1)} %copy.47, s32[2048]{0:T(1024)S(1)} %pad_clamp_fusion), kind=kCustom, calls=%fused_computation.7 | custom fusion | bytes 250880 | tf_op jit(solution)/shard_map/gather | solution.py:98
  17.5 6.5 %fusion.2 = f32[256,2048]{1,0:T(8,128)S(1)} fusion(bf16[1,1,2048,2048]{3,2,1,0:T(8,128)(2,1)} %param.16, bf16[1,1,2048,256]{3,2,1,0:T(8,128)(2,1)} %param.14, f32[2048]{0:T(1024)S(1)} %bitcast.279), kind=kOutput, calls=%fused_computation.13 | convolution fusion | flops 2149056512 | bytes 11542528 | tf_op jit(solution)/shard_map/dot_general | solution.py:82
  24.0 1.2 %fusion.20 = bf16[2048,256]{0,1:T(8,128)(2,1)} fusion(f32[256,2048]{1,0:T(8,128)S(1)} %fusion.2, f32[2048]{0:T(1024)S(1)} %bitcast.280), kind=kLoop, calls=%fused_computation.58 | loop fusion | flops 1048576 | bytes 3153920 | tf_op jit(solution)/shard_map/convert_element_type | solution.py:93
  25.1 1.5 %copy.46 = bf16[2048,256]{1,0:T(8,128)(2,1)S(1)} copy(bf16[2048,256]{0,1:T(8,128)(2,1)} %fusion.20) | data formatting | bytes 2097152 | tf_op jit(solution)/shard_map/convert_element_type | solution.py:93
  26.6 4.7 %gather_fusion.6 = bf16[1280,256]{1,0:T(8,128)(2,1)} fusion(bf16[2048,256]{1,0:T(8,128)(2,1)S(1)} %copy.46, s32[2048]{0:T(1024)S(1)} %pad_clamp_fusion), kind=kCustom, calls=%fused_computation.6 | custom fusion | bytes 1315840 | tf_op jit(solution)/shard_map/gather | solution.py:93
  31.3 1.3 %fusion.34 = (bf16[304,256]{1,0:T(8,128)(2,1)S(1)}, bf16[304,256]{1,0:T(8,128)(2,1)S(1)}, bf16[304,256]{1,0:T(8,128)(2,1)S(1)}, bf16[304,256]{1,0:T(8,128)(2,1)S(1)}, bf16[304,256]{1,0:T(8,128)(2,1)S(1)}) fusion(bf16[5,48,256]{2,1,0:T(8,128)(2,1)} %bitcast.276, bf16[5,256,256]{2,1,0:T(8,128)(2,1)} %bitcast.268), kind=kLoop, calls=%fused_computation.94 | loop fusion | flops 1556480 | bytes 1556480 | tf_op jit(solution)/shard_map/squeeze | solution.py:101
  33.6 1.6 %collective-permute-start.7 = (bf16[304,256]{1,0:T(8,128)(2,1)S(1)}, bf16[304,256]{1,0:T(8,128)(2,1)}, u32[]{:S(2)}, u32[]{:S(2)}) collective-permute-start(bf16[304,256]{1,0:T(8,128)(2,1)S(1)} %get-tuple-element.35), channel_id=1, source_target_pairs={{0,2},{1,3},{2,0},{3,1},{4,6},{5,7},{6,4},{7,5},{8,10},{9,11},{10,... | collective-permute-start | bytes 466952 | tf_op jit(solution)/shard_map/ppermute | solution.py:13
  41.0 4.5 %collective-permute-start.9 = (bf16[304,256]{1,0:T(8,128)(2,1)S(1)}, bf16[304,256]{1,0:T(8,128)(2,1)S(1)}, u32[]{:S(2)}, u32[]{:S(2)}) collective-permute-start(bf16[304,256]{1,0:T(8,128)(2,1)S(1)} %get-tuple-element.37), channel_id=1, source_target_pairs={{0,4},{4,0},{8,12},{12,8},{16,20},{20,16},{24,28},{28,24},{1,5},{5... | collective-permute-start | bytes 466952 | tf_op jit(solution)/shard_map/ppermute | solution.py:13
  46.5 1.5 %collective-permute-start.1 = (f32[2,2,96,96]{3,2,1,0:T(8,128)S(1)}, f32[2,2,96,96]{3,2,1,0:T(8,128)S(1)}, u32[]{:S(2)}, u32[]{:S(2)}) collective-permute-start(f32[2,2,96,96]{3,2,1,0:T(8,128)S(1)} %pad_maximum_fusion.4), channel_id=1, source_target_pairs={{0,8},{4,12},{8,0},{12,4},{16,24},{20,28},{24,16},{28,20},{1,9},{5... | collective-permute-start | bytes 442376 | tf_op jit(solution)/shard_map/ppermute | solution.py:13
  48.9 0.9 bitcast_dynamic-update-slice_fusion.3
  50.9 2.1 %fusion.1 = f32[5,2048,48]{1,2,0:T(8,128)S(1)} fusion(s32[5,256]{1,0:T(8,128)S(1)} %fusion.63, bf16[5,304,256]{2,1,0:T(8,128)(2,1)S(1)} %bitcast_dynamic-update-slice_fusion), kind=kOutput, calls=%fused_computation.12 | convolution fusion | flops 254279680 | bytes 2097152 | tf_op jit(solution)/shard_map/ikb,kpb->kip/dot_general | solution.py:107
  53.1 1.0 copy-done.1
  55.8 1.7 %pad_maximum_fusion.1 = f32[4,2,96,96]{3,2,1,0:T(8,128)} fusion(f32[2,2,96,96]{3,2,1,0:T(8,128)S(1)} %collective-permute-done.1, f32[1,2,96,96]{3,2,1,0:T(8,128)} %collective-permute-done, f32[1,2,96,96]{3,2,1,0:T(8,128)S(1)} %maximum_bitcast_fusion), kind=kLoop, calls=%fused_computation.69 | loop fusion | flops 147456 | bytes 589824 | tf_op jit(solution)/shard_map/concatenate | solution.py:32
  57.5 1.0 collective-permute-start.2
  59.8 1.0 slice_bitcast_fusion
  61.0 1.4 %copy.40 = f32[8,4,4,16,24]{4,3,2,1,0:T(8,128)S(1)} copy(f32[8,4,4,16,24]{4,2,3,1,0:T(4,128)} %slice_bitcast_fusion) | data formatting | bytes 393216 | tf_op jit(solution)/shard_map/transpose | solution.py:119
  63.1 1.4 %convolution_bitcast_fusion = f32[8,64,96]{2,1,0:T(8,128)} fusion(f32[8,4,64,24]{3,2,1,0:T(8,128)S(1)} %bitcast.267, s32[8,4,24]{2,1,0:T(4,128)S(1)} %copy.42), kind=kOutput, calls=%fused_computation.38 | convolution fusion | flops 56696832 | bytes 396288 | tf_op jit(solution)/shard_map/vmcp,vmpg->vcg/dot_general | solution.py:122
  64.5 1.4 %convolution_add_fusion.3 = f32[2048,96]{0,1:T(8,128)} fusion(f32[2048,96]{0,1:T(8,128)S(1)} %fusion.24, f32[5,2048,24]{1,2,0:T(8,128)S(1)} %copy-done.2, pred[8,4,24,96]{3,2,1,0:T(8,128)(4,1)S(1)} %iota_compare_fusion.6, s32[]{:T(128)S(6)} %select_n.91, s32[]{:T(128)S(6)} %select_n.95), kind=kOutput, calls=%fused_computation.26 | convolution fusion | flops 56819712 | bytes 1772552 | tf_op jit(solution)/shard_map/dot_general | solution.py:24
  66.0 2.7 %collective-permute-done.2 = f32[4,2,96,96]{3,2,1,0:T(8,128)} collective-permute-done((f32[4,2,96,96]{3,2,1,0:T(8,128)}, f32[4,2,96,96]{3,2,1,0:T(8,128)}, u32[]{:S(2)}, u32[]{:S(2)}) %collective-permute-start.2) | collective-permute-done | bytes 294944 | tf_op jit(solution)/shard_map/ppermute | solution.py:13
  68.6 1.1 %pad_maximum_fusion = f32[8,2,96,96]{3,2,1,0:T(8,128)S(1)} fusion(f32[4,2,96,96]{3,2,1,0:T(8,128)} %collective-permute-done.2, f32[2,2,96,96]{3,2,1,0:T(8,128)S(1)} %copy-done.7, f32[1,2,96,96]{3,2,1,0:T(8,128)} %collective-permute-done, f32[1,2,96,96]{3,2,1,0:T(8,128)S(1)} %maximum_bitcast_fusion), kind=kLoop, calls=%fused_computation.61 | loop fusion | flops 442368 | bytes 1179648 | tf_op jit(solution)/shard_map/concatenate | solution.py:32
  69.7 1.0 slice_bitcast_fusion.1
  70.7 1.6 %gather_fusion.1 = f32[8,96,96]{2,1,0:T(8,128)S(1)} fusion(f32[8,96,96]{2,1,0:T(8,128)} %get-tuple-element.31, s32[1024]{0:T(1024)S(1)} %pad_clamp_fusion.3), kind=kCustom, calls=%fused_computation.1 | custom fusion | bytes 589856 | tf_op jit(solution)/shard_map/gather | solution.py:124
  72.3 2.3 %gather_fusion = f32[8,96,96]{2,1,0:T(8,128)} fusion(f32[8,96,96]{2,1,0:T(8,128)} %get-tuple-element.32, s32[1024]{0:T(1024)S(1)} %pad_clamp_fusion.3), kind=kCustom, calls=%fused_computation | custom fusion | bytes 589856 | tf_op jit(solution)/shard_map/gather | solution.py:125
  74.6 1.0 convolution_subtract_fusion.13
  75.6 1.0 convolution_subtract_fusion.12
  76.6 1.0 fusion.46
  77.6 1.0 convolution_subtract_fusion.11
  78.6 1.0 fusion.45
  79.6 1.0 convolution_subtract_fusion.10
  80.5 1.0 fusion.44
  81.5 1.0 convolution_subtract_fusion.9
  82.5 1.0 fusion.43
  83.5 1.0 convolution_subtract_fusion.8
  84.5 1.0 fusion.42
  85.4 1.0 fusion.47
  86.4 1.0 convolution_subtract_fusion.7
  87.4 1.0 fusion.41
  88.4 1.0 fusion.40
  93.7 1.5 %gather_fusion.2 = f32[4,64,144]{2,1,0:T(8,128)S(1)} fusion(f32[4,64,144]{2,1,0:T(8,128)} %pad_maximum_fusion.2, s32[1024]{0:T(1024)S(1)} %get-tuple-element.47), kind=kCustom, calls=%fused_computation.2 | custom fusion | bytes 294928 | tf_op jit(solution)/shard_map/gather | solution.py:145
  95.2 1.5 %collective-permute-start.4 = (f32[64,144]{1,0:T(8,128)S(1)}, f32[64,144]{1,0:T(8,128)S(1)}, u32[]{:S(2)}, u32[]{:S(2)}) collective-permute-start(f32[64,144]{1,0:T(8,128)S(1)} %get-tuple-element.39), channel_id=1, source_target_pairs={{0,2},{1,3},{2,0},{3,1},{4,6},{5,7},{6,4},{7,5},{8,10},{9,11},{10,... | collective-permute-start | bytes 110600 | tf_op jit(solution)/shard_map/ppermute | solution.py:13
  97.5 2.5 %convolution_add_fusion.2 = f32[2048,96]{0,1:T(8,128)} fusion(f32[2048,96]{0,1:T(8,128)} %convolution_add_fusion.3, f32[5,2048,24]{1,2,0:T(8,128)S(1)} %copy-done.2, pred[8,4,24,96]{3,2,1,0:T(8,128)(4,1)} %copy-done.11, s32[]{:T(128)S(6)} %select_n.91, s32[]{:T(128)S(6)} %select_n.97), kind=kOutput, calls=%fused_computation.25 | convolution fusion | flops 56819712 | bytes 1772552 | tf_op jit(solution)/shard_map/dot_general | solution.py:24
  101.3 1.2 %fusion.11 = f32[2048,256]{0,1:T(8,128)S(1)} fusion(f32[256,2048]{1,0:T(8,128)S(1)} %fusion.2, f32[24,256]{1,0:T(8,128)S(1)} %fusion.35, f32[2048]{0:T(1024)S(1)} %bitcast.281, bf16[1,1,24,2048]{3,2,1,0:T(8,128)(2,1)S(1)} %copy-done.10), kind=kOutput, calls=%fused_computation.24 | convolution fusion | flops 153092096 | bytes 4325376 | tf_op jit(solution)/shard_map/dot_general | solution.py:25
  102.5 2.6 %fusion.8 = f32[2048,256]{0,1:T(8,128)S(1)} fusion(f32[2048,256]{0,1:T(8,128)S(1)} %fusion.11, bf16[1280,256]{1,0:T(8,128)(2,1)S(1)} %bitcast.275, s32[1280]{0:T(1024)S(1)} %select_n.89), kind=kOutput, calls=%fused_computation.21 | convolution fusion | flops 1345323008 | bytes 4854784 | tf_op jit(solution)/shard_map/dot_general | solution.py:104
  105.1 1.9 %fusion.6 = f32[1,1,2048,256]{2,3,1,0:T(8,128)S(1)} fusion(f32[2048,256]{0,1:T(8,128)S(1)} %fusion.8, f32[256,144]{1,0:T(8,128)S(1)} %bitcast.270, f32[2048,24]{0,1:T(8,128)S(1)} %copy-done.5, f32[2048,24]{0,1:T(8,128)S(1)} %copy-done.4, f32[2048,96]{0,1:T(8,128)S(1)} %copy-done.3), kind=kOutput, calls=%fused_computation.18 | convolution fusion | flops 907083776 | bytes 5521408 | tf_op jit(solution)/shard_map/dot_general | solution.py:25
  107.0 1.8 %copy.52 = f32[1,1,2048,256]{3,2,1,0:T(8,128)} copy(f32[1,1,2048,256]{2,3,1,0:T(8,128)S(1)} %fusion.6) | data formatting | bytes 4194304 | tf_op jit(solution)/shard_map/broadcast_in_dim | solution.py:164
  (120 shorter events, 20.4 us)
Async XLA Ops:
  0.0 36.7 %copy-start = (s32[1,1,6]{2,1,0:T(1,128)S(1)}, s32[1,1,6]{2,1,0:T(1,128)}, u32[]{:S(2)}) copy-start(s32[1,1,6]{2,1,0:T(1,128)} %param.20) | copy-start | bytes 76
  0.0 12.8 %copy-start.9 = (bf16[1,1,24,2048]{3,2,1,0:T(8,128)(2,1)S(1)}, bf16[1,1,24,2048]{3,2,1,0:T(8,128)(2,1)}, u32[]{:S(2)}) copy-start(bf16[1,1,24,2048]{3,2,1,0:T(8,128)(2,1)} %param.17) | copy-start | bytes 294916
  0.0 12.8 %copy-start.12 = (f32[1,1,2048]{2,1,0:T(1,128)S(1)}, f32[1,1,2048]{2,1,0:T(1,128)}, u32[]{:S(2)}) copy-start(f32[1,1,2048]{2,1,0:T(1,128)} %param.15) | copy-start | bytes 24580
  0.0 12.8 %copy-start.13 = (s32[1,1,6,256]{3,1,2,0:T(1,128)S(1)}, s32[1,1,6,256]{3,1,2,0:T(1,128)}, u32[]{:S(2)}) copy-start(s32[1,1,6,256]{3,1,2,0:T(1,128)} %param.19) | copy-start | bytes 18436
  0.9 40.1 %collective-permute-start = (f32[1,2,96,96]{3,2,1,0:T(8,128)S(1)}, f32[1,2,96,96]{3,2,1,0:T(8,128)}, u32[]{:S(2)}, u32[]{:S(2)}) collective-permute-start(f32[1,2,96,96]{3,2,1,0:T(8,128)S(1)} %maximum_bitcast_fusion), channel_id=1, source_target_pairs={{0,16},{4,20},{8,24},{12,28},{16,0},{20,4},{24,8},{28,12},{1,17},{... | collective-permute-start | bytes 221192 | tf_op jit(solution)/shard_map/ppermute | solution.py:13
  8.9 49.6 %all-to-all-start = ((f32[32,16,128]{2,1,0:T(8,128)}), f32[32,16,128]{2,1,0:T(8,128)S(1)}, u32[]{:S(2)}, u32[]{:S(2)}) async-start(f32[32,16,128]{2,1,0:T(8,128)} %bitcast.7), calls=%async_computation | async-start | bytes 524288 | tf_op jit(solution)/shard_map/all_to_all | solution.py:80
  26.6 8.6 %copy-start.15 = (s32[8]{0:T(128)S(1)}, s32[8]{0:T(128)}, u32[]{:S(2)}) copy-start(s32[8]{0:T(128)} %constant.152.clone) | copy-start | bytes 100
  32.6 18.3 %collective-permute-start.10 = (bf16[304,256]{1,0:T(8,128)(2,1)S(1)}, bf16[304,256]{1,0:T(8,128)(2,1)S(1)}, u32[]{:S(2)}, u32[]{:S(2)}) collective-permute-start(bf16[304,256]{1,0:T(8,128)(2,1)S(1)} %get-tuple-element.33), channel_id=1, source_target_pairs={{4,8},{12,16},{20,24},{8,4},{16,12},{24,20},{5,9},{13,17},{21,25},... | collective-permute-start | bytes 466952 | tf_op jit(solution)/shard_map/ppermute | solution.py:19
  33.3 13.2 %collective-permute-start.6 = (bf16[304,256]{1,0:T(8,128)(2,1)S(1)}, bf16[304,256]{1,0:T(8,128)(2,1)}, u32[]{:S(2)}, u32[]{:S(2)}) collective-permute-start(bf16[304,256]{1,0:T(8,128)(2,1)S(1)} %get-tuple-element.34), channel_id=1, source_target_pairs={{0,1},{1,0},{2,3},{3,2},{4,5},{5,4},{6,7},{7,6},{8,9},{9,8},{10,11... | collective-permute-start | bytes 466952 | tf_op jit(solution)/shard_map/ppermute | solution.py:13
  33.6 15.4 %collective-permute-start.7 = (bf16[304,256]{1,0:T(8,128)(2,1)S(1)}, bf16[304,256]{1,0:T(8,128)(2,1)}, u32[]{:S(2)}, u32[]{:S(2)}) collective-permute-start(bf16[304,256]{1,0:T(8,128)(2,1)S(1)} %get-tuple-element.35), channel_id=1, source_target_pairs={{0,2},{1,3},{2,0},{3,1},{4,6},{5,7},{6,4},{7,5},{8,10},{9,11},{10,... | collective-permute-start | bytes 466952 | tf_op jit(solution)/shard_map/ppermute | solution.py:13
  35.2 14.7 %collective-permute-start.8 = (bf16[304,256]{1,0:T(8,128)(2,1)S(1)}, bf16[304,256]{1,0:T(8,128)(2,1)}, u32[]{:S(2)}, u32[]{:S(2)}) collective-permute-start(bf16[304,256]{1,0:T(8,128)(2,1)S(1)} %get-tuple-element.36), channel_id=1, source_target_pairs={{0,3},{1,2},{2,1},{3,0},{4,7},{5,6},{6,5},{7,4},{8,11},{9,10},{10,... | collective-permute-start | bytes 466952 | tf_op jit(solution)/shard_map/ppermute | solution.py:13
  41.0 9.8 %collective-permute-start.9 = (bf16[304,256]{1,0:T(8,128)(2,1)S(1)}, bf16[304,256]{1,0:T(8,128)(2,1)S(1)}, u32[]{:S(2)}, u32[]{:S(2)}) collective-permute-start(bf16[304,256]{1,0:T(8,128)(2,1)S(1)} %get-tuple-element.37), channel_id=1, source_target_pairs={{0,4},{4,0},{8,12},{12,8},{16,20},{20,16},{24,28},{28,24},{1,5},{5... | collective-permute-start | bytes 466952 | tf_op jit(solution)/shard_map/ppermute | solution.py:13
  46.5 9.3 %collective-permute-start.1 = (f32[2,2,96,96]{3,2,1,0:T(8,128)S(1)}, f32[2,2,96,96]{3,2,1,0:T(8,128)S(1)}, u32[]{:S(2)}, u32[]{:S(2)}) collective-permute-start(f32[2,2,96,96]{3,2,1,0:T(8,128)S(1)} %pad_maximum_fusion.4), channel_id=1, source_target_pairs={{0,8},{4,12},{8,0},{12,4},{16,24},{20,28},{24,16},{28,20},{1,9},{5... | collective-permute-start | bytes 442376 | tf_op jit(solution)/shard_map/ppermute | solution.py:13
  53.1 1.0 copy-start.1
  55.8 1.7 %copy-start.6 = (f32[2,2,96,96]{3,2,1,0:T(8,128)}, f32[2,2,96,96]{3,2,1,0:T(8,128)S(1)}, u32[]{:S(2)}) copy-start(f32[2,2,96,96]{3,2,1,0:T(8,128)S(1)} %collective-permute-done.1) | copy-start | bytes 442372
  57.5 11.1 %collective-permute-start.2 = (f32[4,2,96,96]{3,2,1,0:T(8,128)}, f32[4,2,96,96]{3,2,1,0:T(8,128)}, u32[]{:S(2)}, u32[]{:S(2)}) collective-permute-start(f32[4,2,96,96]{3,2,1,0:T(8,128)} %pad_maximum_fusion.1), channel_id=1, source_target_pairs={{0,4},{4,0},{8,12},{12,8},{16,20},{20,16},{24,28},{28,24},{1,5},{5... | collective-permute-start | bytes 884744 | tf_op jit(solution)/shard_map/ppermute | solution.py:13
  60.8 1.8 %copy-start.2 = (f32[5,2048,24]{1,2,0:T(8,128)S(1)}, f32[5,2048,24]{1,2,0:T(8,128)}, u32[]{:S(2)}) copy-start(f32[5,2048,24]{1,2,0:T(8,128)} %copy-done.1) | copy-start | bytes 2949124
  62.4 6.2 %copy-start.7 = (f32[2,2,96,96]{3,2,1,0:T(8,128)S(1)}, f32[2,2,96,96]{3,2,1,0:T(8,128)}, u32[]{:S(2)}) copy-start(f32[2,2,96,96]{3,2,1,0:T(8,128)} %copy-done.6) | copy-start | bytes 442372
  62.6 7.2 %copy-start.11 = (pred[8,4,24,96]{3,2,1,0:T(8,128)(4,1)}, pred[8,4,24,96]{3,2,1,0:T(8,128)(4,1)S(1)}, u32[]{:S(2)}) copy-start(pred[8,4,24,96]{3,2,1,0:T(8,128)(4,1)S(1)} %iota_compare_fusion.6) | copy-start | bytes 221188
  93.7 7.4 %copy-start.14 = (s32[1,1,24]{2,1,0:T(1,128)S(1)}, s32[1,1,24]{2,1,0:T(1,128)}, u32[]{:S(2)}) copy-start(s32[1,1,24]{2,1,0:T(1,128)} %param.18) | copy-start | bytes 292
  93.7 7.7 %copy-start.10 = (bf16[1,1,24,2048]{3,2,1,0:T(8,128)(2,1)S(1)}, bf16[1,1,24,2048]{3,2,1,0:T(8,128)(2,1)}, u32[]{:S(2)}) copy-start(bf16[1,1,24,2048]{3,2,1,0:T(8,128)(2,1)} %param.17) | copy-start | bytes 294916
  95.2 4.7 %collective-permute-start.4 = (f32[64,144]{1,0:T(8,128)S(1)}, f32[64,144]{1,0:T(8,128)S(1)}, u32[]{:S(2)}, u32[]{:S(2)}) collective-permute-start(f32[64,144]{1,0:T(8,128)S(1)} %get-tuple-element.39), channel_id=1, source_target_pairs={{0,2},{1,3},{2,0},{3,1},{4,6},{5,7},{6,4},{7,5},{8,10},{9,11},{10,... | collective-permute-start | bytes 110600 | tf_op jit(solution)/shard_map/ppermute | solution.py:13
  96.8 3.2 %collective-permute-start.3 = (f32[64,144]{1,0:T(8,128)S(1)}, f32[64,144]{1,0:T(8,128)S(1)}, u32[]{:S(2)}, u32[]{:S(2)}) collective-permute-start(f32[64,144]{1,0:T(8,128)S(1)} %get-tuple-element.40), channel_id=1, source_target_pairs={{0,1},{1,0},{2,3},{3,2},{4,5},{5,4},{6,7},{7,6},{8,9},{9,8},{10,11... | collective-permute-start | bytes 110600 | tf_op jit(solution)/shard_map/ppermute | solution.py:13
  96.8 3.7 %collective-permute-start.5 = (f32[64,144]{1,0:T(8,128)S(1)}, f32[64,144]{1,0:T(8,128)S(1)}, u32[]{:S(2)}, u32[]{:S(2)}) collective-permute-start(f32[64,144]{1,0:T(8,128)S(1)} %get-tuple-element.41), channel_id=1, source_target_pairs={{0,3},{1,2},{2,1},{3,0},{4,7},{5,6},{6,5},{7,4},{8,11},{9,10},{10,... | collective-permute-start | bytes 110600 | tf_op jit(solution)/shard_map/ppermute | solution.py:13
  101.3 1.2 %copy-start.8 = (bf16[5,256,256]{2,1,0:T(8,128)(2,1)S(1)}, bf16[5,256,256]{2,1,0:T(8,128)(2,1)}, u32[]{:S(2)}) copy-start(bf16[5,256,256]{2,1,0:T(8,128)(2,1)} %slice.302) | copy-start | bytes 1966084
  102.5 2.6 %copy-start.3 = (f32[2048,96]{0,1:T(8,128)S(1)}, f32[2048,96]{0,1:T(8,128)}, u32[]{:S(2)}) copy-start(f32[2048,96]{0,1:T(8,128)} %convolution_add_fusion.2) | copy-start | bytes 2359300
  102.5 2.6 %copy-start.4 = (f32[2048,24]{0,1:T(8,128)S(1)}, f32[2048,24]{0,1:T(8,128)}, u32[]{:S(2)}) copy-start(f32[2048,24]{0,1:T(8,128)} %get-tuple-element.29) | copy-start | bytes 589828
  102.5 2.6 %copy-start.5 = (f32[2048,24]{0,1:T(8,128)S(1)}, f32[2048,24]{0,1:T(8,128)}, u32[]{:S(2)}) copy-start(f32[2048,24]{0,1:T(8,128)} %get-tuple-element.30) | copy-start | bytes 589828

commit v2 on v0

v2 whole, which is shorter than its diff:
```python
import functools

import jax
import jax.numpy as jnp
from jax import lax
from jax.experimental import pallas as pl
from jax.experimental.pallas import tpu as pltpu
from jax.sharding import PartitionSpec as P


f32 = jnp.float32
bf16 = jnp.bfloat16
LANES = 128
GROUP = 32


def swap(block, axis, mask):
    count = lax.axis_size(axis)
    return lax.ppermute(block, axis, [(i, i ^ mask) for i in range(count)])


def swap_odd(block, axis):
    count = lax.axis_size(axis)
    pairs = [(i, i + 1) for i in range(1, count - 1, 2)]
    return lax.ppermute(block, axis, pairs + [(b, a) for a, b in pairs])


def ceil_lanes(size):
    return -(-size // LANES) * LANES


def iota(shape, axis):
    return lax.broadcasted_iota(jnp.int32, shape, axis)


def dot(left, right):
    return jnp.dot(left, right, preferred_element_type=f32)


def split_two(value):
    high = value.astype(bf16)
    return high, (value - high.astype(f32)).astype(bf16)


def split_three(value):
    high = value.astype(bf16)
    rest = value - high.astype(f32)
    middle = rest.astype(bf16)
    return high, middle, (rest - middle.astype(f32)).astype(bf16)


def turned_scale(scale_ref):
    scale = scale_ref[...]
    return jnp.concatenate(
        [scale, jnp.zeros((LANES - scale.shape[0], LANES), f32)], axis=0
    ).T


def fixed(shape):
    return pl.BlockSpec(shape, lambda i: (0,) * len(shape))


def call(kernel, outs, in_specs, args, grid=(1,), out_specs=None, scratch=(), flops=0, limit=24):
    many = isinstance(outs, (list, tuple))
    if out_specs is None:
        out_specs = [fixed(o.shape) for o in outs] if many else fixed(outs.shape)
    in_specs = [fixed(a.shape) if s is None else s for s, a in zip(in_specs, args)]
    sizes = [a.size * a.dtype.itemsize for a in list(args) + (list(outs) if many else [outs])]
    return pl.pallas_call(
        kernel,
        out_shape=outs,
        grid=grid,
        in_specs=in_specs,
        out_specs=out_specs,
        scratch_shapes=list(scratch),
        compiler_params=pltpu.CompilerParams(vmem_limit_bytes=limit << 20),
        cost_estimate=pl.CostEstimate(flops=flops, bytes_accessed=sum(sizes), transcendentals=0),
    )(*args)


def join_kernel(*refs):
    start = 0
    for ref in refs[:-2]:
        refs[-1][start : start + ref.shape[0]] = ref[...]
        start += ref.shape[0]


def join(parts, after):
    total = sum(p.shape[0] for p in parts)
    out = jax.ShapeDtypeStruct((total,) + parts[0].shape[1:], parts[0].dtype)
    corner = pl.BlockSpec((16, LANES), lambda i: (0, 0))
    return call(join_kernel, out, [None] * len(parts) + [corner], (*parts, after))


def copies(sources, targets, sems):
    moves = [pltpu.make_async_copy(a, b, sems.at[i]) for i, (a, b) in enumerate(zip(sources, targets))]
    for move in moves:
        move.start()
    return moves


def front_kernel(slabs, groups, res_any, scale_any, basis_any, map_any, weighted_any, sent_ref, res_ref, scale_ref, basis_ref, map_ref, weighted_ref, in_sems, out_sems):
    rows = res_ref.shape[0]
    chunk = min(rows, 512)
    parts = [pl.ds(i * chunk, chunk) for i in range(rows // chunk)]
    sources = [scale_any, basis_any, map_any] + [res_any.at[p] for p in parts]
    targets = [scale_ref, basis_ref, map_ref] + [res_ref.at[p] for p in parts]
    moves = copies(sources, targets, in_sems)
    for move in moves[:3]:
        move.wait()
    scale_turned = turned_scale(scale_ref)
    primal, leaving = None, []
    for i, p in enumerate(parts):
        moves[3 + i].wait()
        for j in range(chunk // LANES):
            here = slice(i * chunk + j * LANES, i * chunk + (j + 1) * LANES)
            column = i * (chunk // LANES) + j
            factor = scale_turned[:, column : column + 1]
            weighted_ref[here, :] = (factor * res_ref[here, :].astype(f32)).astype(bf16)
        leave = pltpu.make_async_copy(weighted_ref.at[p], weighted_any.at[p], out_sems.at[i])
        leave.start()
        leaving.append(leave)
        term = dot(basis_ref[:, i * chunk : (i + 1) * chunk], weighted_ref[i * chunk : (i + 1) * chunk, :])
        primal = term if primal is None else primal + term
    constraints, columns = primal.shape
    turned = jnp.concatenate([primal, jnp.zeros((LANES - constraints, columns), f32)], axis=0).T
    quarter = sent_ref.shape[1]
    spare = GROUP - constraints
    code = map_ref[...].astype(f32)
    code = jnp.concatenate([code, jnp.zeros((1, LANES - constraints), f32)], axis=1)
    lanes = iota((1, LANES), 1)
    tail = jnp.zeros((1, LANES), f32)
    for q in range(-(-constraints // spare)):
        start = GROUP * q + constraints
        inside = (lanes >= start) & (lanes < start + min(spare, constraints - spare * q))
        tail = jnp.where(inside, pltpu.roll(code, start - spare * q, 1), tail)
    tail = jnp.where(iota((quarter, LANES), 0) == 0, tail, 0.0)
    for m in range(groups):
        piece = tail
        for g in range(4):
            start = (m * 4 + g) * quarter
            part = turned[start : start + quarter, :]
            piece = piece + (pltpu.roll(part, GROUP * g, 1) if g else part)
        for v in range(slabs):
            sent_ref[v * groups + m] = piece
    for leave in leaving:
        leave.wait()


def scale_columns(turned_ref, step, block):
    lanes = iota((LANES, LANES), 1)
    for j in range(block // LANES):
        hit = jnp.where(lanes == step * (block // LANES) + j, turned_ref[...], 0.0)
        yield jnp.sum(hit, axis=1, keepdims=True)


def place_of():
    return lax.axis_index("wide"), lax.axis_index("narrow")


def slot_rows(groups):
    w, n = place_of()
    parity = w & 1
    return [n ^ k for k in range(1, groups)] + [groups + 1 - parity, groups + parity]


def local_kernel(inverse_any, weighted_any, scale_any, part_ref, narrow_ref, mark_ref, inverse_ref, weighted_ref, scale_ref, turned_ref, sems):
    rows = inverse_ref.shape[0]
    block = min(rows, 256)
    steps = rows // block
    sources, targets = [scale_any, weighted_any], [scale_ref, weighted_ref]
    for i in range(steps):
        p = pl.ds(i * block, block)
        sources.append(inverse_any.at[p])
        targets.append(inverse_ref.at[p])
    moves = copies(sources, targets, sems)
    for move in moves[:2]:
        move.wait()
    turned_ref[...] = turned_scale(scale_ref)
    mark_ref[...] = jnp.zeros_like(mark_ref)

    def one(i, carry):
        p = pl.ds(pl.multiple_of(i * block, block), block)
        pltpu.make_async_copy(inverse_any.at[p], inverse_ref.at[p], sems.at[2 + i]).wait()
        part = dot(inverse_ref[p, :], weighted_ref[...])
        factors = scale_columns(turned_ref, i, block)
        scaled = jnp.concatenate(list(factors), axis=0) * part
        part_ref[p, :] = scaled
        narrow_ref[p, :] = scaled.astype(bf16)
        return carry

    lax.fori_loop(0, steps, one, 0)


def pick_kernel(groups, narrow_ref, lane_scale_ref, basis_ref, index_ref, *rest):
    slots = groups + 1
    outs, basis = rest[:slots], rest[slots]
    capacity = index_ref.shape[2]
    constraints, total = basis_ref.shape
    picks = [index_ref[r] for r in slot_rows(groups)]
    rows = picks + [jnp.zeros((LANES - slots, capacity), jnp.int32)]
    columns_of = jnp.concatenate(rows, axis=0).astype(f32).T
    basis[...] = lane_scale_ref[...] * basis_ref[...].astype(f32)
    lanes = iota((capacity, LANES), 1).astype(f32)
    for k in range(slots):
        spot = jnp.broadcast_to(columns_of[:, k : k + 1], (capacity, LANES))
        hots = [(spot == lanes + float(j * LANES)).astype(f32).astype(bf16) for j in range(total // LANES)]
        outs[k][:capacity, :] = dot(jnp.concatenate(hots, axis=1), narrow_ref[...]).astype(bf16)
        parts = []
        for c in range(capacity // LANES):
            spot = jnp.broadcast_to(picks[k][:, c * LANES : (c + 1) * LANES], (constraints, LANES))
            inner, outer = spot & (LANES - 1), spot // LANES
            value = jnp.zeros((constraints, LANES), f32)
            for j in range(total // LANES):
                found = jnp.take_along_axis(basis[:, j * LANES : (j + 1) * LANES], inner, axis=1)
                value = jnp.where(outer == j, found, value)
            parts.append(value)
        fill = jnp.zeros((GROUP - constraints, capacity), f32)
        outs[k][capacity:, :] = jnp.concatenate([jnp.concatenate(parts, axis=1), fill], axis=0).astype(bf16)


def unpack_kernel(slabs, groups, constraints, got_ref, right_ref, maps_ref):
    pieces, quarter, _ = got_ref.shape
    spare = GROUP - constraints
    heads = jnp.concatenate([got_ref[i, 0:1, :] for i in range(pieces)], axis=0)
    lanes = iota((pieces, LANES), 1)
    maps = jnp.full((pieces, LANES), -1.0, f32)
    for q in range(-(-constraints // spare)):
        shift = (spare * q - GROUP * q - constraints) % LANES
        moved = pltpu.roll(heads, shift, 1) if shift else heads
        inside = (lanes >= spare * q) & (lanes < min(spare * (q + 1), constraints))
        maps = jnp.where(inside, moved, maps)
    maps_ref[...] = maps
    order = right_ref.shape[2]
    halves = groups * GROUP // LANES
    lanes = iota((quarter, LANES), 1) // GROUP
    wide = iota((1, LANES), 1) // GROUP

    def one(v, carry):
        value, codes = [], []
        for h in range(halves):
            rows = []
            for g in range(4):
                row = None
                for j in range(4):
                    part = got_ref[v * groups + 4 * h + j]
                    shift = (GROUP * (j - g)) % LANES
                    part = pltpu.roll(part, shift, 1) if shift else part
                    row = part if row is None else jnp.where(lanes == j, part, row)
                rows.append(row)
            value.append(jnp.concatenate(rows, axis=0))
            code = None
            for j in range(4):
                part = maps_ref[pl.ds(v * groups + 4 * h + j, 1), :]
                part = pltpu.roll(part, GROUP * j, 1) if j else part
                code = part if code is None else jnp.where(wide == j, part, code)
            codes.append(code)
        value = jnp.concatenate(value, axis=1) if halves > 1 else value[0]
        code = jnp.concatenate(codes, axis=1) if halves > 1 else codes[0]
        hot = (iota((order, halves * LANES), 0).astype(f32) == code).astype(f32).astype(bf16)
        stacked = jnp.concatenate(split_three(value), axis=0)
        total = lax.dot_general(stacked, hot, (((1,), (1,)), ((), ())), preferred_element_type=f32)
        c = value.shape[0]
        right_ref[v] = total[:c] + total[c : 2 * c] + total[2 * c :]
        return carry

    lax.fori_loop(0, slabs, one, 0, unroll=slabs <= 8)


def solve_kernel(slabs, groups, constraints, offsets, right_ref, maps_ref, *rest):
    count = len(offsets).bit_length()
    mine, other = rest[:count], rest[count : 2 * count]
    shares = rest[2 * count : 2 * count + groups]
    raw, forward, backward, pivots, solved = rest[2 * count + groups :]
    w, n = place_of()
    core = n & 1
    size = mine[0].shape[1]
    order = raw.shape[2]
    if size != order:
        raw[...] = jnp.zeros_like(raw)
    start = 0
    for a, b in zip(mine, other):
        for i in range(a.shape[0]):
            slab = w ^ offsets[start + i]
            raw[core, slab, :size, :size] = a[i]
            raw[1 - core, slab, :size, :size] = b[i]
        start += a.shape[0]
    c = right_ref.shape[1]
    few = slabs <= 8

    def prepare(v, carry):
        sub = raw[0, v]
        for ref, value in ((forward, sub.T), (backward, sub), (pivots, raw[1, v])):
            high, low = split_two(value)
            ref[v, :, :order] = high
            ref[v, :, order:] = low
        return carry

    def times(value, factor):
        total = dot(jnp.concatenate(split_two(value), axis=0), factor)
        return total[:c, :order] + (total[:c, order:] + total[c:, :order])

    def down(v, value):
        value = right_ref[v] - times(value, forward[v])
        solved[v] = value
        return value

    def pivot(v, carry):
        solved[v] = times(solved[v], pivots[v])
        return carry

    def up(i, value):
        v = slabs - 2 - i
        value = solved[v] - times(value, backward[v + 1])
        solved[v] = value
        return value

    lax.fori_loop(0, slabs, prepare, 0, unroll=few)
    solved[0] = right_ref[0]
    lax.fori_loop(1, slabs, down, right_ref[0], unroll=few)
    lax.fori_loop(0, slabs, pivot, 0, unroll=few)
    lax.fori_loop(0, slabs - 1, up, solved[slabs - 1], unroll=few)

    parity = w & 1
    sides = [w, w ^ 1, jnp.clip(w - 1 + 2 * parity, 0, slabs - 1)]
    value = jnp.concatenate([solved[s] for s in sides], axis=1)
    stacked = jnp.concatenate(split_three(value), axis=0)
    width = shares[0].shape[1]
    lanes = iota((1, width), 1)
    rows = iota((order, width), 0).astype(f32)
    starts = [
        [size + (2 + i) * constraints for i in range(3)],
        [size],
        [size + constraints],
    ]
    for k in range(groups):
        hots = []
        for s, (side, places) in enumerate(zip(sides, starts)):
            code = maps_ref[pl.ds(side * groups + (n ^ k), 1), :]
            code = jnp.concatenate([code, jnp.full((1, width - LANES), -1.0, f32)], axis=1)
            full = jnp.where(lanes < size, lanes.astype(f32), -1.0) if s == 0 else jnp.full((1, width), -1.0, f32)
            for place in places:
                inside = (lanes >= place) & (lanes < place + constraints)
                full = jnp.where(inside, pltpu.roll(code, place, 1), full)
            hots.append((rows == full).astype(f32).astype(bf16))
        total = dot(stacked, jnp.concatenate(hots, axis=0))
        shares[k][...] = total[:c] + total[c : 2 * c] + total[2 * c :]


def scatter_kernel(groups, size, length_ref, index_ref, maps_ref, lane_scale_ref, basis_ref, *rest):
    slots = groups + 1
    arrived = rest[:slots]
    early_ref, late_ref, own_ref, joined, targets = rest[slots:]
    step = pl.program_id(0)
    columns, width = early_ref.shape[1], late_ref.shape[1]
    block = early_ref.shape[0] // pl.num_programs(0)
    here_rows = pl.ds(pl.multiple_of(step * block, block), block)
    constraints = basis_ref.shape[0]
    capacity = index_ref.shape[2]
    w, n = place_of()

    @pl.when(step == 0)
    def _():
        for k, r in enumerate(slot_rows(groups)):
            spot = index_ref[r]
            live = iota((1, capacity), 1) < length_ref[r]
            targets[:, k * capacity : (k + 1) * capacity] = jnp.where(live, spot, -1)
            here = slice(k * capacity, (k + 1) * capacity)
            joined[here, :columns] = arrived[k][:capacity, :]
            lanes = iota((1, LANES), 1)
            if k < groups - 1:
                code = maps_ref[pl.ds(w * groups + (n ^ (k + 1)), 1), :]
            else:
                start = size + (k - groups + 1) * constraints
                code = jnp.where(lanes < constraints, lanes + start, -1).astype(f32)
            hot = (iota((width, LANES), 0).astype(f32) == code).astype(f32).astype(bf16)
            spread = dot(hot[:, :GROUP], arrived[k][capacity:, :])
            joined[here, columns:] = spread.T.astype(bf16)

    rows = iota((block, capacity), 0) + step * block
    hots = []
    for k in range(slots):
        target = targets[:, k * capacity : (k + 1) * capacity]
        hots.append((rows == target).astype(f32).astype(bf16))
    total = dot(jnp.concatenate(hots, axis=1), joined[...])
    early_ref[here_rows, :] = total[:, :columns]
    late_ref[here_rows, :] = total[:, columns:].astype(bf16)
    scaled = lane_scale_ref[...] * basis_ref[...].astype(f32)
    high = scaled.astype(bf16).astype(f32)
    start = size + 2 * constraints
    stop = start + 3 * constraints
    stack = jnp.concatenate(
        [jnp.zeros((start, block), f32), high, scaled - high, high, jnp.zeros((width - stop, block), f32)],
        axis=0,
    )
    own_ref[here_rows, :] = stack.T.astype(bf16)


def final_kernel(groups, size, constraints, part_ref, early_ref, late_ref, own_ref, *rest):
    pieces = rest[:groups]
    out_ref, values, highs, lows, owns = rest[groups:]
    _, n = place_of()

    @pl.when(pl.program_id(0) == 0)
    def _():
        c = pieces[0].shape[0]
        for k in range(groups):
            values[pl.ds(pl.multiple_of((n ^ k) * c, c), c), :] = pieces[k][...]
        value = values[...].T
        high = value.astype(bf16).astype(f32)
        low = value - high
        highs[...] = high.astype(bf16)
        lows[...] = low.astype(bf16)
        upper = iota(value.shape, 0) < size + 4 * constraints
        owns[...] = jnp.where(upper, high, low).astype(bf16)

    block = out_ref.shape[0]
    here = pl.ds(pl.multiple_of(pl.program_id(0) * block, block), block)
    late = late_ref[here, :]
    combined = (part_ref[here, :] + dot(own_ref[here, :], owns[...])).astype(bf16).astype(f32)
    out_ref[...] = combined + (early_ref[here, :] + (dot(late, highs[...]) + dot(late, lows[...])))


def body(
    residual,
    scaling,
    local_inverse,
    coarse_basis,
    primal_map,
    slot_index,
    slot_length,
    coarse_sub,
    coarse_pivot,
):
    slabs, groups = lax.axis_size("wide"), lax.axis_size("narrow")
    n = lax.axis_index("narrow")
    residual, inverse = residual[0, 0], local_inverse[0, 0]
    basis = coarse_basis[0, 0]
    slots, capacity = slot_index.shape[2] - 1, slot_index.shape[3]
    index = slot_index.reshape(slots + 1, 1, capacity)
    length = slot_length[0, 0]
    size = coarse_sub.shape[1]
    order = ceil_lanes(size)
    rows, columns = residual.shape
    constraints = basis.shape[0]
    own_columns = columns // groups
    quarter = own_columns // 4
    width = ceil_lanes(size + 5 * constraints)
    scale = scaling[0, 0].reshape(rows // LANES, LANES)
    lane_scale = scaling[0]
    smem = pl.BlockSpec(memory_space=pltpu.SMEM)
    struct = jax.ShapeDtypeStruct

    def by_rows(block, cols):
        return pl.BlockSpec((block, cols), lambda i: (i, 0))

    def by_lanes(count, block):
        return pl.BlockSpec((count, block), lambda i: (0, i))

    any_space = pl.BlockSpec(memory_space=pl.ANY)
    vmem = pl.BlockSpec(memory_space=pltpu.VMEM)
    factor = jnp.where((n & 1) == 0, coarse_sub, coarse_pivot)
    chunks = -(-rows // 512)
    weighted, sent = call(
        functools.partial(front_kernel, slabs, groups),
        [struct((rows, columns), bf16), struct((slabs * groups, quarter, LANES), f32)],
        [any_space] * 4,
        (residual, scale, basis, primal_map[0]),
        out_specs=[any_space, fixed((slabs * groups, quarter, LANES))],
        scratch=[
            pltpu.VMEM((rows, columns), bf16),
            pltpu.VMEM(scale.shape, f32),
            pltpu.VMEM(basis.shape, bf16),
            pltpu.VMEM(primal_map[0].shape, jnp.int32),
            pltpu.VMEM((rows, columns), bf16),
            pltpu.SemaphoreType.DMA((3 + chunks,)),
            pltpu.SemaphoreType.DMA((chunks,)),
        ],
        flops=2 * constraints * rows * columns,
        limit=62,
    )
    got = lax.all_to_all(sent, ("wide", "narrow"), split_axis=0, concat_axis=0, tiled=True)

    part, narrow, mark = call(
        local_kernel,
        [struct((rows, columns), f32), struct((rows, columns), bf16), struct((16, LANES), f32)],
        [any_space] * 3,
        (inverse, weighted, scale),
        out_specs=[vmem] * 3,
        scratch=[
            pltpu.VMEM((rows, rows), bf16),
            pltpu.VMEM((rows, columns), bf16),
            pltpu.VMEM(scale.shape, f32),
            pltpu.VMEM((LANES, LANES), f32),
            pltpu.SemaphoreType.DMA((2 + rows // min(rows, 256),)),
        ],
        flops=2 * rows * columns * rows,
        limit=57,
    )
    outgoing = call(
        functools.partial(pick_kernel, groups),
        [struct((capacity + GROUP, columns), bf16)] * slots,
        [vmem] + [None] * 3,
        (narrow, lane_scale, basis, index),
        scratch=[pltpu.VMEM((constraints, rows), f32)],
        flops=2 * rows * columns * slots * capacity,
    )
    waits = [weighted] + [mark] * slabs
    mine, held, offsets, mask = [factor], factor, [0], slabs // 2
    while mask:
        mine.append(swap(held, "wide", mask))
        offsets = offsets + [o ^ mask for o in offsets]
        mask //= 2
        if mask:
            held = join(mine, waits[len(mine) - 2])
    other = []
    for piece in mine:
        other.append(swap(piece, "narrow", 1))
    arrived = []
    for k in range(slots):
        if k < groups - 1:
            arrived.append(swap(outgoing[k], "narrow", k + 1))
        elif k == groups - 1:
            arrived.append(swap(outgoing[k], "wide", 1))
        else:
            arrived.append(swap_odd(outgoing[k], "wide"))

    right, maps = call(
        functools.partial(unpack_kernel, slabs, groups, constraints),
        [struct((slabs, own_columns, order), f32), struct((slabs * groups, LANES), f32)],
        [None],
        (got,),
        flops=2 * slabs * 3 * own_columns * LANES * order,
    )
    shares = call(
        functools.partial(solve_kernel, slabs, groups, constraints, offsets),
        [struct((own_columns, width), f32)] * groups,
        [None] * (2 + len(mine) + len(other)),
        (right, maps, *mine, *other),
        scratch=[
            pltpu.VMEM((2, slabs, order, order), f32),
            pltpu.VMEM((slabs, order, 2 * order), bf16),
            pltpu.VMEM((slabs, order, 2 * order), bf16),
            pltpu.VMEM((slabs, order, 2 * order), bf16),
            pltpu.VMEM((slabs, own_columns, order), f32),
        ],
        flops=2 * 3 * slabs * 2 * own_columns * order * 2 * order,
        limit=24 if slabs <= 8 else 62,
    )
    pieces = [shares[0]] + [swap(shares[k], "narrow", k) for k in range(1, groups)]

    block = min(rows, 512)
    early, late, own = call(
        functools.partial(scatter_kernel, groups, size),
        [struct((rows, columns), f32), struct((rows, width), bf16), struct((rows, width), bf16)],
        [smem, None, None, by_lanes(1, block), by_lanes(constraints, block)] + [None] * slots,
        (length, index, maps, lane_scale, basis, *arrived),
        grid=(rows // block,),
        out_specs=[vmem] * 3,
        scratch=[
            pltpu.VMEM((slots * capacity, columns + width), bf16),
            pltpu.VMEM((1, slots * capacity), jnp.int32),
        ],
        flops=2 * rows * slots * capacity * (columns + width),
    )
    result = call(
        functools.partial(final_kernel, groups, size, constraints),
        struct((rows, columns), f32),
        [vmem] * 4 + [None] * groups,
        (part, early, late, own, *pieces),
        grid=(rows // block,),
        out_specs=by_rows(block, columns),
        scratch=[
            pltpu.VMEM((columns, width), f32),
            pltpu.VMEM((width, columns), bf16),
            pltpu.VMEM((width, columns), bf16),
            pltpu.VMEM((width, columns), bf16),
        ],
        flops=2 * rows * columns * 3 * width,
    )
    return result[None, None]


def solution(mesh):
    in_specs = (
        P("wide", "narrow", None, None),
        P("wide", "narrow", None),
        P("wide", "narrow", None, None),
        P("wide", "narrow", None, None),
        P("wide", "narrow", None),
        P("wide", "narrow", None, None),
        P("wide", "narrow", None),
        P("wide", None, None),
        P("wide", None, None),
    )
    out_specs = P("wide", "narrow", None, None)

    return jax.shard_map(body, mesh=mesh, in_specs=in_specs, out_specs=out_specs, check_vma=False)
```

time: 195 us -> 52.3 us (0.27)
  blocking collectives: 132 us -> 0 us
  Pallas kernels: 0 us -> 22.7 us
  matrix products: 14.4 us -> 0 us
  between operations: 13.6 us -> 0.17 us
  other arithmetic: 12.2 us -> 0.81 us
  starting transfers between devices: 8.46 us -> 19.4 us
  local copies, waits for them, and re-layouts: 8.77 us -> 3.15 us
    all_gather x5 -> x0, blocking collectives: 132 us -> none  [the longest x4 127 us: entering(): gathered = jax.tree.map(lambda a: lax.all_gather(a, axis), part)]
    pallas_call x0 -> x9, Pallas kernels: none -> 22.7 us  [call(): pl.pallas_call(kernel, out_shape=outs, grid=grid, in_specs=in_specs, out_...]
    dot_general x15 -> x0, matrix products: 14.4 us -> none  [the longest x1 6.48 us: body(): jnp.dot(local_inverse[0, 0], weighted, preferred_element_type=jnp.float32)]
    scatter-add x1 -> x0, other arithmetic: 11.7 us -> none  [body(): summed = combined.astype(jnp.float32).at[indices.reshape(-1)].add(incomin...]
    ppermute x2 -> x15, starting transfers between devices: 4.95 us -> 15.5 us  [the longest x14 14.9 us: swap(): return lax.ppermute(block, axis, [(i, i ^ mask) for i in range(count)])]
    gather x1 -> x0, local copies, waits for them, and re-layouts: 4.76 us -> none  [body(): combined[indices]]
    unnamed x15 -> x16, local copies, waits for them, and re-layouts: 0.99 us -> 3.15 us
    convert_element_type x2 -> x0, local copies, waits for them, and re-layouts: 2.14 us -> none  [the longest x1 1.61 us: body(): combined.astype(jnp.float32).at[indices.reshape(-1)]]
  transfers between devices with their start and end apart: 4 -> 16, of which waited for: 2 -> 1; matrix products, arithmetic and copies ran while one was open for 4% -> 0% of each run, Pallas kernels for 0% -> 38%
where the time goes in v2:
time: 52.3 us; the launch traced here: 51.4 us
  Pallas kernels  22.7 us (43%)
  starting transfers between devices  19.4 us (37%)
  waiting for transfers between devices  5.26 us (10%)
  local copies, waits for them, and re-layouts  3.15 us (6%)
  other arithmetic  0.81 us (2%)
    pallas_call x9, Pallas kernels, call(): pl.pallas_call(kernel, out_shape=outs, grid=grid, in_specs=in_specs, out_...  22.7 us
    ppermute x14, starting transfers between devices, swap(): return lax.ppermute(block, axis, [(i, i ^ mask) for i in range(count)])  14.9 us
    ppermute x14, waiting for transfers between devices, swap(): return lax.ppermute(block, axis, [(i, i ^ mask) for i in range(count)])  5.26 us
    all_to_all x1, starting transfers between devices, body(): lax.all_to_all(sent, ('wide', 'narrow'), split_axis=0, concat_axis=0, til...  3.83 us
    unnamed x16, local copies, waits for them, and re-layouts  3.15 us
  transfers between devices with their start and end apart: 16, of which 1 were waited for; matrix products, arithmetic and copies ran while one was open for 0% of the time, Pallas kernels for 38%

profile of v2, /device:TPU:0, one launch (start us, length us, event | category | flops | bytes accessed | tf_op | source)
XLA Modules:
  0.0 51.4 jit_solution(8167303167931897114)
XLA Ops:
  0.0 0.8 %broadcast_select_fusion.refs_0_.rest_0_ = f32[1,96,96]{2,1,0:T(8,128)S(1)} fusion(f32[1,96,96]{2,1,0:T(8,128)} %param.16, f32[1,96,96]{2,1,0:T(8,128)} %param.17, pred[]{:T(512)S(6)} %eq.3), kind=kLoop, calls=%fused_computation | loop fusion | flops 9216 | bytes 110593 | tf_op jit(solution)/shard_map/jit(_where)/select_n | solution.py:462
  0.8 4.1 %collective-permute-start.5 = (f32[1,96,96]{2,1,0:T(8,128)S(1)}, f32[1,96,96]{2,1,0:T(8,128)S(1)}, u32[]{:S(2)}, u32[]{:S(2)}) collective-permute-start(f32[1,96,96]{2,1,0:T(8,128)S(1)} %broadcast_select_fusion.refs_0_.rest_0_), channel_id=1, source_target_pairs={{0,16},{4,20},{8,24},{12,28},{16,0},{20,4},{24,8},{28,12},{1,17},{... | collective-permute-start | bytes 110600 | tf_op jit(solution)/shard_map/ppermute | solution.py:19
  4.9 3.3 %shard_map.91 = (bf16[2048,256]{1,0:T(8,128)(2,1)}, f32[32,16,128]{2,1,0:T(8,128)}) custom-call(bf16[2048,256]{1,0:T(8,128)(2,1)} %bitcast.20, f32[16,128]{1,0:T(8,128)} %bitcast.12, bf16[24,2048]{1,0:T(8,128)(2,1)} %bitcast.9, s32[1,24]{1,0:T(1,128)} %bitcast.21), custom_call_target="tpu_custom_call" | custom-call | flops 25165824 | bytes 2465888 | tf_op jit(solution)/shard_map/pallas_call | solution.py:69
  8.2 3.8 %all-to-all-start = ((f32[32,16,128]{2,1,0:T(8,128)}), f32[32,16,128]{2,1,0:T(8,128)S(1)}, u32[]{:S(2)}, u32[]{:S(2)}) async-start(f32[32,16,128]{2,1,0:T(8,128)} %get-tuple-element.26), calls=%async_computation | async-start | bytes 524288 | tf_op jit(solution)/shard_map/all_to_all | solution.py:482
  12.0 0.0 collective-permute-done.5.refs_1_.rest_1_
  12.0 0.0 copy-start
  12.1 1.2 %copy-done = bf16[2048,256]{1,0:T(8,128)(2,1)S(1)} copy-done((bf16[2048,256]{1,0:T(8,128)(2,1)S(1)}, bf16[2048,256]{1,0:T(8,128)(2,1)}, u32[]{:S(2)}) %copy-start) | copy-done | bytes 1048600
  13.3 1.8 %collective-permute-start.6 = (f32[2,96,96]{2,1,0:T(8,128)S(1)}, f32[2,96,96]{2,1,0:T(8,128)S(1)}, u32[]{:S(2)}, u32[]{:S(2)}) collective-permute-start(f32[2,96,96]{2,1,0:T(8,128)S(1)} %shard_map.96), channel_id=1, source_target_pairs={{0,8},{4,12},{8,0},{12,4},{16,24},{20,28},{24,16},{28,20},{1,9},{5... | collective-permute-start | bytes 221192 | tf_op jit(solution)/shard_map/ppermute | solution.py:19
  15.1 6.9 %shard_map.92 = (f32[2048,256]{1,0:T(8,128)}, bf16[2048,256]{1,0:T(8,128)(2,1)}, f32[16,128]{1,0:T(8,128)}) custom-call(bf16[2048,2048]{1,0:T(8,128)(2,1)} %bitcast.19, bf16[2048,256]{1,0:T(8,128)(2,1)} %get-tuple-element.24.weighted_any.refs_2_, f32[16,128]{1,0:T(8,128)} %bitcast.13), custom_call_target="tpu_custom_call" | custom-call | flops 2147483648 | bytes 12599296 | tf_op jit(solution)/shard_map/pallas_call | solution.py:69
  22.0 0.0 collective-permute-done.6.refs_2_.rest_2_
  22.0 0.0 copy-start.4
  22.1 0.7 %copy-done.4 = f32[16,128]{1,0:T(8,128)S(1)} copy-done((f32[16,128]{1,0:T(8,128)S(1)}, f32[16,128]{1,0:T(8,128)}, u32[]{:S(2)}) %copy-start.4) | copy-done | bytes 8216
  22.8 1.5 %collective-permute-start.7 = (f32[4,96,96]{2,1,0:T(8,128)S(1)}, f32[4,96,96]{2,1,0:T(8,128)S(1)}, u32[]{:S(2)}, u32[]{:S(2)}) collective-permute-start(f32[4,96,96]{2,1,0:T(8,128)S(1)} %shard_map.97), channel_id=1, source_target_pairs={{0,4},{4,0},{8,12},{12,8},{16,20},{20,16},{24,28},{28,24},{1,5},{5... | collective-permute-start | bytes 442376 | tf_op jit(solution)/shard_map/ppermute | solution.py:19
  24.3 5.2 %collective-permute-done.7.rest_3_ = f32[4,96,96]{2,1,0:T(8,128)S(1)} collective-permute-done((f32[4,96,96]{2,1,0:T(8,128)S(1)}, f32[4,96,96]{2,1,0:T(8,128)S(1)}, u32[]{:S(2)}, u32[]{:S(2)}) %collective-permute-start.7) | collective-permute-done | bytes 147488 | tf_op jit(solution)/shard_map/ppermute | solution.py:19
  29.5 0.0 collective-permute-start.11
  29.5 0.5 collective-permute-start.8
  30.0 0.0 collective-permute-start.9
  30.0 0.5 collective-permute-start.10
  30.5 0.0 copy-done.3
  30.5 1.2 %copy-done.5 = bf16[2048,256]{1,0:T(8,128)(2,1)S(1)} copy-done((bf16[2048,256]{1,0:T(8,128)(2,1)S(1)}, bf16[2048,256]{1,0:T(8,128)(2,1)}, u32[]{:S(2)}) %copy-start.5) | copy-done | bytes 1048600
  31.7 1.8 %shard_map.94 = (bf16[288,256]{1,0:T(8,128)(2,1)S(1)}, bf16[288,256]{1,0:T(8,128)(2,1)S(1)}, bf16[288,256]{1,0:T(8,128)(2,1)S(1)}, bf16[288,256]{1,0:T(8,128)(2,1)S(1)}, bf16[288,256]{1,0:T(8,128)(2,1)S(1)}) custom-call(bf16[2048,256]{1,0:T(8,128)(2,1)S(1)} %copy-done.5, f32[1,2048]{1,0:T(1,128)S(1)} %bitcast.14, bf16[24,2048]{1,0:T(8,128)(2,1)S(1)} %bitcast.10, ...), custom_call_target="tpu_custom_call" | custom-call | flops 1342177280 | bytes 1898496 | tf_op jit(solution)/shard_map/pallas_call | solution.py:69
  33.5 0.1 collective-permute-start
  33.6 0.0 collective-permute-done.8.rest_4_
  33.6 1.5 %collective-permute-start.1 = (bf16[288,256]{1,0:T(8,128)(2,1)S(1)}, bf16[288,256]{1,0:T(8,128)(2,1)S(1)}, u32[]{:S(2)}, u32[]{:S(2)}) collective-permute-start(bf16[288,256]{1,0:T(8,128)(2,1)S(1)} %get-tuple-element.30), channel_id=1, source_target_pairs={{0,2},{1,3},{2,0},{3,1},{4,6},{5,7},{6,4},{7,5},{8,10},{9,11},{10,... | collective-permute-start | bytes 442376 | tf_op jit(solution)/shard_map/ppermute | solution.py:19
  35.1 0.0 collective-permute-done.9.rest_5_
  35.1 0.3 collective-permute-start.2
  35.5 0.0 collective-permute-done.10.rest_6_
  35.5 1.5 %collective-permute-start.3 = (bf16[288,256]{1,0:T(8,128)(2,1)S(1)}, bf16[288,256]{1,0:T(8,128)(2,1)S(1)}, u32[]{:S(2)}, u32[]{:S(2)}) collective-permute-start(bf16[288,256]{1,0:T(8,128)(2,1)S(1)} %get-tuple-element.32), channel_id=1, source_target_pairs={{0,4},{4,0},{8,12},{12,8},{16,20},{20,16},{24,28},{28,24},{1,5},{5... | collective-permute-start | bytes 442376 | tf_op jit(solution)/shard_map/ppermute | solution.py:19
  36.9 0.0 collective-permute-done.11.rest_7_
  36.9 0.7 %collective-permute-start.4 = (bf16[288,256]{1,0:T(8,128)(2,1)S(1)}, bf16[288,256]{1,0:T(8,128)(2,1)S(1)}, u32[]{:S(2)}, u32[]{:S(2)}) collective-permute-start(bf16[288,256]{1,0:T(8,128)(2,1)S(1)} %get-tuple-element.33), channel_id=1, source_target_pairs={{4,8},{12,16},{20,24},{8,4},{16,12},{24,20},{5,9},{13,17},{21,25},... | collective-permute-start | bytes 442376 | tf_op jit(solution)/shard_map/ppermute | solution.py:25
  37.6 0.0 all-to-all-done.got_ref
  37.6 0.5 shard_map.93
  38.1 2.7 %shard_map.98 = (f32[64,256]{1,0:T(8,128)S(1)}, f32[64,256]{1,0:T(8,128)S(1)}, f32[64,256]{1,0:T(8,128)S(1)}, f32[64,256]{1,0:T(8,128)S(1)}) custom-call(f32[8,64,128]{2,1,0:T(8,128)S(1)} %get-tuple-element.37.right_ref, f32[32,128]{1,0:T(8,128)S(1)} %get-tuple-element.27.maps_ref, f32[1,96,96]{2,1,0:T(8,128)S(1)} %broadcast_select_fusion.refs_0_.rest_0_, ...), custom_call_target="tpu_custom_call" | custom-call | flops 201326592 | bytes 1130496 | tf_op jit(solution)/shard_map/pallas_call | solution.py:69
  40.8 0.0 collective-permute-done.rest_0_
  40.8 0.2 collective-permute-start.12
  41.0 0.0 collective-permute-done.1.rest_1_
  41.0 1.5 %collective-permute-start.13 = (f32[64,256]{1,0:T(8,128)S(1)}, f32[64,256]{1,0:T(8,128)S(1)}, u32[]{:S(2)}, u32[]{:S(2)}) collective-permute-start(f32[64,256]{1,0:T(8,128)S(1)} %get-tuple-element.41), channel_id=1, source_target_pairs={{0,2},{1,3},{2,0},{3,1},{4,6},{5,7},{6,4},{7,5},{8,10},{9,11},{10,... | collective-permute-start | bytes 196616 | tf_op jit(solution)/shard_map/ppermute | solution.py:19
  42.4 0.0 collective-permute-done.2.rest_2_
  42.5 1.4 %collective-permute-start.14 = (f32[64,256]{1,0:T(8,128)S(1)}, f32[64,256]{1,0:T(8,128)S(1)}, u32[]{:S(2)}, u32[]{:S(2)}) collective-permute-start(f32[64,256]{1,0:T(8,128)S(1)} %get-tuple-element.42), channel_id=1, source_target_pairs={{0,3},{1,2},{2,1},{3,0},{4,7},{5,6},{6,5},{7,4},{8,11},{9,10},{10,... | collective-permute-start | bytes 196616 | tf_op jit(solution)/shard_map/ppermute | solution.py:19
  43.9 0.0 collective-permute-done.3.rest_3_
  43.9 0.0 collective-permute-done.4.rest_4_
  43.9 0.0 copy-start.1
  43.9 4.5 %shard_map.95 = (f32[2048,256]{1,0:T(8,128)S(1)}, bf16[2048,256]{1,0:T(8,128)(2,1)S(1)}, bf16[2048,256]{1,0:T(8,128)(2,1)S(1)}) custom-call(s32[6]{0:T(128)S(1)} %bitcast.18, s32[6,1,256]{2,1,0:T(1,128)S(1)} %bitcast.17, f32[32,128]{1,0:T(8,128)S(1)} %get-tuple-element.27.maps_ref, f32[1,2048]{1,0:T(1,128)S(1)} %bitcast.15, bf16[24,2048]{1,0:T(8,128)(2,1)S(1)} %bitcast.11, ...), custom_call_target="tpu_custom_call" | custom-call | flops 2684354560 | bytes 5060632 | tf_op jit(solution)/shard_map/pallas_call | solution.py:69
  48.5 0.0 collective-permute-done.12.rest_1_
  48.5 0.0 collective-permute-done.13.rest_2_
  48.5 0.0 collective-permute-done.14.rest_3_
  48.5 0.0 copy-done.1
  48.5 2.9 %shard_map.99 = f32[2048,256]{1,0:T(8,128)} custom-call(f32[2048,256]{1,0:T(8,128)S(1)} %copy-done.1, f32[2048,256]{1,0:T(8,128)S(1)} %get-tuple-element.34.early_ref, bf16[2048,256]{1,0:T(8,128)(2,1)S(1)} %get-tuple-element.35.late_ref, bf16[2048,256]{1,0:T(8,128)(2,1)S(1)} %get-tuple-element.36.own_ref, f32[64,256]{1,0:T(8,128)S(1)} %get-tuple-element.39.rest_0_, ...), custom_call_target="tpu_custom_call" | custom-call | flops 805306368 | bytes 8650752 | tf_op jit(solution)/shard_map/pallas_call | solution.py:69
  (10 shorter events, 0.0 us)
Async XLA Ops:
  0.8 11.2 %collective-permute-start.5 = (f32[1,96,96]{2,1,0:T(8,128)S(1)}, f32[1,96,96]{2,1,0:T(8,128)S(1)}, u32[]{:S(2)}, u32[]{:S(2)}) collective-permute-start(f32[1,96,96]{2,1,0:T(8,128)S(1)} %broadcast_select_fusion.refs_0_.rest_0_), channel_id=1, source_target_pairs={{0,16},{4,20},{8,24},{12,28},{16,0},{20,4},{24,8},{28,12},{1,17},{... | collective-permute-start | bytes 110600 | tf_op jit(solution)/shard_map/ppermute | solution.py:19
  8.2 29.4 %all-to-all-start = ((f32[32,16,128]{2,1,0:T(8,128)}), f32[32,16,128]{2,1,0:T(8,128)S(1)}, u32[]{:S(2)}, u32[]{:S(2)}) async-start(f32[32,16,128]{2,1,0:T(8,128)} %get-tuple-element.26), calls=%async_computation | async-start | bytes 524288 | tf_op jit(solution)/shard_map/all_to_all | solution.py:482
  12.0 1.2 %copy-start = (bf16[2048,256]{1,0:T(8,128)(2,1)S(1)}, bf16[2048,256]{1,0:T(8,128)(2,1)}, u32[]{:S(2)}) copy-start(bf16[2048,256]{1,0:T(8,128)(2,1)} %get-tuple-element.24.weighted_any.refs_2_) | copy-start | bytes 3145732
  13.3 8.8 %collective-permute-start.6 = (f32[2,96,96]{2,1,0:T(8,128)S(1)}, f32[2,96,96]{2,1,0:T(8,128)S(1)}, u32[]{:S(2)}, u32[]{:S(2)}) collective-permute-start(f32[2,96,96]{2,1,0:T(8,128)S(1)} %shard_map.96), channel_id=1, source_target_pairs={{0,8},{4,12},{8,0},{12,4},{16,24},{20,28},{24,16},{28,20},{1,9},{5... | collective-permute-start | bytes 221192 | tf_op jit(solution)/shard_map/ppermute | solution.py:19
  15.1 15.4 %copy-start.2 = (bf16[1,1,24,2048]{3,2,1,0:T(8,128)(2,1)S(1)}, bf16[1,1,24,2048]{3,2,1,0:T(8,128)(2,1)}, u32[]{:S(2)}) copy-start(bf16[1,1,24,2048]{3,2,1,0:T(8,128)(2,1)} %param.12) | copy-start | bytes 294916
  15.1 15.4 %copy-start.3 = (f32[1,1,2048]{2,1,0:T(1,128)S(1)}, f32[1,1,2048]{2,1,0:T(1,128)}, u32[]{:S(2)}) copy-start(f32[1,1,2048]{2,1,0:T(1,128)} %param.10) | copy-start | bytes 24580
  15.1 15.4 %copy-start.6 = (s32[1,1,6,256]{3,1,2,0:T(1,128)S(1)}, s32[1,1,6,256]{3,1,2,0:T(1,128)}, u32[]{:S(2)}) copy-start(s32[1,1,6,256]{3,1,2,0:T(1,128)} %param.14) | copy-start | bytes 18436
  22.0 0.7 %copy-start.4 = (f32[16,128]{1,0:T(8,128)S(1)}, f32[16,128]{1,0:T(8,128)}, u32[]{:S(2)}) copy-start(f32[16,128]{1,0:T(8,128)} %get-tuple-element.38.refs_3_) | copy-start | bytes 24580
  22.8 6.7 %collective-permute-start.7 = (f32[4,96,96]{2,1,0:T(8,128)S(1)}, f32[4,96,96]{2,1,0:T(8,128)S(1)}, u32[]{:S(2)}, u32[]{:S(2)}) collective-permute-start(f32[4,96,96]{2,1,0:T(8,128)S(1)} %shard_map.97), channel_id=1, source_target_pairs={{0,4},{4,0},{8,12},{12,8},{16,20},{20,16},{24,28},{28,24},{1,5},{5... | collective-permute-start | bytes 442376 | tf_op jit(solution)/shard_map/ppermute | solution.py:19
  29.5 7.5 %collective-permute-start.11 = (f32[4,96,96]{2,1,0:T(8,128)S(1)}, f32[4,96,96]{2,1,0:T(8,128)S(1)}, u32[]{:S(2)}, u32[]{:S(2)}) collective-permute-start(f32[4,96,96]{2,1,0:T(8,128)S(1)} %collective-permute-done.7.rest_3_), channel_id=1, source_target_pairs={{0,1},{1,0},{2,3},{3,2},{4,5},{5,4},{6,7},{7,6},{8,9},{9,8},{10,11... | collective-permute-start | bytes 442376 | tf_op jit(solution)/shard_map/ppermute | solution.py:19
  29.5 4.1 %collective-permute-start.8 = (f32[1,96,96]{2,1,0:T(8,128)S(1)}, f32[1,96,96]{2,1,0:T(8,128)S(1)}, u32[]{:S(2)}, u32[]{:S(2)}) collective-permute-start(f32[1,96,96]{2,1,0:T(8,128)S(1)} %broadcast_select_fusion.refs_0_.rest_0_), channel_id=1, source_target_pairs={{0,1},{1,0},{2,3},{3,2},{4,5},{5,4},{6,7},{7,6},{8,9},{9,8},{10,11... | collective-permute-start | bytes 110600 | tf_op jit(solution)/shard_map/ppermute | solution.py:19
  30.0 5.2 %collective-permute-start.9 = (f32[1,96,96]{2,1,0:T(8,128)S(1)}, f32[1,96,96]{2,1,0:T(8,128)S(1)}, u32[]{:S(2)}, u32[]{:S(2)}) collective-permute-start(f32[1,96,96]{2,1,0:T(8,128)S(1)} %collective-permute-done.5.refs_1_.rest_1_), channel_id=1, source_target_pairs={{0,1},{1,0},{2,3},{3,2},{4,5},{5,4},{6,7},{7,6},{8,9},{9,8},{10,11... | collective-permute-start | bytes 110600 | tf_op jit(solution)/shard_map/ppermute | solution.py:19
  30.0 5.5 %collective-permute-start.10 = (f32[2,96,96]{2,1,0:T(8,128)S(1)}, f32[2,96,96]{2,1,0:T(8,128)S(1)}, u32[]{:S(2)}, u32[]{:S(2)}) collective-permute-start(f32[2,96,96]{2,1,0:T(8,128)S(1)} %collective-permute-done.6.refs_2_.rest_2_), channel_id=1, source_target_pairs={{0,1},{1,0},{2,3},{3,2},{4,5},{5,4},{6,7},{7,6},{8,9},{9,8},{10,11... | collective-permute-start | bytes 221192 | tf_op jit(solution)/shard_map/ppermute | solution.py:19
  30.5 1.2 %copy-start.5 = (bf16[2048,256]{1,0:T(8,128)(2,1)S(1)}, bf16[2048,256]{1,0:T(8,128)(2,1)}, u32[]{:S(2)}) copy-start(bf16[2048,256]{1,0:T(8,128)(2,1)} %get-tuple-element.28.narrow_ref) | copy-start | bytes 3145732
  31.7 12.2 %copy-start.7 = (s32[1,1,6]{2,1,0:T(1,128)S(1)}, s32[1,1,6]{2,1,0:T(1,128)}, u32[]{:S(2)}) copy-start(s32[1,1,6]{2,1,0:T(1,128)} %param.15) | copy-start | bytes 76
  33.5 7.3 %collective-permute-start = (bf16[288,256]{1,0:T(8,128)(2,1)S(1)}, bf16[288,256]{1,0:T(8,128)(2,1)S(1)}, u32[]{:S(2)}, u32[]{:S(2)}) collective-permute-start(bf16[288,256]{1,0:T(8,128)(2,1)S(1)} %get-tuple-element.29), channel_id=1, source_target_pairs={{0,1},{1,0},{2,3},{3,2},{4,5},{5,4},{6,7},{7,6},{8,9},{9,8},{10,11... | collective-permute-start | bytes 442376 | tf_op jit(solution)/shard_map/ppermute | solution.py:19
  33.6 7.4 %collective-permute-start.1 = (bf16[288,256]{1,0:T(8,128)(2,1)S(1)}, bf16[288,256]{1,0:T(8,128)(2,1)S(1)}, u32[]{:S(2)}, u32[]{:S(2)}) collective-permute-start(bf16[288,256]{1,0:T(8,128)(2,1)S(1)} %get-tuple-element.30), channel_id=1, source_target_pairs={{0,2},{1,3},{2,0},{3,1},{4,6},{5,7},{6,4},{7,5},{8,10},{9,11},{10,... | collective-permute-start | bytes 442376 | tf_op jit(solution)/shard_map/ppermute | solution.py:19
  35.1 7.3 %collective-permute-start.2 = (bf16[288,256]{1,0:T(8,128)(2,1)S(1)}, bf16[288,256]{1,0:T(8,128)(2,1)S(1)}, u32[]{:S(2)}, u32[]{:S(2)}) collective-permute-start(bf16[288,256]{1,0:T(8,128)(2,1)S(1)} %get-tuple-element.31), channel_id=1, source_target_pairs={{0,3},{1,2},{2,1},{3,0},{4,7},{5,6},{6,5},{7,4},{8,11},{9,10},{10,... | collective-permute-start | bytes 442376 | tf_op jit(solution)/shard_map/ppermute | solution.py:19
  35.5 8.4 %collective-permute-start.3 = (bf16[288,256]{1,0:T(8,128)(2,1)S(1)}, bf16[288,256]{1,0:T(8,128)(2,1)S(1)}, u32[]{:S(2)}, u32[]{:S(2)}) collective-permute-start(bf16[288,256]{1,0:T(8,128)(2,1)S(1)} %get-tuple-element.32), channel_id=1, source_target_pairs={{0,4},{4,0},{8,12},{12,8},{16,20},{20,16},{24,28},{28,24},{1,5},{5... | collective-permute-start | bytes 442376 | tf_op jit(solution)/shard_map/ppermute | solution.py:19
  36.9 7.0 %collective-permute-start.4 = (bf16[288,256]{1,0:T(8,128)(2,1)S(1)}, bf16[288,256]{1,0:T(8,128)(2,1)S(1)}, u32[]{:S(2)}, u32[]{:S(2)}) collective-permute-start(bf16[288,256]{1,0:T(8,128)(2,1)S(1)} %get-tuple-element.33), channel_id=1, source_target_pairs={{4,8},{12,16},{20,24},{8,4},{16,12},{24,20},{5,9},{13,17},{21,25},... | collective-permute-start | bytes 442376 | tf_op jit(solution)/shard_map/ppermute | solution.py:25
  40.8 7.7 %collective-permute-start.12 = (f32[64,256]{1,0:T(8,128)S(1)}, f32[64,256]{1,0:T(8,128)S(1)}, u32[]{:S(2)}, u32[]{:S(2)}) collective-permute-start(f32[64,256]{1,0:T(8,128)S(1)} %get-tuple-element.40), channel_id=1, source_target_pairs={{0,1},{1,0},{2,3},{3,2},{4,5},{5,4},{6,7},{7,6},{8,9},{9,8},{10,11... | collective-permute-start | bytes 196616 | tf_op jit(solution)/shard_map/ppermute | solution.py:19
  41.0 7.5 %collective-permute-start.13 = (f32[64,256]{1,0:T(8,128)S(1)}, f32[64,256]{1,0:T(8,128)S(1)}, u32[]{:S(2)}, u32[]{:S(2)}) collective-permute-start(f32[64,256]{1,0:T(8,128)S(1)} %get-tuple-element.41), channel_id=1, source_target_pairs={{0,2},{1,3},{2,0},{3,1},{4,6},{5,7},{6,4},{7,5},{8,10},{9,11},{10,... | collective-permute-start | bytes 196616 | tf_op jit(solution)/shard_map/ppermute | solution.py:19
  42.5 6.0 %collective-permute-start.14 = (f32[64,256]{1,0:T(8,128)S(1)}, f32[64,256]{1,0:T(8,128)S(1)}, u32[]{:S(2)}, u32[]{:S(2)}) collective-permute-start(f32[64,256]{1,0:T(8,128)S(1)} %get-tuple-element.42), channel_id=1, source_target_pairs={{0,3},{1,2},{2,1},{3,0},{4,7},{5,6},{6,5},{7,4},{8,11},{9,10},{10,... | collective-permute-start | bytes 196616 | tf_op jit(solution)/shard_map/ppermute | solution.py:19
  43.9 4.6 %copy-start.1 = (f32[2048,256]{1,0:T(8,128)S(1)}, f32[2048,256]{1,0:T(8,128)}, u32[]{:S(2)}) copy-start(f32[2048,256]{1,0:T(8,128)} %get-tuple-element.25.part_ref) | copy-start | bytes 6291460

commit v3 on v2

--- a/solution.py
+++ b/solution.py
@@ -62,9 +62,10 @@
 
 def call(kernel, outs, in_specs, args, grid=(1,), out_specs=None, scratch=(), flops=0, limit=24):
     many = isinstance(outs, (list, tuple))
+    resident = pl.BlockSpec(memory_space=pltpu.VMEM)
     if out_specs is None:
-        out_specs = [fixed(o.shape) for o in outs] if many else fixed(outs.shape)
-    in_specs = [fixed(a.shape) if s is None else s for s, a in zip(in_specs, args)]
+        out_specs = [resident] * len(outs) if many else resident
+    in_specs = [resident if s is None else s for s in in_specs]
     sizes = [a.size * a.dtype.itemsize for a in list(args) + (list(outs) if many else [outs])]
     return pl.pallas_call(
         kernel,
@@ -80,16 +81,15 @@
 
 def join_kernel(*refs):
     start = 0
-    for ref in refs[:-2]:
+    for ref in refs[:-1]:
         refs[-1][start : start + ref.shape[0]] = ref[...]
         start += ref.shape[0]
 
 
-def join(parts, after):
+def join(parts):
     total = sum(p.shape[0] for p in parts)
     out = jax.ShapeDtypeStruct((total,) + parts[0].shape[1:], parts[0].dtype)
-    corner = pl.BlockSpec((16, LANES), lambda i: (0, 0))
-    return call(join_kernel, out, [None] * len(parts) + [corner], (*parts, after))
+    return call(join_kernel, out, [None] * len(parts), parts)
 
 
 def copies(sources, targets, sems):
@@ -99,29 +99,28 @@
     return moves
 
 
-def front_kernel(slabs, groups, res_any, scale_any, basis_any, map_any, weighted_any, sent_ref, res_ref, scale_ref, basis_ref, map_ref, weighted_ref, in_sems, out_sems):
+def weigh(scale_turned, res_ref, start, count):
+    for j in range(count // LANES):
+        row = start + j * LANES
+        factor = scale_turned[:, row // LANES : row // LANES + 1]
+        yield (factor * res_ref[row : row + LANES, :].astype(f32)).astype(bf16)
+
+
+def front_kernel(slabs, groups, res_any, scale_any, basis_any, map_any, sent_ref, res_ref, scale_ref, basis_ref, map_ref, sems):
     rows = res_ref.shape[0]
-    chunk = min(rows, 512)
+    chunk = rows // 2
     parts = [pl.ds(i * chunk, chunk) for i in range(rows // chunk)]
     sources = [scale_any, basis_any, map_any] + [res_any.at[p] for p in parts]
     targets = [scale_ref, basis_ref, map_ref] + [res_ref.at[p] for p in parts]
-    moves = copies(sources, targets, in_sems)
+    moves = copies(sources, targets, sems)
     for move in moves[:3]:
         move.wait()
     scale_turned = turned_scale(scale_ref)
-    primal, leaving = None, []
-    for i, p in enumerate(parts):
+    weighted = []
+    for i in range(rows // chunk):
         moves[3 + i].wait()
-        for j in range(chunk // LANES):
-            here = slice(i * chunk + j * LANES, i * chunk + (j + 1) * LANES)
-            column = i * (chunk // LANES) + j
-            factor = scale_turned[:, column : column + 1]
-            weighted_ref[here, :] = (factor * res_ref[here, :].astype(f32)).astype(bf16)
-        leave = pltpu.make_async_copy(weighted_ref.at[p], weighted_any.at[p], out_sems.at[i])
-        leave.start()
-        leaving.append(leave)
-        term = dot(basis_ref[:, i * chunk : (i + 1) * chunk], weighted_ref[i * chunk : (i + 1) * chunk, :])
-        primal = term if primal is None else primal + term
+        weighted += list(weigh(scale_turned, res_ref, i * chunk, chunk))
+    primal = dot(basis_ref[...], jnp.concatenate(weighted, axis=0))
     constraints, columns = primal.shape
     turned = jnp.concatenate([primal, jnp.zeros((LANES - constraints, columns), f32)], axis=0).T
     quarter = sent_ref.shape[1]
@@ -143,15 +142,6 @@
             piece = piece + (pltpu.roll(part, GROUP * g, 1) if g else part)
         for v in range(slabs):
             sent_ref[v * groups + m] = piece
-    for leave in leaving:
-        leave.wait()
-
-
-def scale_columns(turned_ref, step, block):
-    lanes = iota((LANES, LANES), 1)
-    for j in range(block // LANES):
-        hit = jnp.where(lanes == step * (block // LANES) + j, turned_ref[...], 0.0)
-        yield jnp.sum(hit, axis=1, keepdims=True)
 
 
 def place_of():
@@ -164,59 +154,68 @@
     return [n ^ k for k in range(1, groups)] + [groups + 1 - parity, groups + parity]
 
 
-def local_kernel(inverse_any, weighted_any, scale_any, part_ref, narrow_ref, mark_ref, inverse_ref, weighted_ref, scale_ref, turned_ref, sems):
+def local_kernel(groups, inverse_any, res_any, scale_any, lane_scale_any, basis_any, index_any, part_any, *rest):
+    slots = groups + 1
+    outs_any, outs = rest[:slots], rest[slots : 2 * slots]
+    lane_scale_ref, basis_ref, index_ref, inverse_ref, res_ref, scale_ref, weighted_ref, narrow_ref, part_ref, scaled_ref, sems, out_sems = rest[2 * slots :]
     rows = inverse_ref.shape[0]
-    block = min(rows, 256)
-    steps = rows // block
-    sources, targets = [scale_any, weighted_any], [scale_ref, weighted_ref]
-    for i in range(steps):
-        p = pl.ds(i * block, block)
-        sources.append(inverse_any.at[p])
-        targets.append(inverse_ref.at[p])
+    half = rows // 2
+    halves = [pl.ds(i * half, half) for i in range(2)]
+    sources = [lane_scale_any, basis_any, index_any, scale_any, res_any]
+    targets = [lane_scale_ref, basis_ref, index_ref, scale_ref, res_ref]
+    sources += [inverse_any.at[p] for p in halves]
+    targets += [inverse_ref.at[p] for p in halves]
     moves = copies(sources, targets, sems)
-    for move in moves[:2]:
+    for move in moves[:3]:
         move.wait()
-    turned_ref[...] = turned_scale(scale_ref)
-    mark_ref[...] = jnp.zeros_like(mark_ref)
-
-    def one(i, carry):
-        p = pl.ds(pl.multiple_of(i * block, block), block)
-        pltpu.make_async_copy(inverse_any.at[p], inverse_ref.at[p], sems.at[2 + i]).wait()
-        part = dot(inverse_ref[p, :], weighted_ref[...])
-        factors = scale_columns(turned_ref, i, block)
-        scaled = jnp.concatenate(list(factors), axis=0) * part
-        part_ref[p, :] = scaled
-        narrow_ref[p, :] = scaled.astype(bf16)
-        return carry
-
-    lax.fori_loop(0, steps, one, 0)
-
-
-def pick_kernel(groups, narrow_ref, lane_scale_ref, basis_ref, index_ref, *rest):
-    slots = groups + 1
-    outs, basis = rest[:slots], rest[slots]
     capacity = index_ref.shape[2]
-    constraints, total = basis_ref.shape
+    constraints = basis_ref.shape[0]
     picks = [index_ref[r] for r in slot_rows(groups)]
-    rows = picks + [jnp.zeros((LANES - slots, capacity), jnp.int32)]
-    columns_of = jnp.concatenate(rows, axis=0).astype(f32).T
-    basis[...] = lane_scale_ref[...] * basis_ref[...].astype(f32)
-    lanes = iota((capacity, LANES), 1).astype(f32)
+    scaled_ref[...] = lane_scale_ref[...] * basis_ref[...].astype(f32)
     for k in range(slots):
-        spot = jnp.broadcast_to(columns_of[:, k : k + 1], (capacity, LANES))
-        hots = [(spot == lanes + float(j * LANES)).astype(f32).astype(bf16) for j in range(total // LANES)]
-        outs[k][:capacity, :] = dot(jnp.concatenate(hots, axis=1), narrow_ref[...]).astype(bf16)
         parts = []
         for c in range(capacity // LANES):
             spot = jnp.broadcast_to(picks[k][:, c * LANES : (c + 1) * LANES], (constraints, LANES))
             inner, outer = spot & (LANES - 1), spot // LANES
             value = jnp.zeros((constraints, LANES), f32)
-            for j in range(total // LANES):
-                found = jnp.take_along_axis(basis[:, j * LANES : (j + 1) * LANES], inner, axis=1)
+            for j in range(rows // LANES):
+                found = jnp.take_along_axis(scaled_ref[:, j * LANES : (j + 1) * LANES], inner, axis=1)
                 value = jnp.where(outer == j, found, value)
             parts.append(value)
         fill = jnp.zeros((GROUP - constraints, capacity), f32)
         outs[k][capacity:, :] = jnp.concatenate([jnp.concatenate(parts, axis=1), fill], axis=0).astype(bf16)
+    for move in moves[3:5]:
+        move.wait()
+    turned = turned_scale(scale_ref)
+    for j, value in enumerate(weigh(turned, res_ref, 0, rows)):
+        weighted_ref[j * LANES : (j + 1) * LANES, :] = value
+    leaving = []
+    for i, p in enumerate(halves):
+        moves[5 + i].wait()
+        block = min(half, 256)
+        for start in range(i * half, (i + 1) * half, block):
+            part = dot(inverse_ref[start : start + block, :], weighted_ref[...])
+            for j in range(block // LANES):
+                row = start + j * LANES
+                column = row // LANES
+                scaled = turned[:, column : column + 1] * part[j * LANES : (j + 1) * LANES, :]
+                part_ref[row : row + LANES, :] = scaled
+                narrow_ref[row : row + LANES, :] = scaled.astype(bf16)
+        leave = pltpu.make_async_copy(part_ref.at[p], part_any.at[p], out_sems.at[i])
+        leave.start()
+        leaving.append(leave)
+    spare_rows = [jnp.zeros((LANES - slots, capacity), jnp.int32)]
+    columns_of = jnp.concatenate(picks + spare_rows, axis=0).astype(f32).T
+    lanes = iota((capacity, LANES), 1).astype(f32)
+    for k in range(slots):
+        spot = jnp.broadcast_to(columns_of[:, k : k + 1], (capacity, LANES))
+        hots = [(spot == lanes + float(j * LANES)).astype(f32).astype(bf16) for j in range(rows // LANES)]
+        outs[k][:capacity, :] = dot(jnp.concatenate(hots, axis=1), narrow_ref[...]).astype(bf16)
+        leave = pltpu.make_async_copy(outs[k], outs_any[k], out_sems.at[2 + k])
+        leave.start()
+        leaving.append(leave)
+    for leave in leaving:
+        leave.wait()
 
 
 def unpack_kernel(slabs, groups, constraints, got_ref, right_ref, maps_ref):
@@ -269,22 +268,20 @@
 
 def solve_kernel(slabs, groups, constraints, offsets, right_ref, maps_ref, *rest):
     count = len(offsets).bit_length()
-    mine, other = rest[:count], rest[count : 2 * count]
-    shares = rest[2 * count : 2 * count + groups]
-    raw, forward, backward, pivots, solved = rest[2 * count + groups :]
+    held, shares = rest[:count], rest[count : count + groups]
+    raw, forward, backward, pivots, solved = rest[count + groups :]
     w, n = place_of()
-    core = n & 1
-    size = mine[0].shape[1]
+    size = held[0].shape[2]
     order = raw.shape[2]
     if size != order:
         raw[...] = jnp.zeros_like(raw)
     start = 0
-    for a, b in zip(mine, other):
-        for i in range(a.shape[0]):
+    for ref in held:
+        for i in range(ref.shape[0]):
             slab = w ^ offsets[start + i]
-            raw[core, slab, :size, :size] = a[i]
-            raw[1 - core, slab, :size, :size] = b[i]
-        start += a.shape[0]
+            for j in range(2):
+                raw[j, slab, :size, :size] = ref[i, j]
+        start += ref.shape[0]
     c = right_ref.shape[1]
     few = slabs <= 8
 
@@ -363,7 +360,8 @@
     def _():
         for k, r in enumerate(slot_rows(groups)):
             spot = index_ref[r]
-            live = iota((1, capacity), 1) < length_ref[r]
+            count = jnp.where(iota(length_ref.shape, 1) == r, length_ref[...], 0)
+            live = iota((1, capacity), 1) < jnp.sum(count, axis=1, keepdims=True)
             targets[:, k * capacity : (k + 1) * capacity] = jnp.where(live, spot, -1)
             here = slice(k * capacity, (k + 1) * capacity)
             joined[here, :columns] = arrived[k][:capacity, :]
@@ -433,12 +431,11 @@
     coarse_pivot,
 ):
     slabs, groups = lax.axis_size("wide"), lax.axis_size("narrow")
-    n = lax.axis_index("narrow")
     residual, inverse = residual[0, 0], local_inverse[0, 0]
     basis = coarse_basis[0, 0]
     slots, capacity = slot_index.shape[2] - 1, slot_index.shape[3]
     index = slot_index.reshape(slots + 1, 1, capacity)
-    length = slot_length[0, 0]
+    length = slot_length[0]
     size = coarse_sub.shape[1]
     order = ceil_lanes(size)
     rows, columns = residual.shape
@@ -448,7 +445,6 @@
     width = ceil_lanes(size + 5 * constraints)
     scale = scaling[0, 0].reshape(rows // LANES, LANES)
     lane_scale = scaling[0]
-    smem = pl.BlockSpec(memory_space=pltpu.SMEM)
     struct = jax.ShapeDtypeStruct
 
     def by_rows(block, cols):
@@ -459,63 +455,57 @@
 
     any_space = pl.BlockSpec(memory_space=pl.ANY)
     vmem = pl.BlockSpec(memory_space=pltpu.VMEM)
-    factor = jnp.where((n & 1) == 0, coarse_sub, coarse_pivot)
-    chunks = -(-rows // 512)
-    weighted, sent = call(
+    factors = [jnp.stack([coarse_sub, coarse_pivot], axis=1)]
+    held, offsets, mask = factors[0], [0], slabs // 2
+    while mask:
+        factors.append(swap(held, "wide", mask))
+        offsets = offsets + [o ^ mask for o in offsets]
+        mask //= 2
+        if mask:
+            held = join(factors)
+
+    sent = call(
         functools.partial(front_kernel, slabs, groups),
-        [struct((rows, columns), bf16), struct((slabs * groups, quarter, LANES), f32)],
+        struct((slabs * groups, quarter, LANES), f32),
         [any_space] * 4,
         (residual, scale, basis, primal_map[0]),
-        out_specs=[any_space, fixed((slabs * groups, quarter, LANES))],
+        out_specs=fixed((slabs * groups, quarter, LANES)),
         scratch=[
             pltpu.VMEM((rows, columns), bf16),
             pltpu.VMEM(scale.shape, f32),
             pltpu.VMEM(basis.shape, bf16),
             pltpu.VMEM(primal_map[0].shape, jnp.int32),
-            pltpu.VMEM((rows, columns), bf16),
-            pltpu.SemaphoreType.DMA((3 + chunks,)),
-            pltpu.SemaphoreType.DMA((chunks,)),
+            pltpu.SemaphoreType.DMA((5,)),
         ],
         flops=2 * constraints * rows * columns,
-        limit=62,
+        limit=63,
     )
     got = lax.all_to_all(sent, ("wide", "narrow"), split_axis=0, concat_axis=0, tiled=True)
 
-    part, narrow, mark = call(
-        local_kernel,
-        [struct((rows, columns), f32), struct((rows, columns), bf16), struct((16, LANES), f32)],
-        [any_space] * 3,
-        (inverse, weighted, scale),
-        out_specs=[vmem] * 3,
-        scratch=[
+    part, *outgoing = call(
+        functools.partial(local_kernel, groups),
+        [struct((rows, columns), f32)] + [struct((capacity + GROUP, columns), bf16)] * slots,
+        [any_space] * 6,
+        (inverse, residual, scale, lane_scale, basis, index),
+        out_specs=[any_space] * (1 + slots),
+        scratch=[pltpu.VMEM((capacity + GROUP, columns), bf16)] * slots
+        + [
+            pltpu.VMEM(lane_scale.shape, f32),
+            pltpu.VMEM(basis.shape, bf16),
+            pltpu.VMEM(index.shape, jnp.int32),
             pltpu.VMEM((rows, rows), bf16),
             pltpu.VMEM((rows, columns), bf16),
             pltpu.VMEM(scale.shape, f32),
-            pltpu.VMEM((LANES, LANES), f32),
-            pltpu.SemaphoreType.DMA((2 + rows // min(rows, 256),)),
+            pltpu.VMEM((rows, columns), bf16),
+            pltpu.VMEM((rows, columns), bf16),
+            pltpu.VMEM((rows, columns), f32),
+            pltpu.VMEM((constraints, rows), f32),
+            pltpu.SemaphoreType.DMA((7,)),
+            pltpu.SemaphoreType.DMA((2 + slots,)),
         ],
-        flops=2 * rows * columns * rows,
+        flops=2 * rows * columns * (rows + slots * capacity),
         limit=57,
     )
-    outgoing = call(
-        functools.partial(pick_kernel, groups),
-        [struct((capacity + GROUP, columns), bf16)] * slots,
-        [vmem] + [None] * 3,
-        (narrow, lane_scale, basis, index),
-        scratch=[pltpu.VMEM((constraints, rows), f32)],
-        flops=2 * rows * columns * slots * capacity,
-    )
-    waits = [weighted] + [mark] * slabs
-    mine, held, offsets, mask = [factor], factor, [0], slabs // 2
-    while mask:
-        mine.append(swap(held, "wide", mask))
-        offsets = offsets + [o ^ mask for o in offsets]
-        mask //= 2
-        if mask:
-            held = join(mine, waits[len(mine) - 2])
-    other = []
-    for piece in mine:
-        other.append(swap(piece, "narrow", 1))
     arrived = []
     for k in range(slots):
         if k < groups - 1:
@@ -535,8 +525,8 @@
     shares = call(
         functools.partial(solve_kernel, slabs, groups, constraints, offsets),
         [struct((own_columns, width), f32)] * groups,
-        [None] * (2 + len(mine) + len(other)),
-        (right, maps, *mine, *other),
+        [None] * (2 + len(factors)),
+        (right, maps, *factors),
         scratch=[
             pltpu.VMEM((2, slabs, order, order), f32),
             pltpu.VMEM((slabs, order, 2 * order), bf16),
@@ -549,11 +539,11 @@
     )
     pieces = [shares[0]] + [swap(shares[k], "narrow", k) for k in range(1, groups)]
 
-    block = min(rows, 512)
+    block = min(rows, 1024)
     early, late, own = call(
         functools.partial(scatter_kernel, groups, size),
         [struct((rows, columns), f32), struct((rows, width), bf16), struct((rows, width), bf16)],
-        [smem, None, None, by_lanes(1, block), by_lanes(constraints, block)] + [None] * slots,
+        [None, None, None, by_lanes(1, block), by_lanes(constraints, block)] + [None] * slots,
         (length, index, maps, lane_scale, basis, *arrived),
         grid=(rows // block,),
         out_specs=[vmem] * 3,

time: 52.3 us -> 47 us (0.90)
  the two profiles are of different devices: /device:TPU:0 before, /device:TPU:5 now
where the time goes in v3:
time: 47 us; the launch traced here: 46.8 us
  starting transfers between devices  22.8 us (49%)
  Pallas kernels  19.7 us (42%)
  waiting for transfers between devices  3.2 us (7%)
  other arithmetic  0.83 us (2%)
    pallas_call x8, Pallas kernels, call(): pl.pallas_call(kernel, out_shape=outs, grid=grid, in_specs=in_specs, out_...  19.7 us
    ppermute x10, starting transfers between devices, swap(): return lax.ppermute(block, axis, [(i, i ^ mask) for i in range(count)])  13.2 us
    all_to_all x1, starting transfers between devices, body(): lax.all_to_all(sent, ('wide', 'narrow'), split_axis=0, concat_axis=0, til...  6.26 us
    ppermute x1, starting transfers between devices, swap_odd(): return lax.ppermute(block, axis, pairs + [(b, a) for a, b in pairs])  3.32 us
    ppermute x10, waiting for transfers between devices, swap(): return lax.ppermute(block, axis, [(i, i ^ mask) for i in range(count)])  3.19 us
  transfers between devices with their start and end apart: 12, of which 2 were waited for; matrix products, arithmetic and copies ran while one was open for 0% of the time, Pallas kernels for 37%

profile of v3, /device:TPU:5, one launch (start us, length us, event | category | flops | bytes accessed | tf_op | source)
XLA Modules:
  0.0 46.8 jit_solution(3184154799166879564)
XLA Ops:
  0.0 0.8 %pad_maximum_fusion.refs_0_.rest_0_ = f32[1,2,96,96]{3,2,1,0:T(8,128)S(1)} fusion(f32[1,1,96,96]{3,2,1,0:T(8,128)} %bitcast.23, f32[1,1,96,96]{3,2,1,0:T(8,128)} %bitcast.24), kind=kLoop, calls=%fused_computation | loop fusion | flops 18432 | bytes 147456 | tf_op jit(solution)/shard_map/stack | solution.py:458
  0.8 2.4 %collective-permute-start.5 = (f32[1,2,96,96]{3,2,1,0:T(8,128)S(1)}, f32[1,2,96,96]{3,2,1,0:T(8,128)S(1)}, u32[]{:S(2)}, u32[]{:S(2)}) collective-permute-start(f32[1,2,96,96]{3,2,1,0:T(8,128)S(1)} %pad_maximum_fusion.refs_0_.rest_0_), channel_id=1, source_target_pairs={{0,16},{4,20},{8,24},{12,28},{16,0},{20,4},{24,8},{28,12},{1,17},{... | collective-permute-start | bytes 221192 | tf_op jit(solution)/shard_map/ppermute | solution.py:19
  3.2 2.1 %collective-permute-done.5.refs_1_.rest_1_ = f32[1,2,96,96]{3,2,1,0:T(8,128)S(1)} collective-permute-done((f32[1,2,96,96]{3,2,1,0:T(8,128)S(1)}, f32[1,2,96,96]{3,2,1,0:T(8,128)S(1)}, u32[]{:S(2)}, u32[]{:S(2)}) %collective-permute-start.5) | collective-permute-done | bytes 73760 | tf_op jit(solution)/shard_map/ppermute | solution.py:19
  5.3 3.8 %collective-permute-start.6 = (f32[2,2,96,96]{3,2,1,0:T(8,128)S(1)}, f32[2,2,96,96]{3,2,1,0:T(8,128)S(1)}, u32[]{:S(2)}, u32[]{:S(2)}) collective-permute-start(f32[2,2,96,96]{3,2,1,0:T(8,128)S(1)} %shard_map.95), channel_id=1, source_target_pairs={{0,8},{4,12},{8,0},{12,4},{16,24},{20,28},{24,16},{28,20},{1,9},{5... | collective-permute-start | bytes 442376 | tf_op jit(solution)/shard_map/ppermute | solution.py:19
  9.1 2.6 %shard_map.92 = f32[32,16,128]{2,1,0:T(8,128)} custom-call(bf16[2048,256]{1,0:T(8,128)(2,1)} %bitcast.21, f32[16,128]{1,0:T(8,128)} %bitcast.14, bf16[24,2048]{1,0:T(8,128)(2,1)} %bitcast.11, s32[1,24]{1,0:T(1,128)} %bitcast.25), custom_call_target="tpu_custom_call" | custom-call | flops 25165824 | bytes 1417312 | tf_op jit(solution)/shard_map/pallas_call | solution.py:70
  11.7 6.3 %all-to-all-start = ((f32[32,16,128]{2,1,0:T(8,128)}), f32[32,16,128]{2,1,0:T(8,128)S(1)}, u32[]{:S(2)}, u32[]{:S(2)}) async-start(f32[32,16,128]{2,1,0:T(8,128)} %shard_map.92), calls=%async_computation | async-start | bytes 524288 | tf_op jit(solution)/shard_map/all_to_all | solution.py:483
  18.0 0.0 collective-permute-done.6.refs_2_.rest_2_
  18.0 0.2 collective-permute-start.7
  18.2 0.0 copy-start.1
  18.2 0.0 copy-start.2
  18.2 0.0 copy-start.3
  18.2 0.0 copy-start.4
  18.2 7.9 %shard_map.91 = (f32[2048,256]{1,0:T(8,128)}, bf16[288,256]{1,0:T(8,128)(2,1)}, bf16[288,256]{1,0:T(8,128)(2,1)}, bf16[288,256]{1,0:T(8,128)(2,1)}, bf16[288,256]{1,0:T(8,128)(2,1)}, /*index=5*/bf16[288,256]{1,0:T(8,128)(2,1)}) custom-call(bf16[2048,2048]{1,0:T(8,128)(2,1)} %bitcast.26, bf16[2048,256]{1,0:T(8,128)(2,1)} %bitcast.22, f32[16,128]{1,0:T(8,128)} %bitcast.15, ...), custom_call_target="tpu_custom_call" | custom-call | flops 3489660928 | bytes 12392448 | tf_op jit(solution)/shard_map/pallas_call | solution.py:70
  26.1 0.6 %collective-permute-start = (bf16[288,256]{1,0:T(8,128)(2,1)}, bf16[288,256]{1,0:T(8,128)(2,1)S(1)}, u32[]{:S(2)}, u32[]{:S(2)}) collective-permute-start(bf16[288,256]{1,0:T(8,128)(2,1)} %get-tuple-element.22), channel_id=1, source_target_pairs={{0,1},{1,0},{2,3},{3,2},{4,5},{5,4},{6,7},{7,6},{8,9},{9,8},{10,11... | collective-permute-start | bytes 442376 | tf_op jit(solution)/shard_map/ppermute | solution.py:19
  26.7 1.5 %collective-permute-start.1 = (bf16[288,256]{1,0:T(8,128)(2,1)}, bf16[288,256]{1,0:T(8,128)(2,1)S(1)}, u32[]{:S(2)}, u32[]{:S(2)}) collective-permute-start(bf16[288,256]{1,0:T(8,128)(2,1)} %get-tuple-element.23), channel_id=1, source_target_pairs={{0,2},{1,3},{2,0},{3,1},{4,6},{5,7},{6,4},{7,5},{8,10},{9,11},{10,... | collective-permute-start | bytes 442376 | tf_op jit(solution)/shard_map/ppermute | solution.py:19
  28.2 0.2 collective-permute-start.2
  28.4 1.5 %collective-permute-start.3 = (bf16[288,256]{1,0:T(8,128)(2,1)}, bf16[288,256]{1,0:T(8,128)(2,1)S(1)}, u32[]{:S(2)}, u32[]{:S(2)}) collective-permute-start(bf16[288,256]{1,0:T(8,128)(2,1)} %get-tuple-element.25), channel_id=1, source_target_pairs={{0,4},{4,0},{8,12},{12,8},{16,20},{20,16},{24,28},{28,24},{1,5},{5... | collective-permute-start | bytes 442376 | tf_op jit(solution)/shard_map/ppermute | solution.py:19
  29.9 1.1 %collective-permute-done.7.rest_3_ = f32[4,2,96,96]{3,2,1,0:T(8,128)S(1)} collective-permute-done((f32[4,2,96,96]{3,2,1,0:T(8,128)S(1)}, f32[4,2,96,96]{3,2,1,0:T(8,128)S(1)}, u32[]{:S(2)}, u32[]{:S(2)}) %collective-permute-start.7) | collective-permute-done | bytes 294944 | tf_op jit(solution)/shard_map/ppermute | solution.py:19
  31.0 3.3 %collective-permute-start.4 = (bf16[288,256]{1,0:T(8,128)(2,1)}, bf16[288,256]{1,0:T(8,128)(2,1)S(1)}, u32[]{:S(2)}, u32[]{:S(2)}) collective-permute-start(bf16[288,256]{1,0:T(8,128)(2,1)} %get-tuple-element.26), channel_id=1, source_target_pairs={{4,8},{12,16},{20,24},{8,4},{16,12},{24,20},{5,9},{13,17},{21,25},... | collective-permute-start | bytes 442376 | tf_op jit(solution)/shard_map/ppermute | solution.py:25
  34.4 0.0 all-to-all-done.got_ref
  34.4 0.5 %shard_map.93 = (f32[8,64,128]{2,1,0:T(8,128)S(1)}, f32[32,128]{1,0:T(8,128)S(1)}) custom-call(f32[32,16,128]{2,1,0:T(8,128)S(1)} %all-to-all-done.got_ref), custom_call_target="tpu_custom_call" | custom-call | flops 50331648 | bytes 540672 | tf_op jit(solution)/shard_map/pallas_call | solution.py:70
  34.9 2.7 %shard_map.97 = (f32[64,256]{1,0:T(8,128)S(1)}, f32[64,256]{1,0:T(8,128)S(1)}, f32[64,256]{1,0:T(8,128)S(1)}, f32[64,256]{1,0:T(8,128)S(1)}) custom-call(f32[8,64,128]{2,1,0:T(8,128)S(1)} %get-tuple-element.30.right_ref, f32[32,128]{1,0:T(8,128)S(1)} %get-tuple-element.21.maps_ref, f32[1,2,96,96]{3,2,1,0:T(8,128)S(1)} %pad_maximum_fusion.refs_0_.rest_0_, ...), custom_call_target="tpu_custom_call" | custom-call | flops 201326592 | bytes 1130496 | tf_op jit(solution)/shard_map/pallas_call | solution.py:70
  37.6 0.0 collective-permute-done.rest_0_
  37.6 1.3 %collective-permute-start.8 = (f32[64,256]{1,0:T(8,128)S(1)}, f32[64,256]{1,0:T(8,128)S(1)}, u32[]{:S(2)}, u32[]{:S(2)}) collective-permute-start(f32[64,256]{1,0:T(8,128)S(1)} %get-tuple-element.32), channel_id=1, source_target_pairs={{0,1},{1,0},{2,3},{3,2},{4,5},{5,4},{6,7},{7,6},{8,9},{9,8},{10,11... | collective-permute-start | bytes 196616 | tf_op jit(solution)/shard_map/ppermute | solution.py:19
  38.9 0.0 collective-permute-done.1.rest_1_
  38.9 1.1 %collective-permute-start.9 = (f32[64,256]{1,0:T(8,128)S(1)}, f32[64,256]{1,0:T(8,128)S(1)}, u32[]{:S(2)}, u32[]{:S(2)}) collective-permute-start(f32[64,256]{1,0:T(8,128)S(1)} %get-tuple-element.33), channel_id=1, source_target_pairs={{0,2},{1,3},{2,0},{3,1},{4,6},{5,7},{6,4},{7,5},{8,10},{9,11},{10,... | collective-permute-start | bytes 196616 | tf_op jit(solution)/shard_map/ppermute | solution.py:19
  40.0 0.0 collective-permute-done.2.rest_2_
  40.0 0.7 %collective-permute-start.10 = (f32[64,256]{1,0:T(8,128)S(1)}, f32[64,256]{1,0:T(8,128)S(1)}, u32[]{:S(2)}, u32[]{:S(2)}) collective-permute-start(f32[64,256]{1,0:T(8,128)S(1)} %get-tuple-element.34), channel_id=1, source_target_pairs={{0,3},{1,2},{2,1},{3,0},{4,7},{5,6},{6,5},{7,4},{8,11},{9,10},{10,... | collective-permute-start | bytes 196616 | tf_op jit(solution)/shard_map/ppermute | solution.py:19
  40.6 0.0 collective-permute-done.3.rest_3_
  40.6 0.0 collective-permute-done.4.rest_4_
  40.6 0.0 copy-done.1
  40.6 0.0 copy-done.2
  40.6 0.0 copy-done.3
  40.7 0.0 copy-done.4
  40.7 0.0 copy-start
  40.7 3.6 %shard_map.94 = (f32[2048,256]{1,0:T(8,128)S(1)}, bf16[2048,256]{1,0:T(8,128)(2,1)S(1)}, bf16[2048,256]{1,0:T(8,128)(2,1)S(1)}) custom-call(s32[1,6]{1,0:T(1,128)S(1)} %bitcast.20, s32[6,1,256]{2,1,0:T(1,128)S(1)} %bitcast.19, f32[32,128]{1,0:T(8,128)S(1)} %get-tuple-element.21.maps_ref, f32[1,2048]{1,0:T(1,128)S(1)} %bitcast.17, ...), custom_call_target="tpu_custom_call" | custom-call | flops 2684354560 | bytes 5060632 | tf_op jit(solution)/shard_map/pallas_call | solution.py:70
  44.3 0.0 collective-permute-done.8.rest_1_
  44.3 0.0 collective-permute-done.9.rest_2_
  44.3 0.0 collective-permute-done.10.rest_3_
  44.3 0.0 copy-done
  44.3 2.5 %shard_map.98 = f32[2048,256]{1,0:T(8,128)} custom-call(f32[2048,256]{1,0:T(8,128)S(1)} %copy-done, f32[2048,256]{1,0:T(8,128)S(1)} %get-tuple-element.27.early_ref, bf16[2048,256]{1,0:T(8,128)(2,1)S(1)} %get-tuple-element.28.late_ref, bf16[2048,256]{1,0:T(8,128)(2,1)S(1)} %get-tuple-element.29.own_ref, f32[64,256]{1,0:T(8,128)S(1)} %get-tuple-element.31.rest_0_, ...), custom_call_target="tpu_custom_call" | custom-call | flops 805306368 | bytes 8650752 | tf_op jit(solution)/shard_map/pallas_call | solution.py:70
  (2 shorter events, 0.0 us)
Async XLA Ops:
  0.8 4.4 %collective-permute-start.5 = (f32[1,2,96,96]{3,2,1,0:T(8,128)S(1)}, f32[1,2,96,96]{3,2,1,0:T(8,128)S(1)}, u32[]{:S(2)}, u32[]{:S(2)}) collective-permute-start(f32[1,2,96,96]{3,2,1,0:T(8,128)S(1)} %pad_maximum_fusion.refs_0_.rest_0_), channel_id=1, source_target_pairs={{0,16},{4,20},{8,24},{12,28},{16,0},{20,4},{24,8},{28,12},{1,17},{... | collective-permute-start | bytes 221192 | tf_op jit(solution)/shard_map/ppermute | solution.py:19
  5.3 12.7 %collective-permute-start.6 = (f32[2,2,96,96]{3,2,1,0:T(8,128)S(1)}, f32[2,2,96,96]{3,2,1,0:T(8,128)S(1)}, u32[]{:S(2)}, u32[]{:S(2)}) collective-permute-start(f32[2,2,96,96]{3,2,1,0:T(8,128)S(1)} %shard_map.95), channel_id=1, source_target_pairs={{0,8},{4,12},{8,0},{12,4},{16,24},{20,28},{24,16},{28,20},{1,9},{5... | collective-permute-start | bytes 442376 | tf_op jit(solution)/shard_map/ppermute | solution.py:19
  11.7 22.7 %all-to-all-start = ((f32[32,16,128]{2,1,0:T(8,128)}), f32[32,16,128]{2,1,0:T(8,128)S(1)}, u32[]{:S(2)}, u32[]{:S(2)}) async-start(f32[32,16,128]{2,1,0:T(8,128)} %shard_map.92), calls=%async_computation | async-start | bytes 524288 | tf_op jit(solution)/shard_map/all_to_all | solution.py:483
  18.0 13.0 %collective-permute-start.7 = (f32[4,2,96,96]{3,2,1,0:T(8,128)S(1)}, f32[4,2,96,96]{3,2,1,0:T(8,128)S(1)}, u32[]{:S(2)}, u32[]{:S(2)}) collective-permute-start(f32[4,2,96,96]{3,2,1,0:T(8,128)S(1)} %shard_map.96), channel_id=1, source_target_pairs={{0,4},{4,0},{8,12},{12,8},{16,20},{20,16},{24,28},{28,24},{1,5},{5... | collective-permute-start | bytes 884744 | tf_op jit(solution)/shard_map/ppermute | solution.py:19
  18.2 22.4 %copy-start.1 = (bf16[1,1,24,2048]{3,2,1,0:T(8,128)(2,1)S(1)}, bf16[1,1,24,2048]{3,2,1,0:T(8,128)(2,1)}, u32[]{:S(2)}) copy-start(bf16[1,1,24,2048]{3,2,1,0:T(8,128)(2,1)} %param.12) | copy-start | bytes 294916
  18.2 22.4 %copy-start.2 = (f32[1,1,2048]{2,1,0:T(1,128)S(1)}, f32[1,1,2048]{2,1,0:T(1,128)}, u32[]{:S(2)}) copy-start(f32[1,1,2048]{2,1,0:T(1,128)} %param.10) | copy-start | bytes 24580
  18.2 22.4 %copy-start.3 = (s32[1,1,6,256]{3,1,2,0:T(1,128)S(1)}, s32[1,1,6,256]{3,1,2,0:T(1,128)}, u32[]{:S(2)}) copy-start(s32[1,1,6,256]{3,1,2,0:T(1,128)} %param.14) | copy-start | bytes 18436
  18.2 22.5 %copy-start.4 = (s32[1,1,6]{2,1,0:T(1,128)S(1)}, s32[1,1,6]{2,1,0:T(1,128)}, u32[]{:S(2)}) copy-start(s32[1,1,6]{2,1,0:T(1,128)} %param.15) | copy-start | bytes 76
  26.1 11.5 %collective-permute-start = (bf16[288,256]{1,0:T(8,128)(2,1)}, bf16[288,256]{1,0:T(8,128)(2,1)S(1)}, u32[]{:S(2)}, u32[]{:S(2)}) collective-permute-start(bf16[288,256]{1,0:T(8,128)(2,1)} %get-tuple-element.22), channel_id=1, source_target_pairs={{0,1},{1,0},{2,3},{3,2},{4,5},{5,4},{6,7},{7,6},{8,9},{9,8},{10,11... | collective-permute-start | bytes 442376 | tf_op jit(solution)/shard_map/ppermute | solution.py:19
  26.7 12.2 %collective-permute-start.1 = (bf16[288,256]{1,0:T(8,128)(2,1)}, bf16[288,256]{1,0:T(8,128)(2,1)S(1)}, u32[]{:S(2)}, u32[]{:S(2)}) collective-permute-start(bf16[288,256]{1,0:T(8,128)(2,1)} %get-tuple-element.23), channel_id=1, source_target_pairs={{0,2},{1,3},{2,0},{3,1},{4,6},{5,7},{6,4},{7,5},{8,10},{9,11},{10,... | collective-permute-start | bytes 442376 | tf_op jit(solution)/shard_map/ppermute | solution.py:19
  28.2 11.8 %collective-permute-start.2 = (bf16[288,256]{1,0:T(8,128)(2,1)}, bf16[288,256]{1,0:T(8,128)(2,1)S(1)}, u32[]{:S(2)}, u32[]{:S(2)}) collective-permute-start(bf16[288,256]{1,0:T(8,128)(2,1)} %get-tuple-element.24), channel_id=1, source_target_pairs={{0,3},{1,2},{2,1},{3,0},{4,7},{5,6},{6,5},{7,4},{8,11},{9,10},{10,... | collective-permute-start | bytes 442376 | tf_op jit(solution)/shard_map/ppermute | solution.py:19
  28.4 12.2 %collective-permute-start.3 = (bf16[288,256]{1,0:T(8,128)(2,1)}, bf16[288,256]{1,0:T(8,128)(2,1)S(1)}, u32[]{:S(2)}, u32[]{:S(2)}) collective-permute-start(bf16[288,256]{1,0:T(8,128)(2,1)} %get-tuple-element.25), channel_id=1, source_target_pairs={{0,4},{4,0},{8,12},{12,8},{16,20},{20,16},{24,28},{28,24},{1,5},{5... | collective-permute-start | bytes 442376 | tf_op jit(solution)/shard_map/ppermute | solution.py:19
  31.0 9.6 %collective-permute-start.4 = (bf16[288,256]{1,0:T(8,128)(2,1)}, bf16[288,256]{1,0:T(8,128)(2,1)S(1)}, u32[]{:S(2)}, u32[]{:S(2)}) collective-permute-start(bf16[288,256]{1,0:T(8,128)(2,1)} %get-tuple-element.26), channel_id=1, source_target_pairs={{4,8},{12,16},{20,24},{8,4},{16,12},{24,20},{5,9},{13,17},{21,25},... | collective-permute-start | bytes 442376 | tf_op jit(solution)/shard_map/ppermute | solution.py:25
  37.6 6.7 %collective-permute-start.8 = (f32[64,256]{1,0:T(8,128)S(1)}, f32[64,256]{1,0:T(8,128)S(1)}, u32[]{:S(2)}, u32[]{:S(2)}) collective-permute-start(f32[64,256]{1,0:T(8,128)S(1)} %get-tuple-element.32), channel_id=1, source_target_pairs={{0,1},{1,0},{2,3},{3,2},{4,5},{5,4},{6,7},{7,6},{8,9},{9,8},{10,11... | collective-permute-start | bytes 196616 | tf_op jit(solution)/shard_map/ppermute | solution.py:19
  38.9 5.4 %collective-permute-start.9 = (f32[64,256]{1,0:T(8,128)S(1)}, f32[64,256]{1,0:T(8,128)S(1)}, u32[]{:S(2)}, u32[]{:S(2)}) collective-permute-start(f32[64,256]{1,0:T(8,128)S(1)} %get-tuple-element.33), channel_id=1, source_target_pairs={{0,2},{1,3},{2,0},{3,1},{4,6},{5,7},{6,4},{7,5},{8,10},{9,11},{10,... | collective-permute-start | bytes 196616 | tf_op jit(solution)/shard_map/ppermute | solution.py:19
  40.0 4.3 %collective-permute-start.10 = (f32[64,256]{1,0:T(8,128)S(1)}, f32[64,256]{1,0:T(8,128)S(1)}, u32[]{:S(2)}, u32[]{:S(2)}) collective-permute-start(f32[64,256]{1,0:T(8,128)S(1)} %get-tuple-element.34), channel_id=1, source_target_pairs={{0,3},{1,2},{2,1},{3,0},{4,7},{5,6},{6,5},{7,4},{8,11},{9,10},{10,... | collective-permute-start | bytes 196616 | tf_op jit(solution)/shard_map/ppermute | solution.py:19
  40.7 3.6 %copy-start = (f32[2048,256]{1,0:T(8,128)S(1)}, f32[2048,256]{1,0:T(8,128)}, u32[]{:S(2)}) copy-start(f32[2048,256]{1,0:T(8,128)} %get-tuple-element.20.part_ref) | copy-start | bytes 6291460

commit v4 on v3

--- a/solution.py
+++ b/solution.py
@@ -54,10 +54,6 @@
     return jnp.concatenate(
         [scale, jnp.zeros((LANES - scale.shape[0], LANES), f32)], axis=0
     ).T
-
-
-def fixed(shape):
-    return pl.BlockSpec(shape, lambda i: (0,) * len(shape))
 
 
 def call(kernel, outs, in_specs, args, grid=(1,), out_specs=None, scratch=(), flops=0, limit=24):
@@ -106,21 +102,7 @@
         yield (factor * res_ref[row : row + LANES, :].astype(f32)).astype(bf16)
 
 
-def front_kernel(slabs, groups, res_any, scale_any, basis_any, map_any, sent_ref, res_ref, scale_ref, basis_ref, map_ref, sems):
-    rows = res_ref.shape[0]
-    chunk = rows // 2
-    parts = [pl.ds(i * chunk, chunk) for i in range(rows // chunk)]
-    sources = [scale_any, basis_any, map_any] + [res_any.at[p] for p in parts]
-    targets = [scale_ref, basis_ref, map_ref] + [res_ref.at[p] for p in parts]
-    moves = copies(sources, targets, sems)
-    for move in moves[:3]:
-        move.wait()
-    scale_turned = turned_scale(scale_ref)
-    weighted = []
-    for i in range(rows // chunk):
-        moves[3 + i].wait()
-        weighted += list(weigh(scale_turned, res_ref, i * chunk, chunk))
-    primal = dot(basis_ref[...], jnp.concatenate(weighted, axis=0))
+def pack_pieces(slabs, groups, primal, map_ref, sent_ref):
     constraints, columns = primal.shape
     turned = jnp.concatenate([primal, jnp.zeros((LANES - constraints, columns), f32)], axis=0).T
     quarter = sent_ref.shape[1]
@@ -154,20 +136,26 @@
     return [n ^ k for k in range(1, groups)] + [groups + 1 - parity, groups + parity]
 
 
-def local_kernel(groups, inverse_any, res_any, scale_any, lane_scale_any, basis_any, index_any, part_any, *rest):
+def local_kernel(slabs, groups, inverse_any, res_any, scale_any, lane_scale_any, basis_any, index_any, map_any, sent_any, part_any, *rest):
     slots = groups + 1
     outs_any, outs = rest[:slots], rest[slots : 2 * slots]
-    lane_scale_ref, basis_ref, index_ref, inverse_ref, res_ref, scale_ref, weighted_ref, narrow_ref, part_ref, scaled_ref, sems, out_sems = rest[2 * slots :]
+    sent_ref, map_ref, lane_scale_ref, basis_ref, index_ref, inverse_ref, res_ref, scale_ref, weighted_ref, narrow_ref, part_ref, scaled_ref, sems, out_sems = rest[2 * slots :]
     rows = inverse_ref.shape[0]
     half = rows // 2
     halves = [pl.ds(i * half, half) for i in range(2)]
-    sources = [lane_scale_any, basis_any, index_any, scale_any, res_any]
-    targets = [lane_scale_ref, basis_ref, index_ref, scale_ref, res_ref]
+    sources = [scale_any, res_any, basis_any, map_any, lane_scale_any, index_any]
+    targets = [scale_ref, res_ref, basis_ref, map_ref, lane_scale_ref, index_ref]
     sources += [inverse_any.at[p] for p in halves]
     targets += [inverse_ref.at[p] for p in halves]
     moves = copies(sources, targets, sems)
-    for move in moves[:3]:
+    for move in moves[:6]:
         move.wait()
+    turned = turned_scale(scale_ref)
+    for j, value in enumerate(weigh(turned, res_ref, 0, rows)):
+        weighted_ref[j * LANES : (j + 1) * LANES, :] = value
+    pack_pieces(slabs, groups, dot(basis_ref[...], weighted_ref[...]), map_ref, sent_ref)
+    leaving = [pltpu.make_async_copy(sent_ref, sent_any, out_sems.at[2 + slots])]
+    leaving[0].start()
     capacity = index_ref.shape[2]
     constraints = basis_ref.shape[0]
     picks = [index_ref[r] for r in slot_rows(groups)]
@@ -184,14 +172,8 @@
             parts.append(value)
         fill = jnp.zeros((GROUP - constraints, capacity), f32)
         outs[k][capacity:, :] = jnp.concatenate([jnp.concatenate(parts, axis=1), fill], axis=0).astype(bf16)
-    for move in moves[3:5]:
-        move.wait()
-    turned = turned_scale(scale_ref)
-    for j, value in enumerate(weigh(turned, res_ref, 0, rows)):
-        weighted_ref[j * LANES : (j + 1) * LANES, :] = value
-    leaving = []
     for i, p in enumerate(halves):
-        moves[5 + i].wait()
+        moves[6 + i].wait()
         block = min(half, 256)
         for start in range(i * half, (i + 1) * half, block):
             part = dot(inverse_ref[start : start + block, :], weighted_ref[...])
@@ -267,21 +249,21 @@
 
 
 def solve_kernel(slabs, groups, constraints, offsets, right_ref, maps_ref, *rest):
-    count = len(offsets).bit_length()
-    held, shares = rest[:count], rest[count : count + groups]
-    raw, forward, backward, pivots, solved = rest[count + groups :]
+    mine, other, shares = rest[:2], rest[2:4], rest[4 : 4 + groups]
+    raw, forward, backward, pivots, solved = rest[4 + groups :]
     w, n = place_of()
-    size = held[0].shape[2]
+    core = n & 1
+    size = mine[0].shape[2]
     order = raw.shape[2]
     if size != order:
         raw[...] = jnp.zeros_like(raw)
     start = 0
-    for ref in held:
-        for i in range(ref.shape[0]):
+    for a, b in zip(mine, other):
+        for i in range(a.shape[0]):
             slab = w ^ offsets[start + i]
-            for j in range(2):
-                raw[j, slab, :size, :size] = ref[i, j]
-        start += ref.shape[0]
+            raw[core, slab, :size, :size] = a[i]
+            raw[1 - core, slab, :size, :size] = b[i]
+        start += a.shape[0]
     c = right_ref.shape[1]
     few = slabs <= 8
 
@@ -455,41 +437,32 @@
 
     any_space = pl.BlockSpec(memory_space=pl.ANY)
     vmem = pl.BlockSpec(memory_space=pltpu.VMEM)
-    factors = [jnp.stack([coarse_sub, coarse_pivot], axis=1)]
-    held, offsets, mask = factors[0], [0], slabs // 2
-    while mask:
+    n = lax.axis_index("narrow")
+    factors = [jnp.where((n & 1) == 0, coarse_sub, coarse_pivot)]
+    held, offsets = factors[0], [0]
+    masks = [1 << i for i in reversed(range(slabs.bit_length() - 1))]
+    masks[-2:] = masks[:-3:-1]
+    for mask in masks:
         factors.append(swap(held, "wide", mask))
         offsets = offsets + [o ^ mask for o in offsets]
-        mask //= 2
-        if mask:
+        if len(offsets) < slabs:
             held = join(factors)
 
-    sent = call(
-        functools.partial(front_kernel, slabs, groups),
-        struct((slabs * groups, quarter, LANES), f32),
-        [any_space] * 4,
-        (residual, scale, basis, primal_map[0]),
-        out_specs=fixed((slabs * groups, quarter, LANES)),
-        scratch=[
-            pltpu.VMEM((rows, columns), bf16),
-            pltpu.VMEM(scale.shape, f32),
-            pltpu.VMEM(basis.shape, bf16),
-            pltpu.VMEM(primal_map[0].shape, jnp.int32),
-            pltpu.SemaphoreType.DMA((5,)),
-        ],
-        flops=2 * constraints * rows * columns,
-        limit=63,
-    )
-    got = lax.all_to_all(sent, ("wide", "narrow"), split_axis=0, concat_axis=0, tiled=True)
-
-    part, *outgoing = call(
-        functools.partial(local_kernel, groups),
-        [struct((rows, columns), f32)] + [struct((capacity + GROUP, columns), bf16)] * slots,
-        [any_space] * 6,
-        (inverse, residual, scale, lane_scale, basis, index),
-        out_specs=[any_space] * (1 + slots),
+    mine, other = [held, factors[-1]], []
+    for piece in mine:
+        other.append(swap(piece, "narrow", 1))
+
+    sent, part, *outgoing = call(
+        functools.partial(local_kernel, slabs, groups),
+        [struct((slabs * groups, quarter, LANES), f32), struct((rows, columns), f32)]
+        + [struct((capacity + GROUP, columns), bf16)] * slots,
+        [any_space] * 7,
+        (inverse, residual, scale, lane_scale, basis, index, primal_map[0]),
+        out_specs=[any_space] * (2 + slots),
         scratch=[pltpu.VMEM((capacity + GROUP, columns), bf16)] * slots
         + [
+            pltpu.VMEM((slabs * groups, quarter, LANES), f32),
+            pltpu.VMEM(primal_map[0].shape, jnp.int32),
             pltpu.VMEM(lane_scale.shape, f32),
             pltpu.VMEM(basis.shape, bf16),
             pltpu.VMEM(index.shape, jnp.int32),
@@ -500,12 +473,13 @@
             pltpu.VMEM((rows, columns), bf16),
             pltpu.VMEM((rows, columns), f32),
             pltpu.VMEM((constraints, rows), f32),
-            pltpu.SemaphoreType.DMA((7,)),
-            pltpu.SemaphoreType.DMA((2 + slots,)),
+            pltpu.SemaphoreType.DMA((8,)),
+            pltpu.SemaphoreType.DMA((3 + slots,)),
         ],
         flops=2 * rows * columns * (rows + slots * capacity),
         limit=57,
     )
+    got = lax.all_to_all(sent, ("wide", "narrow"), split_axis=0, concat_axis=0, tiled=True)
     arrived = []
     for k in range(slots):
         if k < groups - 1:
@@ -525,8 +499,8 @@
     shares = call(
         functools.partial(solve_kernel, slabs, groups, constraints, offsets),
         [struct((own_columns, width), f32)] * groups,
-        [None] * (2 + len(factors)),
-        (right, maps, *factors),
+        [None] * (2 + len(mine) + len(other)),
+        (right, maps, *mine, *other),
         scratch=[
             pltpu.VMEM((2, slabs, order, order), f32),
             pltpu.VMEM((slabs, order, 2 * order), bf16),

time: 47 us -> 47.7 us (1.015)
  waiting for transfers between devices: 3.2 us -> 9.38 us
  Pallas kernels: 19.7 us -> 16.9 us
  starting transfers between devices: 22.8 us -> 20.1 us
    ppermute x10 -> x12, waiting for transfers between devices: 3.19 us -> 9.38 us  [swap(): return lax.ppermute(block, axis, [(i, i ^ mask) for i in range(count)])]
    pallas_call x8 -> x7, Pallas kernels: 19.7 us -> 16.9 us  [call(): pl.pallas_call(kernel, out_shape=outs, grid=grid, in_specs=in_specs, out_...]
    ppermute x10 -> x12, starting transfers between devices: 13.2 us -> 11 us  [swap(): return lax.ppermute(block, axis, [(i, i ^ mask) for i in range(count)])]
    all_to_all x1, starting transfers between devices: 6.26 us -> 4.64 us  [body(): lax.all_to_all(sent, ('wide', 'narrow'), split_axis=0, concat_axis=0, til...]
    ppermute x1, starting transfers between devices: 3.32 us -> 4.53 us  [swap_odd(): return lax.ppermute(block, axis, pairs + [(b, a) for a, b in pairs])]
    another operation x1 -> x0, other arithmetic: 0.83 us -> none  [body(): factors = [jnp.stack([coarse_sub, coarse_pivot], axis=1)]]
    select_n x0 -> x1, other arithmetic: none -> 0.81 us  [body(): factors = [jnp.where(n & 1 == 0, coarse_sub, coarse_pivot)]]
  transfers between devices with their start and end apart: 12 -> 14, of which waited for: 2 -> 2; matrix products, arithmetic and copies ran while one was open for 0% -> 0% of each run, Pallas kernels for 37% -> 31%
where the time goes in v4:
time: 47.7 us; the launch traced here: 47.4 us
  starting transfers between devices  20.1 us (42%)
  Pallas kernels  16.9 us (35%)
  waiting for transfers between devices  9.38 us (20%)
  other arithmetic  0.81 us (2%)
    pallas_call x7, Pallas kernels, call(): pl.pallas_call(kernel, out_shape=outs, grid=grid, in_specs=in_specs, out_...  16.9 us
    ppermute x12, starting transfers between devices, swap(): return lax.ppermute(block, axis, [(i, i ^ mask) for i in range(count)])  11 us
    ppermute x12, waiting for transfers between devices, swap(): return lax.ppermute(block, axis, [(i, i ^ mask) for i in range(count)])  9.38 us
    all_to_all x1, starting transfers between devices, body(): lax.all_to_all(sent, ('wide', 'narrow'), split_axis=0, concat_axis=0, til...  4.64 us
    ppermute x1, starting transfers between devices, swap_odd(): return lax.ppermute(block, axis, pairs + [(b, a) for a, b in pairs])  4.53 us
  transfers between devices with their start and end apart: 14, of which 2 were waited for; matrix products, arithmetic and copies ran while one was open for 0% of the time, Pallas kernels for 31%

profile of v4, /device:TPU:5, one launch (start us, length us, event | category | flops | bytes accessed | tf_op | source)
XLA Modules:
  0.0 47.4 jit_solution(15302900549800864733)
XLA Ops:
  0.0 0.8 %broadcast_select_fusion.refs_0_ = f32[1,96,96]{2,1,0:T(8,128)S(1)} fusion(f32[1,96,96]{2,1,0:T(8,128)} %param.16, f32[1,96,96]{2,1,0:T(8,128)} %param.17, pred[]{:T(512)S(6)} %eq.3), kind=kLoop, calls=%fused_computation | loop fusion | flops 9216 | bytes 110593 | tf_op jit(solution)/shard_map/jit(_where)/select_n | solution.py:441
  0.8 2.3 %collective-permute-start.5 = (f32[1,96,96]{2,1,0:T(8,128)S(1)}, f32[1,96,96]{2,1,0:T(8,128)S(1)}, u32[]{:S(2)}, u32[]{:S(2)}) collective-permute-start(f32[1,96,96]{2,1,0:T(8,128)S(1)} %broadcast_select_fusion.refs_0_), channel_id=1, source_target_pairs={{0,16},{4,20},{8,24},{12,28},{16,0},{20,4},{24,8},{28,12},{1,17},{... | collective-permute-start | bytes 110600 | tf_op jit(solution)/shard_map/ppermute | solution.py:19
  3.1 7.7 %shard_map.91 = (f32[32,16,128]{2,1,0:T(8,128)}, f32[2048,256]{1,0:T(8,128)}, bf16[288,256]{1,0:T(8,128)(2,1)}, bf16[288,256]{1,0:T(8,128)(2,1)}, bf16[288,256]{...) custom-call(bf16[2048,2048]{1,0:T(8,128)(2,1)} %bitcast.17, bf16[2048,256]{1,0:T(8,128)(2,1)} %bitcast.18, ...), custom_call_target="tpu_custom_call" | custom-call | flops 3489660928 | bytes 12654688 | tf_op jit(solution)/shard_map/pallas_call | solution.py:66
  10.8 0.0 copy-start.1
  10.9 0.0 copy-start.2
  10.9 0.0 copy-start.3
  10.9 0.0 copy-start.4
  10.9 4.6 %all-to-all-start = ((f32[32,16,128]{2,1,0:T(8,128)}), f32[32,16,128]{2,1,0:T(8,128)S(1)}, u32[]{:S(2)}, u32[]{:S(2)}) async-start(f32[32,16,128]{2,1,0:T(8,128)} %get-tuple-element.22), calls=%async_computation | async-start | bytes 524288 | tf_op jit(solution)/shard_map/all_to_all | solution.py:482
  15.5 0.0 collective-permute-done.5.refs_1_
  15.6 0.2 collective-permute-start.6
  15.7 5.8 %collective-permute-done.6.refs_2_ = f32[2,96,96]{2,1,0:T(8,128)S(1)} collective-permute-done((f32[2,96,96]{2,1,0:T(8,128)S(1)}, f32[2,96,96]{2,1,0:T(8,128)S(1)}, u32[]{:S(2)}, u32[]{:S(2)}) %collective-permute-start.6) | collective-permute-done | bytes 73760 | tf_op jit(solution)/shard_map/ppermute | solution.py:19
  21.5 1.9 %collective-permute-start.7 = (f32[4,96,96]{2,1,0:T(8,128)S(1)}, f32[4,96,96]{2,1,0:T(8,128)S(1)}, u32[]{:S(2)}, u32[]{:S(2)}) collective-permute-start(f32[4,96,96]{2,1,0:T(8,128)S(1)} %shard_map.95.rest_0_), channel_id=1, source_target_pairs={{0,8},{4,12},{8,0},{12,4},{16,24},{20,28},{24,16},{28,20},{1,9},{5... | collective-permute-start | bytes 442376 | tf_op jit(solution)/shard_map/ppermute | solution.py:19
  23.4 0.8 %collective-permute-start.8 = (f32[4,96,96]{2,1,0:T(8,128)S(1)}, f32[4,96,96]{2,1,0:T(8,128)S(1)}, u32[]{:S(2)}, u32[]{:S(2)}) collective-permute-start(f32[4,96,96]{2,1,0:T(8,128)S(1)} %shard_map.95.rest_0_), channel_id=1, source_target_pairs={{0,1},{1,0},{2,3},{3,2},{4,5},{5,4},{6,7},{7,6},{8,9},{9,8},{10,11... | collective-permute-start | bytes 442376 | tf_op jit(solution)/shard_map/ppermute | solution.py:19
  24.2 3.6 %collective-permute-done.7.rest_1_ = f32[4,96,96]{2,1,0:T(8,128)S(1)} collective-permute-done((f32[4,96,96]{2,1,0:T(8,128)S(1)}, f32[4,96,96]{2,1,0:T(8,128)S(1)}, u32[]{:S(2)}, u32[]{:S(2)}) %collective-permute-start.7) | collective-permute-done | bytes 147488 | tf_op jit(solution)/shard_map/ppermute | solution.py:19
  27.8 1.4 %collective-permute-start.9 = (f32[4,96,96]{2,1,0:T(8,128)S(1)}, f32[4,96,96]{2,1,0:T(8,128)S(1)}, u32[]{:S(2)}, u32[]{:S(2)}) collective-permute-start(f32[4,96,96]{2,1,0:T(8,128)S(1)} %collective-permute-done.7.rest_1_), channel_id=1, source_target_pairs={{0,1},{1,0},{2,3},{3,2},{4,5},{5,4},{6,7},{7,6},{8,9},{9,8},{10,11... | collective-permute-start | bytes 442376 | tf_op jit(solution)/shard_map/ppermute | solution.py:19
  29.2 0.0 collective-permute-start
  29.2 0.7 %collective-permute-start.1 = (bf16[288,256]{1,0:T(8,128)(2,1)}, bf16[288,256]{1,0:T(8,128)(2,1)S(1)}, u32[]{:S(2)}, u32[]{:S(2)}) collective-permute-start(bf16[288,256]{1,0:T(8,128)(2,1)} %get-tuple-element.25), channel_id=1, source_target_pairs={{0,2},{1,3},{2,0},{3,1},{4,6},{5,7},{6,4},{7,5},{8,10},{9,11},{10,... | collective-permute-start | bytes 442376 | tf_op jit(solution)/shard_map/ppermute | solution.py:19
  30.0 1.4 %collective-permute-start.2 = (bf16[288,256]{1,0:T(8,128)(2,1)}, bf16[288,256]{1,0:T(8,128)(2,1)S(1)}, u32[]{:S(2)}, u32[]{:S(2)}) collective-permute-start(bf16[288,256]{1,0:T(8,128)(2,1)} %get-tuple-element.26), channel_id=1, source_target_pairs={{0,3},{1,2},{2,1},{3,0},{4,7},{5,6},{6,5},{7,4},{8,11},{9,10},{10,... | collective-permute-start | bytes 442376 | tf_op jit(solution)/shard_map/ppermute | solution.py:19
  31.4 0.0 collective-permute-done.8.rest_2_
  31.4 0.0 collective-permute-start.3
  31.4 0.0 collective-permute-done.9.rest_3_
  31.4 4.5 %collective-permute-start.4 = (bf16[288,256]{1,0:T(8,128)(2,1)}, bf16[288,256]{1,0:T(8,128)(2,1)S(1)}, u32[]{:S(2)}, u32[]{:S(2)}) collective-permute-start(bf16[288,256]{1,0:T(8,128)(2,1)} %get-tuple-element.28), channel_id=1, source_target_pairs={{4,8},{12,16},{20,24},{8,4},{16,12},{24,20},{5,9},{13,17},{21,25},... | collective-permute-start | bytes 442376 | tf_op jit(solution)/shard_map/ppermute | solution.py:25
  35.9 0.0 all-to-all-done.got_ref
  35.9 0.5 %shard_map.92 = (f32[8,64,128]{2,1,0:T(8,128)S(1)}, f32[32,128]{1,0:T(8,128)S(1)}) custom-call(f32[32,16,128]{2,1,0:T(8,128)S(1)} %all-to-all-done.got_ref), custom_call_target="tpu_custom_call" | custom-call | flops 50331648 | bytes 540672 | tf_op jit(solution)/shard_map/pallas_call | solution.py:66
  36.4 2.7 %shard_map.96 = (f32[64,256]{1,0:T(8,128)S(1)}, f32[64,256]{1,0:T(8,128)S(1)}, f32[64,256]{1,0:T(8,128)S(1)}, f32[64,256]{1,0:T(8,128)S(1)}) custom-call(f32[8,64,128]{2,1,0:T(8,128)S(1)} %get-tuple-element.32.right_ref, f32[32,128]{1,0:T(8,128)S(1)} %get-tuple-element.23.maps_ref, f32[4,96,96]{2,1,0:T(8,128)S(1)} %shard_map.95.rest_0_, ...), custom_call_target="tpu_custom_call" | custom-call | flops 201326592 | bytes 1130496 | tf_op jit(solution)/shard_map/pallas_call | solution.py:66
  39.1 0.0 collective-permute-done.rest_0_
  39.2 0.4 collective-permute-start.10
  39.5 0.0 collective-permute-done.1.rest_1_
  39.5 0.4 collective-permute-start.11
  39.9 0.0 collective-permute-done.2.rest_2_
  39.9 1.5 %collective-permute-start.12 = (f32[64,256]{1,0:T(8,128)S(1)}, f32[64,256]{1,0:T(8,128)S(1)}, u32[]{:S(2)}, u32[]{:S(2)}) collective-permute-start(f32[64,256]{1,0:T(8,128)S(1)} %get-tuple-element.36), channel_id=1, source_target_pairs={{0,3},{1,2},{2,1},{3,0},{4,7},{5,6},{6,5},{7,4},{8,11},{9,10},{10,... | collective-permute-start | bytes 196616 | tf_op jit(solution)/shard_map/ppermute | solution.py:19
  41.4 0.0 collective-permute-done.3.rest_3_
  41.4 0.0 collective-permute-done.4.rest_4_
  41.4 0.0 copy-done.1
  41.4 0.0 copy-done.2
  41.4 0.0 copy-done.3
  41.4 0.0 copy-done.4
  41.4 0.0 copy-start
  41.4 3.6 %shard_map.93 = (f32[2048,256]{1,0:T(8,128)S(1)}, bf16[2048,256]{1,0:T(8,128)(2,1)S(1)}, bf16[2048,256]{1,0:T(8,128)(2,1)S(1)}) custom-call(s32[1,6]{1,0:T(1,128)S(1)} %bitcast.16, s32[6,1,256]{2,1,0:T(1,128)S(1)} %bitcast.15, f32[32,128]{1,0:T(8,128)S(1)} %get-tuple-element.23.maps_ref, f32[1,2048]{1,0:T(1,128)S(1)} %bitcast.13, ...), custom_call_target="tpu_custom_call" | custom-call | flops 2684354560 | bytes 5060632 | tf_op jit(solution)/shard_map/pallas_call | solution.py:66
  45.0 0.0 collective-permute-done.10.rest_1_
  45.0 0.0 collective-permute-done.11.rest_2_
  45.0 0.0 collective-permute-done.12.rest_3_
  45.0 0.0 copy-done
  45.0 2.4 %shard_map.97 = f32[2048,256]{1,0:T(8,128)} custom-call(f32[2048,256]{1,0:T(8,128)S(1)} %copy-done, f32[2048,256]{1,0:T(8,128)S(1)} %get-tuple-element.29.early_ref, bf16[2048,256]{1,0:T(8,128)(2,1)S(1)} %get-tuple-element.30.late_ref, bf16[2048,256]{1,0:T(8,128)(2,1)S(1)} %get-tuple-element.31.own_ref, f32[64,256]{1,0:T(8,128)S(1)} %get-tuple-element.33.rest_0_, ...), custom_call_target="tpu_custom_call" | custom-call | flops 805306368 | bytes 8650752 | tf_op jit(solution)/shard_map/pallas_call | solution.py:66
  (2 shorter events, 0.0 us)
Async XLA Ops:
  0.8 14.7 %collective-permute-start.5 = (f32[1,96,96]{2,1,0:T(8,128)S(1)}, f32[1,96,96]{2,1,0:T(8,128)S(1)}, u32[]{:S(2)}, u32[]{:S(2)}) collective-permute-start(f32[1,96,96]{2,1,0:T(8,128)S(1)} %broadcast_select_fusion.refs_0_), channel_id=1, source_target_pairs={{0,16},{4,20},{8,24},{12,28},{16,0},{20,4},{24,8},{28,12},{1,17},{... | collective-permute-start | bytes 110600 | tf_op jit(solution)/shard_map/ppermute | solution.py:19
  10.8 30.5 %copy-start.1 = (bf16[1,1,24,2048]{3,2,1,0:T(8,128)(2,1)S(1)}, bf16[1,1,24,2048]{3,2,1,0:T(8,128)(2,1)}, u32[]{:S(2)}) copy-start(bf16[1,1,24,2048]{3,2,1,0:T(8,128)(2,1)} %param.12) | copy-start | bytes 294916
  10.9 30.5 %copy-start.2 = (f32[1,1,2048]{2,1,0:T(1,128)S(1)}, f32[1,1,2048]{2,1,0:T(1,128)}, u32[]{:S(2)}) copy-start(f32[1,1,2048]{2,1,0:T(1,128)} %param.10) | copy-start | bytes 24580
  10.9 30.5 %copy-start.3 = (s32[1,1,6,256]{3,1,2,0:T(1,128)S(1)}, s32[1,1,6,256]{3,1,2,0:T(1,128)}, u32[]{:S(2)}) copy-start(s32[1,1,6,256]{3,1,2,0:T(1,128)} %param.14) | copy-start | bytes 18436
  10.9 30.5 %copy-start.4 = (s32[1,1,6]{2,1,0:T(1,128)S(1)}, s32[1,1,6]{2,1,0:T(1,128)}, u32[]{:S(2)}) copy-start(s32[1,1,6]{2,1,0:T(1,128)} %param.15) | copy-start | bytes 76
  10.9 25.0 %all-to-all-start = ((f32[32,16,128]{2,1,0:T(8,128)}), f32[32,16,128]{2,1,0:T(8,128)S(1)}, u32[]{:S(2)}, u32[]{:S(2)}) async-start(f32[32,16,128]{2,1,0:T(8,128)} %get-tuple-element.22), calls=%async_computation | async-start | bytes 524288 | tf_op jit(solution)/shard_map/all_to_all | solution.py:482
  15.6 5.9 %collective-permute-start.6 = (f32[2,96,96]{2,1,0:T(8,128)S(1)}, f32[2,96,96]{2,1,0:T(8,128)S(1)}, u32[]{:S(2)}, u32[]{:S(2)}) collective-permute-start(f32[2,96,96]{2,1,0:T(8,128)S(1)} %shard_map.94), channel_id=1, source_target_pairs={{0,4},{4,0},{8,12},{12,8},{16,20},{20,16},{24,28},{28,24},{1,5},{5... | collective-permute-start | bytes 221192 | tf_op jit(solution)/shard_map/ppermute | solution.py:19
  21.5 6.3 %collective-permute-start.7 = (f32[4,96,96]{2,1,0:T(8,128)S(1)}, f32[4,96,96]{2,1,0:T(8,128)S(1)}, u32[]{:S(2)}, u32[]{:S(2)}) collective-permute-start(f32[4,96,96]{2,1,0:T(8,128)S(1)} %shard_map.95.rest_0_), channel_id=1, source_target_pairs={{0,8},{4,12},{8,0},{12,4},{16,24},{20,28},{24,16},{28,20},{1,9},{5... | collective-permute-start | bytes 442376 | tf_op jit(solution)/shard_map/ppermute | solution.py:19
  23.4 8.0 %collective-permute-start.8 = (f32[4,96,96]{2,1,0:T(8,128)S(1)}, f32[4,96,96]{2,1,0:T(8,128)S(1)}, u32[]{:S(2)}, u32[]{:S(2)}) collective-permute-start(f32[4,96,96]{2,1,0:T(8,128)S(1)} %shard_map.95.rest_0_), channel_id=1, source_target_pairs={{0,1},{1,0},{2,3},{3,2},{4,5},{5,4},{6,7},{7,6},{8,9},{9,8},{10,11... | collective-permute-start | bytes 442376 | tf_op jit(solution)/shard_map/ppermute | solution.py:19
  27.8 3.6 %collective-permute-start.9 = (f32[4,96,96]{2,1,0:T(8,128)S(1)}, f32[4,96,96]{2,1,0:T(8,128)S(1)}, u32[]{:S(2)}, u32[]{:S(2)}) collective-permute-start(f32[4,96,96]{2,1,0:T(8,128)S(1)} %collective-permute-done.7.rest_1_), channel_id=1, source_target_pairs={{0,1},{1,0},{2,3},{3,2},{4,5},{5,4},{6,7},{7,6},{8,9},{9,8},{10,11... | collective-permute-start | bytes 442376 | tf_op jit(solution)/shard_map/ppermute | solution.py:19
  29.2 9.9 %collective-permute-start = (bf16[288,256]{1,0:T(8,128)(2,1)}, bf16[288,256]{1,0:T(8,128)(2,1)S(1)}, u32[]{:S(2)}, u32[]{:S(2)}) collective-permute-start(bf16[288,256]{1,0:T(8,128)(2,1)} %get-tuple-element.24), channel_id=1, source_target_pairs={{0,1},{1,0},{2,3},{3,2},{4,5},{5,4},{6,7},{7,6},{8,9},{9,8},{10,11... | collective-permute-start | bytes 442376 | tf_op jit(solution)/shard_map/ppermute | solution.py:19
  29.2 10.3 %collective-permute-start.1 = (bf16[288,256]{1,0:T(8,128)(2,1)}, bf16[288,256]{1,0:T(8,128)(2,1)S(1)}, u32[]{:S(2)}, u32[]{:S(2)}) collective-permute-start(bf16[288,256]{1,0:T(8,128)(2,1)} %get-tuple-element.25), channel_id=1, source_target_pairs={{0,2},{1,3},{2,0},{3,1},{4,6},{5,7},{6,4},{7,5},{8,10},{9,11},{10,... | collective-permute-start | bytes 442376 | tf_op jit(solution)/shard_map/ppermute | solution.py:19
  30.0 9.9 %collective-permute-start.2 = (bf16[288,256]{1,0:T(8,128)(2,1)}, bf16[288,256]{1,0:T(8,128)(2,1)S(1)}, u32[]{:S(2)}, u32[]{:S(2)}) collective-permute-start(bf16[288,256]{1,0:T(8,128)(2,1)} %get-tuple-element.26), channel_id=1, source_target_pairs={{0,3},{1,2},{2,1},{3,0},{4,7},{5,6},{6,5},{7,4},{8,11},{9,10},{10,... | collective-permute-start | bytes 442376 | tf_op jit(solution)/shard_map/ppermute | solution.py:19
  31.4 10.0 %collective-permute-start.3 = (bf16[288,256]{1,0:T(8,128)(2,1)}, bf16[288,256]{1,0:T(8,128)(2,1)S(1)}, u32[]{:S(2)}, u32[]{:S(2)}) collective-permute-start(bf16[288,256]{1,0:T(8,128)(2,1)} %get-tuple-element.27), channel_id=1, source_target_pairs={{0,4},{4,0},{8,12},{12,8},{16,20},{20,16},{24,28},{28,24},{1,5},{5... | collective-permute-start | bytes 442376 | tf_op jit(solution)/shard_map/ppermute | solution.py:19
  31.4 10.0 %collective-permute-start.4 = (bf16[288,256]{1,0:T(8,128)(2,1)}, bf16[288,256]{1,0:T(8,128)(2,1)S(1)}, u32[]{:S(2)}, u32[]{:S(2)}) collective-permute-start(bf16[288,256]{1,0:T(8,128)(2,1)} %get-tuple-element.28), channel_id=1, source_target_pairs={{4,8},{12,16},{20,24},{8,4},{16,12},{24,20},{5,9},{13,17},{21,25},... | collective-permute-start | bytes 442376 | tf_op jit(solution)/shard_map/ppermute | solution.py:25
  39.2 5.9 %collective-permute-start.10 = (f32[64,256]{1,0:T(8,128)S(1)}, f32[64,256]{1,0:T(8,128)S(1)}, u32[]{:S(2)}, u32[]{:S(2)}) collective-permute-start(f32[64,256]{1,0:T(8,128)S(1)} %get-tuple-element.34), channel_id=1, source_target_pairs={{0,1},{1,0},{2,3},{3,2},{4,5},{5,4},{6,7},{7,6},{8,9},{9,8},{10,11... | collective-permute-start | bytes 196616 | tf_op jit(solution)/shard_map/ppermute | solution.py:19
  39.5 5.5 %collective-permute-start.11 = (f32[64,256]{1,0:T(8,128)S(1)}, f32[64,256]{1,0:T(8,128)S(1)}, u32[]{:S(2)}, u32[]{:S(2)}) collective-permute-start(f32[64,256]{1,0:T(8,128)S(1)} %get-tuple-element.35), channel_id=1, source_target_pairs={{0,2},{1,3},{2,0},{3,1},{4,6},{5,7},{6,4},{7,5},{8,10},{9,11},{10,... | collective-permute-start | bytes 196616 | tf_op jit(solution)/shard_map/ppermute | solution.py:19
  39.9 5.1 %collective-permute-start.12 = (f32[64,256]{1,0:T(8,128)S(1)}, f32[64,256]{1,0:T(8,128)S(1)}, u32[]{:S(2)}, u32[]{:S(2)}) collective-permute-start(f32[64,256]{1,0:T(8,128)S(1)} %get-tuple-element.36), channel_id=1, source_target_pairs={{0,3},{1,2},{2,1},{3,0},{4,7},{5,6},{6,5},{7,4},{8,11},{9,10},{10,... | collective-permute-start | bytes 196616 | tf_op jit(solution)/shard_map/ppermute | solution.py:19
  41.4 3.6 %copy-start = (f32[2048,256]{1,0:T(8,128)S(1)}, f32[2048,256]{1,0:T(8,128)}, u32[]{:S(2)}) copy-start(f32[2048,256]{1,0:T(8,128)} %get-tuple-element.21.part_ref) | copy-start | bytes 6291460

commit v5 on v4

--- a/solution.py
+++ b/solution.py
@@ -139,7 +139,7 @@
 def local_kernel(slabs, groups, inverse_any, res_any, scale_any, lane_scale_any, basis_any, index_any, map_any, sent_any, part_any, *rest):
     slots = groups + 1
     outs_any, outs = rest[:slots], rest[slots : 2 * slots]
-    sent_ref, map_ref, lane_scale_ref, basis_ref, index_ref, inverse_ref, res_ref, scale_ref, weighted_ref, narrow_ref, part_ref, scaled_ref, sems, out_sems = rest[2 * slots :]
+    sent_ref, map_ref, lane_scale_ref, basis_ref, index_ref, inverse_ref, res_ref, scale_ref, weighted_ref, narrow_ref, part_ref, scaled_ref, first_ref, sems, out_sems = rest[2 * slots :]
     rows = inverse_ref.shape[0]
     half = rows // 2
     halves = [pl.ds(i * half, half) for i in range(2)]
@@ -172,6 +172,9 @@
             parts.append(value)
         fill = jnp.zeros((GROUP - constraints, capacity), f32)
         outs[k][capacity:, :] = jnp.concatenate([jnp.concatenate(parts, axis=1), fill], axis=0).astype(bf16)
+    spare_rows = [jnp.zeros((LANES - slots, capacity), jnp.int32)]
+    columns_of = jnp.concatenate(picks + spare_rows, axis=0).astype(f32).T
+    lanes = iota((capacity, LANES), 1).astype(f32)
     for i, p in enumerate(halves):
         moves[6 + i].wait()
         block = min(half, 256)
@@ -186,16 +189,20 @@
         leave = pltpu.make_async_copy(part_ref.at[p], part_any.at[p], out_sems.at[i])
         leave.start()
         leaving.append(leave)
-    spare_rows = [jnp.zeros((LANES - slots, capacity), jnp.int32)]
-    columns_of = jnp.concatenate(picks + spare_rows, axis=0).astype(f32).T
-    lanes = iota((capacity, LANES), 1).astype(f32)
-    for k in range(slots):
-        spot = jnp.broadcast_to(columns_of[:, k : k + 1], (capacity, LANES))
-        hots = [(spot == lanes + float(j * LANES)).astype(f32).astype(bf16) for j in range(rows // LANES)]
-        outs[k][:capacity, :] = dot(jnp.concatenate(hots, axis=1), narrow_ref[...]).astype(bf16)
-        leave = pltpu.make_async_copy(outs[k], outs_any[k], out_sems.at[2 + k])
-        leave.start()
-        leaving.append(leave)
+        for k in range(slots):
+            spot = jnp.broadcast_to(columns_of[:, k : k + 1], (capacity, LANES))
+            hots = [
+                (spot == lanes + float(j * LANES)).astype(f32).astype(bf16)
+                for j in range(i * half // LANES, (i + 1) * half // LANES)
+            ]
+            found = dot(jnp.concatenate(hots, axis=1), narrow_ref[i * half : (i + 1) * half, :])
+            if i == 0:
+                first_ref[k] = found
+                continue
+            outs[k][:capacity, :] = (first_ref[k] + found).astype(bf16)
+            leave = pltpu.make_async_copy(outs[k], outs_any[k], out_sems.at[2 + k])
+            leave.start()
+            leaving.append(leave)
     for leave in leaving:
         leave.wait()
 
@@ -378,27 +385,31 @@
 
 def final_kernel(groups, size, constraints, part_ref, early_ref, late_ref, own_ref, *rest):
     pieces = rest[:groups]
-    out_ref, values, highs, lows, owns = rest[groups:]
+    out_any, out_ref, values, highs, lows, owns, sems = rest[groups:]
     _, n = place_of()
-
-    @pl.when(pl.program_id(0) == 0)
-    def _():
-        c = pieces[0].shape[0]
-        for k in range(groups):
-            values[pl.ds(pl.multiple_of((n ^ k) * c, c), c), :] = pieces[k][...]
-        value = values[...].T
-        high = value.astype(bf16).astype(f32)
-        low = value - high
-        highs[...] = high.astype(bf16)
-        lows[...] = low.astype(bf16)
-        upper = iota(value.shape, 0) < size + 4 * constraints
-        owns[...] = jnp.where(upper, high, low).astype(bf16)
-
-    block = out_ref.shape[0]
-    here = pl.ds(pl.multiple_of(pl.program_id(0) * block, block), block)
-    late = late_ref[here, :]
-    combined = (part_ref[here, :] + dot(own_ref[here, :], owns[...])).astype(bf16).astype(f32)
-    out_ref[...] = combined + (early_ref[here, :] + (dot(late, highs[...]) + dot(late, lows[...])))
+    c = pieces[0].shape[0]
+    for k in range(groups):
+        values[pl.ds(pl.multiple_of((n ^ k) * c, c), c), :] = pieces[k][...]
+    value = values[...].T
+    high = value.astype(bf16).astype(f32)
+    low = value - high
+    highs[...] = high.astype(bf16)
+    lows[...] = low.astype(bf16)
+    upper = iota(value.shape, 0) < size + 4 * constraints
+    owns[...] = jnp.where(upper, high, low).astype(bf16)
+    rows = out_ref.shape[0]
+    block = rows // 4
+    leaving = []
+    for i in range(4):
+        here = slice(i * block, (i + 1) * block)
+        late = late_ref[here, :]
+        combined = (part_ref[here, :] + dot(own_ref[here, :], owns[...])).astype(bf16).astype(f32)
+        out_ref[here, :] = combined + (early_ref[here, :] + (dot(late, highs[...]) + dot(late, lows[...])))
+        p = pl.ds(i * block, block)
+        leaving.append(pltpu.make_async_copy(out_ref.at[p], out_any.at[p], sems.at[i]))
+        leaving[-1].start()
+    for leave in leaving:
+        leave.wait()
 
 
 def body(
@@ -429,9 +440,6 @@
     lane_scale = scaling[0]
     struct = jax.ShapeDtypeStruct
 
-    def by_rows(block, cols):
-        return pl.BlockSpec((block, cols), lambda i: (i, 0))
-
     def by_lanes(count, block):
         return pl.BlockSpec((count, block), lambda i: (0, i))
 
@@ -473,6 +481,7 @@
             pltpu.VMEM((rows, columns), bf16),
             pltpu.VMEM((rows, columns), f32),
             pltpu.VMEM((constraints, rows), f32),
+            pltpu.VMEM((slots, capacity, columns), f32),
             pltpu.SemaphoreType.DMA((8,)),
             pltpu.SemaphoreType.DMA((3 + slots,)),
         ],
@@ -532,13 +541,14 @@
         struct((rows, columns), f32),
         [vmem] * 4 + [None] * groups,
         (part, early, late, own, *pieces),
-        grid=(rows // block,),
-        out_specs=by_rows(block, columns),
+        out_specs=any_space,
         scratch=[
+            pltpu.VMEM((rows, columns), f32),
             pltpu.VMEM((columns, width), f32),
             pltpu.VMEM((width, columns), bf16),
             pltpu.VMEM((width, columns), bf16),
             pltpu.VMEM((width, columns), bf16),
+            pltpu.SemaphoreType.DMA((4,)),
         ],
         flops=2 * rows * columns * 3 * width,
     )

time: 47.7 us -> 47.4 us (level)
  transfers between devices with their start and end apart: 14 -> 14, of which waited for: 2 -> 2; matrix products, arithmetic and copies ran while one was open for 0% -> 0% of each run, Pallas kernels for 31% -> 30%
where the time goes in v5:
time: 47.4 us; the launch traced here: 47.1 us
  starting transfers between devices  20.1 us (42%)
  Pallas kernels  16.6 us (35%)
  waiting for transfers between devices  9.38 us (20%)
  other arithmetic  0.81 us (2%)
    pallas_call x7, Pallas kernels, call(): pl.pallas_call(kernel, out_shape=outs, grid=grid, in_specs=in_specs, out_...  16.6 us
    ppermute x12, starting transfers between devices, swap(): return lax.ppermute(block, axis, [(i, i ^ mask) for i in range(count)])  11 us
    ppermute x12, waiting for transfers between devices, swap(): return lax.ppermute(block, axis, [(i, i ^ mask) for i in range(count)])  9.38 us
    all_to_all x1, starting transfers between devices, body(): lax.all_to_all(sent, ('wide', 'narrow'), split_axis=0, concat_axis=0, til...  4.64 us
    ppermute x1, starting transfers between devices, swap_odd(): return lax.ppermute(block, axis, pairs + [(b, a) for a, b in pairs])  4.53 us
  transfers between devices with their start and end apart: 14, of which 2 were waited for; matrix products, arithmetic and copies ran while one was open for 0% of the time, Pallas kernels for 30%

profile of v5, /device:TPU:5, one launch (start us, length us, event | category | flops | bytes accessed | tf_op | source)
XLA Modules:
  0.0 47.1 jit_solution(8047701992862099577)
XLA Ops:
  0.0 0.8 %broadcast_select_fusion.refs_0_ = f32[1,96,96]{2,1,0:T(8,128)S(1)} fusion(f32[1,96,96]{2,1,0:T(8,128)} %param.16, f32[1,96,96]{2,1,0:T(8,128)} %param.17, pred[]{:T(512)S(6)} %eq.3), kind=kLoop, calls=%fused_computation | loop fusion | flops 9216 | bytes 110593 | tf_op jit(solution)/shard_map/jit(_where)/select_n | solution.py:449
  0.8 2.3 %collective-permute-start.5 = (f32[1,96,96]{2,1,0:T(8,128)S(1)}, f32[1,96,96]{2,1,0:T(8,128)S(1)}, u32[]{:S(2)}, u32[]{:S(2)}) collective-permute-start(f32[1,96,96]{2,1,0:T(8,128)S(1)} %broadcast_select_fusion.refs_0_), channel_id=1, source_target_pairs={{0,16},{4,20},{8,24},{12,28},{16,0},{20,4},{24,8},{28,12},{1,17},{... | collective-permute-start | bytes 110600 | tf_op jit(solution)/shard_map/ppermute | solution.py:19
  3.1 7.6 %shard_map.91 = (f32[32,16,128]{2,1,0:T(8,128)}, f32[2048,256]{1,0:T(8,128)}, bf16[288,256]{1,0:T(8,128)(2,1)}, bf16[288,256]{1,0:T(8,128)(2,1)}, bf16[288,256]{...) custom-call(bf16[2048,2048]{1,0:T(8,128)(2,1)} %bitcast.17, bf16[2048,256]{1,0:T(8,128)(2,1)} %bitcast.18, ...), custom_call_target="tpu_custom_call" | custom-call | flops 3489660928 | bytes 12654688 | tf_op jit(solution)/shard_map/pallas_call | solution.py:66
  10.7 0.0 copy-start.1
  10.7 0.0 copy-start.2
  10.7 0.0 copy-start.3
  10.7 0.0 copy-start.4
  10.7 4.6 %all-to-all-start = ((f32[32,16,128]{2,1,0:T(8,128)}), f32[32,16,128]{2,1,0:T(8,128)S(1)}, u32[]{:S(2)}, u32[]{:S(2)}) async-start(f32[32,16,128]{2,1,0:T(8,128)} %get-tuple-element.22), calls=%async_computation | async-start | bytes 524288 | tf_op jit(solution)/shard_map/all_to_all | solution.py:491
  15.4 0.0 collective-permute-done.5.refs_1_
  15.4 0.2 collective-permute-start.6
  15.6 5.8 %collective-permute-done.6.refs_2_ = f32[2,96,96]{2,1,0:T(8,128)S(1)} collective-permute-done((f32[2,96,96]{2,1,0:T(8,128)S(1)}, f32[2,96,96]{2,1,0:T(8,128)S(1)}, u32[]{:S(2)}, u32[]{:S(2)}) %collective-permute-start.6) | collective-permute-done | bytes 73760 | tf_op jit(solution)/shard_map/ppermute | solution.py:19
  21.4 1.9 %collective-permute-start.7 = (f32[4,96,96]{2,1,0:T(8,128)S(1)}, f32[4,96,96]{2,1,0:T(8,128)S(1)}, u32[]{:S(2)}, u32[]{:S(2)}) collective-permute-start(f32[4,96,96]{2,1,0:T(8,128)S(1)} %shard_map.95.rest_0_), channel_id=1, source_target_pairs={{0,8},{4,12},{8,0},{12,4},{16,24},{20,28},{24,16},{28,20},{1,9},{5... | collective-permute-start | bytes 442376 | tf_op jit(solution)/shard_map/ppermute | solution.py:19
  23.2 0.8 %collective-permute-start.8 = (f32[4,96,96]{2,1,0:T(8,128)S(1)}, f32[4,96,96]{2,1,0:T(8,128)S(1)}, u32[]{:S(2)}, u32[]{:S(2)}) collective-permute-start(f32[4,96,96]{2,1,0:T(8,128)S(1)} %shard_map.95.rest_0_), channel_id=1, source_target_pairs={{0,1},{1,0},{2,3},{3,2},{4,5},{5,4},{6,7},{7,6},{8,9},{9,8},{10,11... | collective-permute-start | bytes 442376 | tf_op jit(solution)/shard_map/ppermute | solution.py:19
  24.1 3.6 %collective-permute-done.7.rest_1_ = f32[4,96,96]{2,1,0:T(8,128)S(1)} collective-permute-done((f32[4,96,96]{2,1,0:T(8,128)S(1)}, f32[4,96,96]{2,1,0:T(8,128)S(1)}, u32[]{:S(2)}, u32[]{:S(2)}) %collective-permute-start.7) | collective-permute-done | bytes 147488 | tf_op jit(solution)/shard_map/ppermute | solution.py:19
  27.7 1.4 %collective-permute-start.9 = (f32[4,96,96]{2,1,0:T(8,128)S(1)}, f32[4,96,96]{2,1,0:T(8,128)S(1)}, u32[]{:S(2)}, u32[]{:S(2)}) collective-permute-start(f32[4,96,96]{2,1,0:T(8,128)S(1)} %collective-permute-done.7.rest_1_), channel_id=1, source_target_pairs={{0,1},{1,0},{2,3},{3,2},{4,5},{5,4},{6,7},{7,6},{8,9},{9,8},{10,11... | collective-permute-start | bytes 442376 | tf_op jit(solution)/shard_map/ppermute | solution.py:19
  29.1 0.0 collective-permute-start
  29.1 0.7 %collective-permute-start.1 = (bf16[288,256]{1,0:T(8,128)(2,1)}, bf16[288,256]{1,0:T(8,128)(2,1)S(1)}, u32[]{:S(2)}, u32[]{:S(2)}) collective-permute-start(bf16[288,256]{1,0:T(8,128)(2,1)} %get-tuple-element.25), channel_id=1, source_target_pairs={{0,2},{1,3},{2,0},{3,1},{4,6},{5,7},{6,4},{7,5},{8,10},{9,11},{10,... | collective-permute-start | bytes 442376 | tf_op jit(solution)/shard_map/ppermute | solution.py:19
  29.8 1.4 %collective-permute-start.2 = (bf16[288,256]{1,0:T(8,128)(2,1)}, bf16[288,256]{1,0:T(8,128)(2,1)S(1)}, u32[]{:S(2)}, u32[]{:S(2)}) collective-permute-start(bf16[288,256]{1,0:T(8,128)(2,1)} %get-tuple-element.26), channel_id=1, source_target_pairs={{0,3},{1,2},{2,1},{3,0},{4,7},{5,6},{6,5},{7,4},{8,11},{9,10},{10,... | collective-permute-start | bytes 442376 | tf_op jit(solution)/shard_map/ppermute | solution.py:19
  31.2 0.0 collective-permute-done.8.rest_2_
  31.2 0.0 collective-permute-start.3
  31.2 0.0 collective-permute-done.9.rest_3_
  31.3 4.5 %collective-permute-start.4 = (bf16[288,256]{1,0:T(8,128)(2,1)}, bf16[288,256]{1,0:T(8,128)(2,1)S(1)}, u32[]{:S(2)}, u32[]{:S(2)}) collective-permute-start(bf16[288,256]{1,0:T(8,128)(2,1)} %get-tuple-element.28), channel_id=1, source_target_pairs={{4,8},{12,16},{20,24},{8,4},{16,12},{24,20},{5,9},{13,17},{21,25},... | collective-permute-start | bytes 442376 | tf_op jit(solution)/shard_map/ppermute | solution.py:25
  35.8 0.0 all-to-all-done.got_ref
  35.8 0.5 %shard_map.92 = (f32[8,64,128]{2,1,0:T(8,128)S(1)}, f32[32,128]{1,0:T(8,128)S(1)}) custom-call(f32[32,16,128]{2,1,0:T(8,128)S(1)} %all-to-all-done.got_ref), custom_call_target="tpu_custom_call" | custom-call | flops 50331648 | bytes 540672 | tf_op jit(solution)/shard_map/pallas_call | solution.py:66
  36.3 2.7 %shard_map.96 = (f32[64,256]{1,0:T(8,128)S(1)}, f32[64,256]{1,0:T(8,128)S(1)}, f32[64,256]{1,0:T(8,128)S(1)}, f32[64,256]{1,0:T(8,128)S(1)}) custom-call(f32[8,64,128]{2,1,0:T(8,128)S(1)} %get-tuple-element.32.right_ref, f32[32,128]{1,0:T(8,128)S(1)} %get-tuple-element.23.maps_ref, f32[4,96,96]{2,1,0:T(8,128)S(1)} %shard_map.95.rest_0_, ...), custom_call_target="tpu_custom_call" | custom-call | flops 201326592 | bytes 1130496 | tf_op jit(solution)/shard_map/pallas_call | solution.py:66
  39.0 0.0 collective-permute-done.rest_0_
  39.0 0.3 collective-permute-start.10
  39.4 0.0 collective-permute-done.1.rest_1_
  39.4 0.4 collective-permute-start.11
  39.8 0.0 collective-permute-done.2.rest_2_
  39.8 1.5 %collective-permute-start.12 = (f32[64,256]{1,0:T(8,128)S(1)}, f32[64,256]{1,0:T(8,128)S(1)}, u32[]{:S(2)}, u32[]{:S(2)}) collective-permute-start(f32[64,256]{1,0:T(8,128)S(1)} %get-tuple-element.36), channel_id=1, source_target_pairs={{0,3},{1,2},{2,1},{3,0},{4,7},{5,6},{6,5},{7,4},{8,11},{9,10},{10,... | collective-permute-start | bytes 196616 | tf_op jit(solution)/shard_map/ppermute | solution.py:19
  41.2 0.0 collective-permute-done.3.rest_3_
  41.2 0.0 collective-permute-done.4.rest_4_
  41.2 0.0 copy-done.1
  41.2 0.0 copy-done.2
  41.3 0.0 copy-done.3
  41.3 0.0 copy-done.4
  41.3 0.0 copy-start
  41.3 3.6 %shard_map.93 = (f32[2048,256]{1,0:T(8,128)S(1)}, bf16[2048,256]{1,0:T(8,128)(2,1)S(1)}, bf16[2048,256]{1,0:T(8,128)(2,1)S(1)}) custom-call(s32[1,6]{1,0:T(1,128)S(1)} %bitcast.16, s32[6,1,256]{2,1,0:T(1,128)S(1)} %bitcast.15, f32[32,128]{1,0:T(8,128)S(1)} %get-tuple-element.23.maps_ref, f32[1,2048]{1,0:T(1,128)S(1)} %bitcast.13, ...), custom_call_target="tpu_custom_call" | custom-call | flops 2684354560 | bytes 5060632 | tf_op jit(solution)/shard_map/pallas_call | solution.py:66
  44.9 0.0 collective-permute-done.10.rest_1_
  44.9 0.0 collective-permute-done.11.rest_2_
  44.9 0.0 collective-permute-done.12.rest_3_
  44.9 0.0 copy-done
  44.9 2.2 %shard_map.97 = f32[2048,256]{1,0:T(8,128)} custom-call(f32[2048,256]{1,0:T(8,128)S(1)} %copy-done, f32[2048,256]{1,0:T(8,128)S(1)} %get-tuple-element.29.early_ref, bf16[2048,256]{1,0:T(8,128)(2,1)S(1)} %get-tuple-element.30.late_ref, bf16[2048,256]{1,0:T(8,128)(2,1)S(1)} %get-tuple-element.31.own_ref, f32[64,256]{1,0:T(8,128)S(1)} %get-tuple-element.33.rest_0_, ...), custom_call_target="tpu_custom_call" | custom-call | flops 805306368 | bytes 8650752 | tf_op jit(solution)/shard_map/pallas_call | solution.py:66
  (2 shorter events, 0.0 us)
Async XLA Ops:
  0.8 14.6 %collective-permute-start.5 = (f32[1,96,96]{2,1,0:T(8,128)S(1)}, f32[1,96,96]{2,1,0:T(8,128)S(1)}, u32[]{:S(2)}, u32[]{:S(2)}) collective-permute-start(f32[1,96,96]{2,1,0:T(8,128)S(1)} %broadcast_select_fusion.refs_0_), channel_id=1, source_target_pairs={{0,16},{4,20},{8,24},{12,28},{16,0},{20,4},{24,8},{28,12},{1,17},{... | collective-permute-start | bytes 110600 | tf_op jit(solution)/shard_map/ppermute | solution.py:19
  10.7 30.5 %copy-start.1 = (bf16[1,1,24,2048]{3,2,1,0:T(8,128)(2,1)S(1)}, bf16[1,1,24,2048]{3,2,1,0:T(8,128)(2,1)}, u32[]{:S(2)}) copy-start(bf16[1,1,24,2048]{3,2,1,0:T(8,128)(2,1)} %param.12) | copy-start | bytes 294916
  10.7 30.5 %copy-start.2 = (f32[1,1,2048]{2,1,0:T(1,128)S(1)}, f32[1,1,2048]{2,1,0:T(1,128)}, u32[]{:S(2)}) copy-start(f32[1,1,2048]{2,1,0:T(1,128)} %param.10) | copy-start | bytes 24580
  10.7 30.5 %copy-start.3 = (s32[1,1,6,256]{3,1,2,0:T(1,128)S(1)}, s32[1,1,6,256]{3,1,2,0:T(1,128)}, u32[]{:S(2)}) copy-start(s32[1,1,6,256]{3,1,2,0:T(1,128)} %param.14) | copy-start | bytes 18436
  10.7 30.5 %copy-start.4 = (s32[1,1,6]{2,1,0:T(1,128)S(1)}, s32[1,1,6]{2,1,0:T(1,128)}, u32[]{:S(2)}) copy-start(s32[1,1,6]{2,1,0:T(1,128)} %param.15) | copy-start | bytes 76
  10.7 25.1 %all-to-all-start = ((f32[32,16,128]{2,1,0:T(8,128)}), f32[32,16,128]{2,1,0:T(8,128)S(1)}, u32[]{:S(2)}, u32[]{:S(2)}) async-start(f32[32,16,128]{2,1,0:T(8,128)} %get-tuple-element.22), calls=%async_computation | async-start | bytes 524288 | tf_op jit(solution)/shard_map/all_to_all | solution.py:491
  15.4 5.9 %collective-permute-start.6 = (f32[2,96,96]{2,1,0:T(8,128)S(1)}, f32[2,96,96]{2,1,0:T(8,128)S(1)}, u32[]{:S(2)}, u32[]{:S(2)}) collective-permute-start(f32[2,96,96]{2,1,0:T(8,128)S(1)} %shard_map.94), channel_id=1, source_target_pairs={{0,4},{4,0},{8,12},{12,8},{16,20},{20,16},{24,28},{28,24},{1,5},{5... | collective-permute-start | bytes 221192 | tf_op jit(solution)/shard_map/ppermute | solution.py:19
  21.4 6.3 %collective-permute-start.7 = (f32[4,96,96]{2,1,0:T(8,128)S(1)}, f32[4,96,96]{2,1,0:T(8,128)S(1)}, u32[]{:S(2)}, u32[]{:S(2)}) collective-permute-start(f32[4,96,96]{2,1,0:T(8,128)S(1)} %shard_map.95.rest_0_), channel_id=1, source_target_pairs={{0,8},{4,12},{8,0},{12,4},{16,24},{20,28},{24,16},{28,20},{1,9},{5... | collective-permute-start | bytes 442376 | tf_op jit(solution)/shard_map/ppermute | solution.py:19
  23.2 8.0 %collective-permute-start.8 = (f32[4,96,96]{2,1,0:T(8,128)S(1)}, f32[4,96,96]{2,1,0:T(8,128)S(1)}, u32[]{:S(2)}, u32[]{:S(2)}) collective-permute-start(f32[4,96,96]{2,1,0:T(8,128)S(1)} %shard_map.95.rest_0_), channel_id=1, source_target_pairs={{0,1},{1,0},{2,3},{3,2},{4,5},{5,4},{6,7},{7,6},{8,9},{9,8},{10,11... | collective-permute-start | bytes 442376 | tf_op jit(solution)/shard_map/ppermute | solution.py:19
  27.7 3.6 %collective-permute-start.9 = (f32[4,96,96]{2,1,0:T(8,128)S(1)}, f32[4,96,96]{2,1,0:T(8,128)S(1)}, u32[]{:S(2)}, u32[]{:S(2)}) collective-permute-start(f32[4,96,96]{2,1,0:T(8,128)S(1)} %collective-permute-done.7.rest_1_), channel_id=1, source_target_pairs={{0,1},{1,0},{2,3},{3,2},{4,5},{5,4},{6,7},{7,6},{8,9},{9,8},{10,11... | collective-permute-start | bytes 442376 | tf_op jit(solution)/shard_map/ppermute | solution.py:19
  29.1 9.9 %collective-permute-start = (bf16[288,256]{1,0:T(8,128)(2,1)}, bf16[288,256]{1,0:T(8,128)(2,1)S(1)}, u32[]{:S(2)}, u32[]{:S(2)}) collective-permute-start(bf16[288,256]{1,0:T(8,128)(2,1)} %get-tuple-element.24), channel_id=1, source_target_pairs={{0,1},{1,0},{2,3},{3,2},{4,5},{5,4},{6,7},{7,6},{8,9},{9,8},{10,11... | collective-permute-start | bytes 442376 | tf_op jit(solution)/shard_map/ppermute | solution.py:19
  29.1 10.3 %collective-permute-start.1 = (bf16[288,256]{1,0:T(8,128)(2,1)}, bf16[288,256]{1,0:T(8,128)(2,1)S(1)}, u32[]{:S(2)}, u32[]{:S(2)}) collective-permute-start(bf16[288,256]{1,0:T(8,128)(2,1)} %get-tuple-element.25), channel_id=1, source_target_pairs={{0,2},{1,3},{2,0},{3,1},{4,6},{5,7},{6,4},{7,5},{8,10},{9,11},{10,... | collective-permute-start | bytes 442376 | tf_op jit(solution)/shard_map/ppermute | solution.py:19
  29.8 9.9 %collective-permute-start.2 = (bf16[288,256]{1,0:T(8,128)(2,1)}, bf16[288,256]{1,0:T(8,128)(2,1)S(1)}, u32[]{:S(2)}, u32[]{:S(2)}) collective-permute-start(bf16[288,256]{1,0:T(8,128)(2,1)} %get-tuple-element.26), channel_id=1, source_target_pairs={{0,3},{1,2},{2,1},{3,0},{4,7},{5,6},{6,5},{7,4},{8,11},{9,10},{10,... | collective-permute-start | bytes 442376 | tf_op jit(solution)/shard_map/ppermute | solution.py:19
  31.2 10.0 %collective-permute-start.3 = (bf16[288,256]{1,0:T(8,128)(2,1)}, bf16[288,256]{1,0:T(8,128)(2,1)S(1)}, u32[]{:S(2)}, u32[]{:S(2)}) collective-permute-start(bf16[288,256]{1,0:T(8,128)(2,1)} %get-tuple-element.27), channel_id=1, source_target_pairs={{0,4},{4,0},{8,12},{12,8},{16,20},{20,16},{24,28},{28,24},{1,5},{5... | collective-permute-start | bytes 442376 | tf_op jit(solution)/shard_map/ppermute | solution.py:19
  31.3 10.0 %collective-permute-start.4 = (bf16[288,256]{1,0:T(8,128)(2,1)}, bf16[288,256]{1,0:T(8,128)(2,1)S(1)}, u32[]{:S(2)}, u32[]{:S(2)}) collective-permute-start(bf16[288,256]{1,0:T(8,128)(2,1)} %get-tuple-element.28), channel_id=1, source_target_pairs={{4,8},{12,16},{20,24},{8,4},{16,12},{24,20},{5,9},{13,17},{21,25},... | collective-permute-start | bytes 442376 | tf_op jit(solution)/shard_map/ppermute | solution.py:25
  39.0 5.9 %collective-permute-start.10 = (f32[64,256]{1,0:T(8,128)S(1)}, f32[64,256]{1,0:T(8,128)S(1)}, u32[]{:S(2)}, u32[]{:S(2)}) collective-permute-start(f32[64,256]{1,0:T(8,128)S(1)} %get-tuple-element.34), channel_id=1, source_target_pairs={{0,1},{1,0},{2,3},{3,2},{4,5},{5,4},{6,7},{7,6},{8,9},{9,8},{10,11... | collective-permute-start | bytes 196616 | tf_op jit(solution)/shard_map/ppermute | solution.py:19
  39.4 5.5 %collective-permute-start.11 = (f32[64,256]{1,0:T(8,128)S(1)}, f32[64,256]{1,0:T(8,128)S(1)}, u32[]{:S(2)}, u32[]{:S(2)}) collective-permute-start(f32[64,256]{1,0:T(8,128)S(1)} %get-tuple-element.35), channel_id=1, source_target_pairs={{0,2},{1,3},{2,0},{3,1},{4,6},{5,7},{6,4},{7,5},{8,10},{9,11},{10,... | collective-permute-start | bytes 196616 | tf_op jit(solution)/shard_map/ppermute | solution.py:19
  39.8 5.1 %collective-permute-start.12 = (f32[64,256]{1,0:T(8,128)S(1)}, f32[64,256]{1,0:T(8,128)S(1)}, u32[]{:S(2)}, u32[]{:S(2)}) collective-permute-start(f32[64,256]{1,0:T(8,128)S(1)} %get-tuple-element.36), channel_id=1, source_target_pairs={{0,3},{1,2},{2,1},{3,0},{4,7},{5,6},{6,5},{7,4},{8,11},{9,10},{10,... | collective-permute-start | bytes 196616 | tf_op jit(solution)/shard_map/ppermute | solution.py:19
  41.3 3.6 %copy-start = (f32[2048,256]{1,0:T(8,128)S(1)}, f32[2048,256]{1,0:T(8,128)}, u32[]{:S(2)}) copy-start(f32[2048,256]{1,0:T(8,128)} %get-tuple-element.21.part_ref) | copy-start | bytes 6291460

commit v6 on v5

--- a/solution.py
+++ b/solution.py
@@ -310,7 +310,7 @@
     parity = w & 1
     sides = [w, w ^ 1, jnp.clip(w - 1 + 2 * parity, 0, slabs - 1)]
     value = jnp.concatenate([solved[s] for s in sides], axis=1)
-    stacked = jnp.concatenate(split_three(value), axis=0)
+    stacked = jnp.concatenate(split_two(value), axis=0)
     width = shares[0].shape[1]
     lanes = iota((1, width), 1)
     rows = iota((order, width), 0).astype(f32)
@@ -330,7 +330,7 @@
                 full = jnp.where(inside, pltpu.roll(code, place, 1), full)
             hots.append((rows == full).astype(f32).astype(bf16))
         total = dot(stacked, jnp.concatenate(hots, axis=0))
-        shares[k][...] = total[:c] + total[c : 2 * c] + total[2 * c :]
+        shares[k][...] = total[:c] + total[c:]
 
 
 def scatter_kernel(groups, size, length_ref, index_ref, maps_ref, lane_scale_ref, basis_ref, *rest):
@@ -520,9 +520,11 @@
         flops=2 * 3 * slabs * 2 * own_columns * order * 2 * order,
         limit=24 if slabs <= 8 else 62,
     )
-    pieces = [shares[0]] + [swap(shares[k], "narrow", k) for k in range(1, groups)]
-
-    block = min(rows, 1024)
+    pieces = [shares[0]]
+    for k in range(1, groups):
+        pieces.append(swap(shares[k], "narrow", k))
+
+    block = min(rows, 2048)
     early, late, own = call(
         functools.partial(scatter_kernel, groups, size),
         [struct((rows, columns), f32), struct((rows, width), bf16), struct((rows, width), bf16)],

time: 47.4 us -> 47.1 us (level)
  the two profiles are of different devices: /device:TPU:5 before, /device:TPU:8 now
where the time goes in v6:
time: 47.1 us; the launch traced here: 46.8 us
  starting transfers between devices  16.8 us (36%)
  Pallas kernels  16.2 us (34%)
  waiting for transfers between devices  12.7 us (27%)
  other arithmetic  0.81 us (2%)
    pallas_call x7, Pallas kernels, call(): pl.pallas_call(kernel, out_shape=outs, grid=grid, in_specs=in_specs, out_...  16.2 us
    ppermute x12, waiting for transfers between devices, swap(): return lax.ppermute(block, axis, [(i, i ^ mask) for i in range(count)])  11 us
    ppermute x12, starting transfers between devices, swap(): return lax.ppermute(block, axis, [(i, i ^ mask) for i in range(count)])  10.6 us
    all_to_all x1, starting transfers between devices, body(): lax.all_to_all(sent, ('wide', 'narrow'), split_axis=0, concat_axis=0, til...  4.03 us
    ppermute x1, starting transfers between devices, swap_odd(): return lax.ppermute(block, axis, pairs + [(b, a) for a, b in pairs])  2.25 us
    ppermute x1, waiting for transfers between devices, swap_odd(): return lax.ppermute(block, axis, pairs + [(b, a) for a, b in pairs])  1.69 us
  transfers between devices with their start and end apart: 14, of which 4 were waited for; matrix products, arithmetic and copies ran while one was open for 0% of the time, Pallas kernels for 30%

profile of v6, /device:TPU:8, one launch (start us, length us, event | category | flops | bytes accessed | tf_op | source)
XLA Modules:
  0.0 46.8 jit_solution(11863349673784885127)
XLA Ops:
  0.0 0.8 %broadcast_select_fusion.refs_0_ = f32[1,96,96]{2,1,0:T(8,128)S(1)} fusion(f32[1,96,96]{2,1,0:T(8,128)} %param.16, f32[1,96,96]{2,1,0:T(8,128)} %param.17, pred[]{:T(512)S(6)} %eq.3), kind=kLoop, calls=%fused_computation | loop fusion | flops 9216 | bytes 110593 | tf_op jit(solution)/shard_map/jit(_where)/select_n | solution.py:449
  0.8 2.6 %collective-permute-start.5 = (f32[1,96,96]{2,1,0:T(8,128)S(1)}, f32[1,96,96]{2,1,0:T(8,128)S(1)}, u32[]{:S(2)}, u32[]{:S(2)}) collective-permute-start(f32[1,96,96]{2,1,0:T(8,128)S(1)} %broadcast_select_fusion.refs_0_), channel_id=1, source_target_pairs={{0,16},{4,20},{8,24},{12,28},{16,0},{20,4},{24,8},{28,12},{1,17},{... | collective-permute-start | bytes 110600 | tf_op jit(solution)/shard_map/ppermute | solution.py:19
  3.4 7.6 %shard_map.91 = (f32[32,16,128]{2,1,0:T(8,128)}, f32[2048,256]{1,0:T(8,128)}, bf16[288,256]{1,0:T(8,128)(2,1)}, bf16[288,256]{1,0:T(8,128)(2,1)}, bf16[288,256]{...) custom-call(bf16[2048,2048]{1,0:T(8,128)(2,1)} %bitcast.17, bf16[2048,256]{1,0:T(8,128)(2,1)} %bitcast.18, ...), custom_call_target="tpu_custom_call" | custom-call | flops 3489660928 | bytes 12654688 | tf_op jit(solution)/shard_map/pallas_call | solution.py:66
  11.0 0.0 copy-start.1
  11.0 0.0 copy-start.2
  11.0 0.0 copy-start.3
  11.0 0.0 copy-start.4
  11.0 4.0 %all-to-all-start = ((f32[32,16,128]{2,1,0:T(8,128)}), f32[32,16,128]{2,1,0:T(8,128)S(1)}, u32[]{:S(2)}, u32[]{:S(2)}) async-start(f32[32,16,128]{2,1,0:T(8,128)} %get-tuple-element.22), calls=%async_computation | async-start | bytes 524288 | tf_op jit(solution)/shard_map/all_to_all | solution.py:491
  15.1 0.0 collective-permute-done.5.refs_1_
  15.1 1.5 %collective-permute-start.6 = (f32[2,96,96]{2,1,0:T(8,128)S(1)}, f32[2,96,96]{2,1,0:T(8,128)S(1)}, u32[]{:S(2)}, u32[]{:S(2)}) collective-permute-start(f32[2,96,96]{2,1,0:T(8,128)S(1)} %shard_map.94), channel_id=1, source_target_pairs={{0,4},{4,0},{8,12},{12,8},{16,20},{20,16},{24,28},{28,24},{1,5},{5... | collective-permute-start | bytes 221192 | tf_op jit(solution)/shard_map/ppermute | solution.py:19
  16.6 5.2 %collective-permute-done.6.refs_2_ = f32[2,96,96]{2,1,0:T(8,128)S(1)} collective-permute-done((f32[2,96,96]{2,1,0:T(8,128)S(1)}, f32[2,96,96]{2,1,0:T(8,128)S(1)}, u32[]{:S(2)}, u32[]{:S(2)}) %collective-permute-start.6) | collective-permute-done | bytes 73760 | tf_op jit(solution)/shard_map/ppermute | solution.py:19
  21.8 0.3 collective-permute-start.7
  22.2 0.0 collective-permute-start.8
  22.2 5.6 %collective-permute-done.7.rest_1_ = f32[4,96,96]{2,1,0:T(8,128)S(1)} collective-permute-done((f32[4,96,96]{2,1,0:T(8,128)S(1)}, f32[4,96,96]{2,1,0:T(8,128)S(1)}, u32[]{:S(2)}, u32[]{:S(2)}) %collective-permute-start.7) | collective-permute-done | bytes 147488 | tf_op jit(solution)/shard_map/ppermute | solution.py:19
  27.8 0.0 collective-permute-start.9
  27.8 0.5 %collective-permute-start = (bf16[288,256]{1,0:T(8,128)(2,1)}, bf16[288,256]{1,0:T(8,128)(2,1)S(1)}, u32[]{:S(2)}, u32[]{:S(2)}) collective-permute-start(bf16[288,256]{1,0:T(8,128)(2,1)} %get-tuple-element.24), channel_id=1, source_target_pairs={{0,1},{1,0},{2,3},{3,2},{4,5},{5,4},{6,7},{7,6},{8,9},{9,8},{10,11... | collective-permute-start | bytes 442376 | tf_op jit(solution)/shard_map/ppermute | solution.py:19
  28.3 2.2 %collective-permute-start.1 = (bf16[288,256]{1,0:T(8,128)(2,1)}, bf16[288,256]{1,0:T(8,128)(2,1)S(1)}, u32[]{:S(2)}, u32[]{:S(2)}) collective-permute-start(bf16[288,256]{1,0:T(8,128)(2,1)} %get-tuple-element.25), channel_id=1, source_target_pairs={{0,2},{1,3},{2,0},{3,1},{4,6},{5,7},{6,4},{7,5},{8,10},{9,11},{10,... | collective-permute-start | bytes 442376 | tf_op jit(solution)/shard_map/ppermute | solution.py:19
  30.5 0.0 collective-permute-start.2
  30.5 0.0 collective-permute-done.8.rest_2_
  30.5 1.5 %collective-permute-start.3 = (bf16[288,256]{1,0:T(8,128)(2,1)}, bf16[288,256]{1,0:T(8,128)(2,1)S(1)}, u32[]{:S(2)}, u32[]{:S(2)}) collective-permute-start(bf16[288,256]{1,0:T(8,128)(2,1)} %get-tuple-element.27), channel_id=1, source_target_pairs={{0,4},{4,0},{8,12},{12,8},{16,20},{20,16},{24,28},{28,24},{1,5},{5... | collective-permute-start | bytes 442376 | tf_op jit(solution)/shard_map/ppermute | solution.py:19
  32.0 0.0 collective-permute-done.9.rest_3_
  32.0 2.3 %collective-permute-start.4 = (bf16[288,256]{1,0:T(8,128)(2,1)}, bf16[288,256]{1,0:T(8,128)(2,1)S(1)}, u32[]{:S(2)}, u32[]{:S(2)}) collective-permute-start(bf16[288,256]{1,0:T(8,128)(2,1)} %get-tuple-element.28), channel_id=1, source_target_pairs={{4,8},{12,16},{20,24},{8,4},{16,12},{24,20},{5,9},{13,17},{21,25},... | collective-permute-start | bytes 442376 | tf_op jit(solution)/shard_map/ppermute | solution.py:25
  34.2 0.0 all-to-all-done.got_ref
  34.3 0.5 %shard_map.92 = (f32[8,64,128]{2,1,0:T(8,128)S(1)}, f32[32,128]{1,0:T(8,128)S(1)}) custom-call(f32[32,16,128]{2,1,0:T(8,128)S(1)} %all-to-all-done.got_ref), custom_call_target="tpu_custom_call" | custom-call | flops 50331648 | bytes 540672 | tf_op jit(solution)/shard_map/pallas_call | solution.py:66
  34.7 2.6 %shard_map.96 = (f32[64,256]{1,0:T(8,128)S(1)}, f32[64,256]{1,0:T(8,128)S(1)}, f32[64,256]{1,0:T(8,128)S(1)}, f32[64,256]{1,0:T(8,128)S(1)}) custom-call(f32[8,64,128]{2,1,0:T(8,128)S(1)} %get-tuple-element.32.right_ref, f32[32,128]{1,0:T(8,128)S(1)} %get-tuple-element.23.maps_ref, f32[4,96,96]{2,1,0:T(8,128)S(1)} %shard_map.95.rest_0_, ...), custom_call_target="tpu_custom_call" | custom-call | flops 201326592 | bytes 1130496 | tf_op jit(solution)/shard_map/pallas_call | solution.py:66
  37.4 0.0 collective-permute-done.rest_0_
  37.4 0.2 collective-permute-start.10
  37.6 0.0 collective-permute-done.1.rest_1_
  37.6 1.4 %collective-permute-start.11 = (f32[64,256]{1,0:T(8,128)S(1)}, f32[64,256]{1,0:T(8,128)S(1)}, u32[]{:S(2)}, u32[]{:S(2)}) collective-permute-start(f32[64,256]{1,0:T(8,128)S(1)} %get-tuple-element.35), channel_id=1, source_target_pairs={{0,2},{1,3},{2,0},{3,1},{4,6},{5,7},{6,4},{7,5},{8,10},{9,11},{10,... | collective-permute-start | bytes 196616 | tf_op jit(solution)/shard_map/ppermute | solution.py:19
  39.1 0.0 collective-permute-done.2.rest_2_
  39.1 0.3 collective-permute-start.12
  39.3 0.2 collective-permute-done.3.rest_3_
  39.5 1.7 %collective-permute-done.4.rest_4_ = bf16[288,256]{1,0:T(8,128)(2,1)S(1)} collective-permute-done((bf16[288,256]{1,0:T(8,128)(2,1)}, bf16[288,256]{1,0:T(8,128)(2,1)S(1)}, u32[]{:S(2)}, u32[]{:S(2)}) %collective-permute-start.4) | collective-permute-done | bytes 147488 | tf_op jit(solution)/shard_map/ppermute | solution.py:25
  41.2 0.0 copy-done.1
  41.2 0.0 copy-done.2
  41.2 0.0 copy-done.3
  41.2 0.0 copy-done.4
  41.3 0.0 copy-start
  41.3 3.3 %shard_map.93 = (f32[2048,256]{1,0:T(8,128)S(1)}, bf16[2048,256]{1,0:T(8,128)(2,1)S(1)}, bf16[2048,256]{1,0:T(8,128)(2,1)S(1)}) custom-call(s32[1,6]{1,0:T(1,128)S(1)} %bitcast.16, s32[6,1,256]{2,1,0:T(1,128)S(1)} %bitcast.15, f32[32,128]{1,0:T(8,128)S(1)} %get-tuple-element.23.maps_ref, f32[1,2048]{1,0:T(1,128)S(1)} %bitcast.13, ...), custom_call_target="tpu_custom_call" | custom-call | flops 2684354560 | bytes 5060632 | tf_op jit(solution)/shard_map/pallas_call | solution.py:66
  44.5 0.0 collective-permute-done.10.rest_1_
  44.5 0.0 collective-permute-done.11.rest_2_
  44.5 0.0 collective-permute-done.12.rest_3_
  44.6 0.0 copy-done
  44.6 2.2 %shard_map.97 = f32[2048,256]{1,0:T(8,128)} custom-call(f32[2048,256]{1,0:T(8,128)S(1)} %copy-done, f32[2048,256]{1,0:T(8,128)S(1)} %get-tuple-element.29.early_ref, bf16[2048,256]{1,0:T(8,128)(2,1)S(1)} %get-tuple-element.30.late_ref, bf16[2048,256]{1,0:T(8,128)(2,1)S(1)} %get-tuple-element.31.own_ref, f32[64,256]{1,0:T(8,128)S(1)} %get-tuple-element.33.rest_0_, ...), custom_call_target="tpu_custom_call" | custom-call | flops 805306368 | bytes 8650752 | tf_op jit(solution)/shard_map/pallas_call | solution.py:66
  (2 shorter events, 0.0 us)
Async XLA Ops:
  0.8 14.3 %collective-permute-start.5 = (f32[1,96,96]{2,1,0:T(8,128)S(1)}, f32[1,96,96]{2,1,0:T(8,128)S(1)}, u32[]{:S(2)}, u32[]{:S(2)}) collective-permute-start(f32[1,96,96]{2,1,0:T(8,128)S(1)} %broadcast_select_fusion.refs_0_), channel_id=1, source_target_pairs={{0,16},{4,20},{8,24},{12,28},{16,0},{20,4},{24,8},{28,12},{1,17},{... | collective-permute-start | bytes 110600 | tf_op jit(solution)/shard_map/ppermute | solution.py:19
  11.0 30.3 %copy-start.1 = (bf16[1,1,24,2048]{3,2,1,0:T(8,128)(2,1)S(1)}, bf16[1,1,24,2048]{3,2,1,0:T(8,128)(2,1)}, u32[]{:S(2)}) copy-start(bf16[1,1,24,2048]{3,2,1,0:T(8,128)(2,1)} %param.12) | copy-start | bytes 294916
  11.0 30.2 %copy-start.2 = (f32[1,1,2048]{2,1,0:T(1,128)S(1)}, f32[1,1,2048]{2,1,0:T(1,128)}, u32[]{:S(2)}) copy-start(f32[1,1,2048]{2,1,0:T(1,128)} %param.10) | copy-start | bytes 24580
  11.0 30.2 %copy-start.3 = (s32[1,1,6,256]{3,1,2,0:T(1,128)S(1)}, s32[1,1,6,256]{3,1,2,0:T(1,128)}, u32[]{:S(2)}) copy-start(s32[1,1,6,256]{3,1,2,0:T(1,128)} %param.14) | copy-start | bytes 18436
  11.0 30.2 %copy-start.4 = (s32[1,1,6]{2,1,0:T(1,128)S(1)}, s32[1,1,6]{2,1,0:T(1,128)}, u32[]{:S(2)}) copy-start(s32[1,1,6]{2,1,0:T(1,128)} %param.15) | copy-start | bytes 76
  11.0 23.2 %all-to-all-start = ((f32[32,16,128]{2,1,0:T(8,128)}), f32[32,16,128]{2,1,0:T(8,128)S(1)}, u32[]{:S(2)}, u32[]{:S(2)}) async-start(f32[32,16,128]{2,1,0:T(8,128)} %get-tuple-element.22), calls=%async_computation | async-start | bytes 524288 | tf_op jit(solution)/shard_map/all_to_all | solution.py:491
  15.1 6.7 %collective-permute-start.6 = (f32[2,96,96]{2,1,0:T(8,128)S(1)}, f32[2,96,96]{2,1,0:T(8,128)S(1)}, u32[]{:S(2)}, u32[]{:S(2)}) collective-permute-start(f32[2,96,96]{2,1,0:T(8,128)S(1)} %shard_map.94), channel_id=1, source_target_pairs={{0,4},{4,0},{8,12},{12,8},{16,20},{20,16},{24,28},{28,24},{1,5},{5... | collective-permute-start | bytes 221192 | tf_op jit(solution)/shard_map/ppermute | solution.py:19
  21.8 6.0 %collective-permute-start.7 = (f32[4,96,96]{2,1,0:T(8,128)S(1)}, f32[4,96,96]{2,1,0:T(8,128)S(1)}, u32[]{:S(2)}, u32[]{:S(2)}) collective-permute-start(f32[4,96,96]{2,1,0:T(8,128)S(1)} %shard_map.95.rest_0_), channel_id=1, source_target_pairs={{0,8},{4,12},{8,0},{12,4},{16,24},{20,28},{24,16},{28,20},{1,9},{5... | collective-permute-start | bytes 442376 | tf_op jit(solution)/shard_map/ppermute | solution.py:19
  22.2 8.3 %collective-permute-start.8 = (f32[4,96,96]{2,1,0:T(8,128)S(1)}, f32[4,96,96]{2,1,0:T(8,128)S(1)}, u32[]{:S(2)}, u32[]{:S(2)}) collective-permute-start(f32[4,96,96]{2,1,0:T(8,128)S(1)} %shard_map.95.rest_0_), channel_id=1, source_target_pairs={{0,1},{1,0},{2,3},{3,2},{4,5},{5,4},{6,7},{7,6},{8,9},{9,8},{10,11... | collective-permute-start | bytes 442376 | tf_op jit(solution)/shard_map/ppermute | solution.py:19
  27.8 4.2 %collective-permute-start.9 = (f32[4,96,96]{2,1,0:T(8,128)S(1)}, f32[4,96,96]{2,1,0:T(8,128)S(1)}, u32[]{:S(2)}, u32[]{:S(2)}) collective-permute-start(f32[4,96,96]{2,1,0:T(8,128)S(1)} %collective-permute-done.7.rest_1_), channel_id=1, source_target_pairs={{0,1},{1,0},{2,3},{3,2},{4,5},{5,4},{6,7},{7,6},{8,9},{9,8},{10,11... | collective-permute-start | bytes 442376 | tf_op jit(solution)/shard_map/ppermute | solution.py:19
  27.8 9.6 %collective-permute-start = (bf16[288,256]{1,0:T(8,128)(2,1)}, bf16[288,256]{1,0:T(8,128)(2,1)S(1)}, u32[]{:S(2)}, u32[]{:S(2)}) collective-permute-start(bf16[288,256]{1,0:T(8,128)(2,1)} %get-tuple-element.24), channel_id=1, source_target_pairs={{0,1},{1,0},{2,3},{3,2},{4,5},{5,4},{6,7},{7,6},{8,9},{9,8},{10,11... | collective-permute-start | bytes 442376 | tf_op jit(solution)/shard_map/ppermute | solution.py:19
  28.3 9.3 %collective-permute-start.1 = (bf16[288,256]{1,0:T(8,128)(2,1)}, bf16[288,256]{1,0:T(8,128)(2,1)S(1)}, u32[]{:S(2)}, u32[]{:S(2)}) collective-permute-start(bf16[288,256]{1,0:T(8,128)(2,1)} %get-tuple-element.25), channel_id=1, source_target_pairs={{0,2},{1,3},{2,0},{3,1},{4,6},{5,7},{6,4},{7,5},{8,10},{9,11},{10,... | collective-permute-start | bytes 442376 | tf_op jit(solution)/shard_map/ppermute | solution.py:19
  30.5 8.6 %collective-permute-start.2 = (bf16[288,256]{1,0:T(8,128)(2,1)}, bf16[288,256]{1,0:T(8,128)(2,1)S(1)}, u32[]{:S(2)}, u32[]{:S(2)}) collective-permute-start(bf16[288,256]{1,0:T(8,128)(2,1)} %get-tuple-element.26), channel_id=1, source_target_pairs={{0,3},{1,2},{2,1},{3,0},{4,7},{5,6},{6,5},{7,4},{8,11},{9,10},{10,... | collective-permute-start | bytes 442376 | tf_op jit(solution)/shard_map/ppermute | solution.py:19
  30.5 9.1 %collective-permute-start.3 = (bf16[288,256]{1,0:T(8,128)(2,1)}, bf16[288,256]{1,0:T(8,128)(2,1)S(1)}, u32[]{:S(2)}, u32[]{:S(2)}) collective-permute-start(bf16[288,256]{1,0:T(8,128)(2,1)} %get-tuple-element.27), channel_id=1, source_target_pairs={{0,4},{4,0},{8,12},{12,8},{16,20},{20,16},{24,28},{28,24},{1,5},{5... | collective-permute-start | bytes 442376 | tf_op jit(solution)/shard_map/ppermute | solution.py:19
  32.0 9.3 %collective-permute-start.4 = (bf16[288,256]{1,0:T(8,128)(2,1)}, bf16[288,256]{1,0:T(8,128)(2,1)S(1)}, u32[]{:S(2)}, u32[]{:S(2)}) collective-permute-start(bf16[288,256]{1,0:T(8,128)(2,1)} %get-tuple-element.28), channel_id=1, source_target_pairs={{4,8},{12,16},{20,24},{8,4},{16,12},{24,20},{5,9},{13,17},{21,25},... | collective-permute-start | bytes 442376 | tf_op jit(solution)/shard_map/ppermute | solution.py:25
  37.4 7.1 %collective-permute-start.10 = (f32[64,256]{1,0:T(8,128)S(1)}, f32[64,256]{1,0:T(8,128)S(1)}, u32[]{:S(2)}, u32[]{:S(2)}) collective-permute-start(f32[64,256]{1,0:T(8,128)S(1)} %get-tuple-element.34), channel_id=1, source_target_pairs={{0,1},{1,0},{2,3},{3,2},{4,5},{5,4},{6,7},{7,6},{8,9},{9,8},{10,11... | collective-permute-start | bytes 196616 | tf_op jit(solution)/shard_map/ppermute | solution.py:19
  37.6 6.9 %collective-permute-start.11 = (f32[64,256]{1,0:T(8,128)S(1)}, f32[64,256]{1,0:T(8,128)S(1)}, u32[]{:S(2)}, u32[]{:S(2)}) collective-permute-start(f32[64,256]{1,0:T(8,128)S(1)} %get-tuple-element.35), channel_id=1, source_target_pairs={{0,2},{1,3},{2,0},{3,1},{4,6},{5,7},{6,4},{7,5},{8,10},{9,11},{10,... | collective-permute-start | bytes 196616 | tf_op jit(solution)/shard_map/ppermute | solution.py:19
  39.1 5.5 %collective-permute-start.12 = (f32[64,256]{1,0:T(8,128)S(1)}, f32[64,256]{1,0:T(8,128)S(1)}, u32[]{:S(2)}, u32[]{:S(2)}) collective-permute-start(f32[64,256]{1,0:T(8,128)S(1)} %get-tuple-element.36), channel_id=1, source_target_pairs={{0,3},{1,2},{2,1},{3,0},{4,7},{5,6},{6,5},{7,4},{8,11},{9,10},{10,... | collective-permute-start | bytes 196616 | tf_op jit(solution)/shard_map/ppermute | solution.py:19
  41.3 3.3 %copy-start = (f32[2048,256]{1,0:T(8,128)S(1)}, f32[2048,256]{1,0:T(8,128)}, u32[]{:S(2)}) copy-start(f32[2048,256]{1,0:T(8,128)} %get-tuple-element.21.part_ref) | copy-start | bytes 6291460
